TPU v7x, 32 devices: a whole 2x2x4 slice. The times are simulated.
32 devices in a mesh: dp: 32 (over z, y, x, core).
Axes of the slice: x: 2, y: 2, z: 4, core: 2. Of those that a mesh axis runs over, the one named last changes fastest.
Arguments:
- tokens: bfloat16 [32768, 1024], P('dp'), may hold values from -6 to 6
- cotangent: bfloat16 [32768, 1024], P('dp'), may hold values from -6 to 6
- lengths: int32 [256], replicated, may hold values from 0 to 512, as said below
- dealing: int32 [256], replicated, may hold values from 0 to 255, as said below
- query_weight: bfloat16 [1024, 1024], P('dp'), may hold values from -0.1875 to 0.1875
- key_weight: bfloat16 [1024, 1024], P('dp'), may hold values from -0.1875 to 0.1875
- value_weight: bfloat16 [1024, 1024], P('dp'), may hold values from -0.1875 to 0.1875
- out_weight: bfloat16 [1024, 1024], P('dp'), may hold values from -1.5 to 1.5
- up_weight: bfloat16 [1024, 4096], P('dp'), may hold values from -0.1875 to 0.1875
- down_weight: bfloat16 [4096, 1024], P('dp'), may hold values from -0.09375 to 0.09375
- query_bias: bfloat16 [1024], P('dp'), may hold values from -3 to 3
- value_bias: bfloat16 [1024], P('dp'), may hold values from -0.3125 to 0.3125
- out_bias: bfloat16 [1024], P('dp'), may hold values from -0.625 to 0.625
- up_bias: bfloat16 [4096], P('dp'), may hold values from -3 to 3
- down_bias: bfloat16 [1024], P('dp'), may hold values from -0.625 to 0.625
- first_gain: bfloat16 [1024], P('dp'), may hold values from 0.5 to 1.5
- first_shift: bfloat16 [1024], P('dp'), may hold values from -1.75 to 1.75
- second_gain: bfloat16 [1024], P('dp'), may hold values from 0.5 to 1.5
- second_shift: bfloat16 [1024], P('dp'), may hold values from -1.75 to 1.75
Outputs:
- layer_out: bfloat16 [32768, 1024], P('dp')
- token_gradient: bfloat16 [32768, 1024], P('dp')
- query_weight_gradient: float32 [1024, 1024], P('dp')
- key_weight_gradient: float32 [1024, 1024], P('dp')
- value_weight_gradient: float32 [1024, 1024], P('dp')
- out_weight_gradient: float32 [1024, 1024], P('dp')
- up_weight_gradient: float32 [1024, 4096], P('dp')
- down_weight_gradient: float32 [4096, 1024], P('dp')
- query_bias_gradient: float32 [1024], P('dp')
- value_bias_gradient: float32 [1024], P('dp')
- out_bias_gradient: float32 [1024], P('dp')
- up_bias_gradient: float32 [4096], P('dp')
- down_bias_gradient: float32 [1024], P('dp')
- first_gain_gradient: float32 [1024], P('dp')
- first_shift_gradient: float32 [1024], P('dp')
- second_gain_gradient: float32 [1024], P('dp')
- second_shift_gradient: float32 [1024], P('dp')
Inputs may be any that keep to these rules, and one draw needn't show every extreme that they name: Every length is a multiple of 128; a length of 0 marks an empty place. The lengths sum to 32768. A permutation of the 256 places: sequence s goes to device dealing[s] // 8, to place dealing[s] % 8 of that device's ordered places. Taken in order, each device's places form 2 groups of 4 places whose lengths sum to 512.
All inputs are finite; a program needn't handle non-finite values.
Results may differ from a plain program's by a relative error of at most 0.014.
Values may be sent and summed in bfloat16 or wider, within the bound.
A program may use at most 256 MiB of HBM per device.

v0:
```python
import jax
import jax.numpy as jnp
from jax import lax
from jax.sharding import PartitionSpec as P

HD = 64
MICRO = 2


norm_epsilon = 1e-12
masked_score = -1000000000.0


def layer_norm(values, norm_gain, norm_shift):
    centered = values - jnp.mean(values, axis=-1, keepdims=True)
    variance = jnp.mean(centered * centered, axis=-1, keepdims=True)
    return centered * lax.rsqrt(variance + norm_epsilon) * norm_gain + norm_shift


def gelu_exact(values):
    return jax.nn.gelu(values, approximate=False)


def route_tables(lengths, dealing, tok_dev, devices, own_index):
    blocks = tok_dev // devices
    seq_count = lengths.shape[0]
    seq_ids = jnp.arange(seq_count, dtype=jnp.int32)
    starts = jnp.cumsum(lengths) - lengths
    deal_match = dealing[:, None] == seq_ids[None, :]
    dealt_lengths = jnp.sum(jnp.where(deal_match, lengths[:, None], 0), axis=0)
    dealt_starts = jnp.cumsum(dealt_lengths) - dealt_lengths
    dealt_start_of = jnp.sum(jnp.where(deal_match, dealt_starts[None, :], 0), axis=1)
    shift_of = dealt_start_of - starts
    held_rows = (
        jnp.arange(blocks, dtype=jnp.int32)[:, None] * devices
        + jnp.arange(devices, dtype=jnp.int32)[None, :] * tok_dev
        + own_index
    ).reshape(blocks * devices)
    inside = (starts[None, :] <= held_rows[:, None]) & (
        held_rows[:, None] < (starts + lengths)[None, :]
    )
    placed = held_rows + jnp.sum(jnp.where(inside, shift_of[None, :], 0), axis=1)
    dest_device = placed // tok_dev
    dest_block = placed % tok_dev // devices
    target = dest_block * devices + dest_device
    send_order = (
        jnp.zeros_like(target).at[target].set(jnp.arange(blocks * devices, dtype=jnp.int32))
    )
    local_rows = own_index * tok_dev + jnp.arange(tok_dev, dtype=jnp.int32)
    in_sequence = (dealt_starts[None, :] <= local_rows[:, None]) & (
        local_rows[:, None] < (dealt_starts + dealt_lengths)[None, :]
    )
    segment_ids = jnp.sum(jnp.where(in_sequence, seq_ids[None, :], 0), axis=1)
    return (send_order, target, segment_ids)


def attention_scores(queries, key_heads, segments):
    scores = jnp.einsum(
        "qhd,khd->hqk", queries, key_heads, preferred_element_type=jnp.float32
    ) * HD ** (-0.5)
    same_doc = segments[:, None] == segments[None, :]
    return jnp.where(same_doc[None], scores, masked_score)


def forward_pass(weights_full, tok_rows, segments):
    (
        query_weight,
        key_weight,
        value_weight,
        out_weight,
        up_weight,
        down_weight,
        query_bias,
        value_bias,
        out_bias,
        up_bias,
        down_bias,
        first_gain,
        first_shift,
        second_gain,
        second_shift,
    ) = weights_full
    row_count, model_width = tok_rows.shape
    head_count = model_width // HD
    queries = (
        (
            jnp.dot(tok_rows, query_weight, preferred_element_type=jnp.float32)
            + query_bias.astype(jnp.float32)
        )
        .astype(jnp.bfloat16)
        .reshape(row_count, head_count, HD)
    )
    key_heads = (
        jnp.dot(tok_rows, key_weight, preferred_element_type=jnp.float32)
        .astype(jnp.bfloat16)
        .reshape(row_count, head_count, HD)
    )
    value_heads = (
        (
            jnp.dot(tok_rows, value_weight, preferred_element_type=jnp.float32)
            + value_bias.astype(jnp.float32)
        )
        .astype(jnp.bfloat16)
        .reshape(row_count, head_count, HD)
    )
    scores = attention_scores(queries, key_heads, segments)
    row_max = jnp.max(scores, axis=-1, keepdims=True)
    row_total = jnp.sum(jnp.exp(scores - row_max), axis=-1, keepdims=True)
    log_total = row_max + jnp.log(row_total)
    attention = jnp.exp(scores - log_total).astype(jnp.bfloat16)
    context = (
        jnp.einsum("hqk,khd->qhd", attention, value_heads, preferred_element_type=jnp.float32)
        .astype(jnp.bfloat16)
        .reshape(row_count, model_width)
    )
    attended = jnp.dot(context, out_weight, preferred_element_type=jnp.float32) + out_bias.astype(
        jnp.float32
    )
    first_norm, first_pull = jax.vjp(
        layer_norm,
        tok_rows.astype(jnp.float32) + attended,
        first_gain.astype(jnp.float32),
        first_shift.astype(jnp.float32),
    )
    first_low = first_norm.astype(jnp.bfloat16)
    up_values = jnp.dot(first_low, up_weight, preferred_element_type=jnp.float32) + up_bias.astype(
        jnp.float32
    )
    activated, gelu_pull = jax.vjp(gelu_exact, up_values)
    hidden = activated.astype(jnp.bfloat16)
    down_values = jnp.dot(
        hidden, down_weight, preferred_element_type=jnp.float32
    ) + down_bias.astype(jnp.float32)
    output, second_pull = jax.vjp(
        layer_norm,
        first_norm + down_values,
        second_gain.astype(jnp.float32),
        second_shift.astype(jnp.float32),
    )
    return (
        output,
        (
            queries,
            key_heads,
            value_heads,
            log_total,
            context,
            first_low,
            hidden,
            first_pull,
            gelu_pull,
            second_pull,
        ),
    )


def backward_pass(weights_full, tok_rows, grad_rows, segments, kept_state):
    (
        query_weight,
        key_weight,
        value_weight,
        out_weight,
        up_weight,
        down_weight,
        query_bias,
        value_bias,
        out_bias,
        up_bias,
        down_bias,
        first_gain,
        first_shift,
        second_gain,
        second_shift,
    ) = weights_full
    (
        queries,
        key_heads,
        value_heads,
        log_total,
        context,
        first_low,
        hidden,
        first_pull,
        gelu_pull,
        second_pull,
    ) = kept_state
    row_count, model_width = tok_rows.shape
    head_count = model_width // HD
    grad_second, second_gain_grad, second_shift_grad = second_pull(grad_rows.astype(jnp.float32))
    grad_down = grad_second.astype(jnp.bfloat16)
    down_bias_grad = jnp.sum(grad_down.astype(jnp.float32), axis=0)
    down_weight_grad = jnp.einsum(
        "rf,rd->fd", hidden, grad_down, preferred_element_type=jnp.float32
    )
    grad_hidden = jnp.einsum(
        "rd,fd->rf", grad_down, down_weight, preferred_element_type=jnp.float32
    )
    grad_up = gelu_pull(grad_hidden)[0].astype(jnp.bfloat16)
    up_bias_grad = jnp.sum(grad_up.astype(jnp.float32), axis=0)
    up_weight_grad = jnp.einsum("rd,rf->df", first_low, grad_up, preferred_element_type=jnp.float32)
    grad_first = grad_second + jnp.einsum(
        "rf,df->rd", grad_up, up_weight, preferred_element_type=jnp.float32
    )
    grad_sum_first, first_gain_grad, first_shift_grad = first_pull(grad_first)
    grad_attended = grad_sum_first.astype(jnp.bfloat16)
    out_bias_grad = jnp.sum(grad_attended.astype(jnp.float32), axis=0)
    out_weight_grad = jnp.einsum(
        "rc,rd->cd", context, grad_attended, preferred_element_type=jnp.float32
    )
    grad_context = (
        jnp.einsum("rd,cd->rc", grad_attended, out_weight, preferred_element_type=jnp.float32)
        .astype(jnp.bfloat16)
        .reshape(row_count, head_count, HD)
    )
    scores = attention_scores(queries, key_heads, segments)
    attention_full = jnp.exp(scores - log_total)
    grad_attention = jnp.einsum(
        "qhd,khd->hqk", grad_context, value_heads, preferred_element_type=jnp.float32
    )
    value_grad = (
        jnp.einsum(
            "hqk,qhd->khd",
            attention_full.astype(jnp.bfloat16),
            grad_context,
            preferred_element_type=jnp.float32,
        )
        .astype(jnp.bfloat16)
        .reshape(row_count, model_width)
    )
    row_dot = jnp.sum(attention_full * grad_attention, axis=-1, keepdims=True)
    grad_scores = (attention_full * (grad_attention - row_dot)).astype(jnp.bfloat16)
    query_grad = (
        (
            jnp.einsum("hqk,khd->qhd", grad_scores, key_heads, preferred_element_type=jnp.float32)
            * HD ** (-0.5)
        )
        .astype(jnp.bfloat16)
        .reshape(row_count, model_width)
    )
    key_grad = (
        (
            jnp.einsum("hqk,qhd->khd", grad_scores, queries, preferred_element_type=jnp.float32)
            * HD ** (-0.5)
        )
        .astype(jnp.bfloat16)
        .reshape(row_count, model_width)
    )
    query_bias_grad = jnp.sum(query_grad.astype(jnp.float32), axis=0)
    value_bias_grad = jnp.sum(value_grad.astype(jnp.float32), axis=0)
    query_weight_grad = jnp.einsum(
        "rd,re->de", tok_rows, query_grad, preferred_element_type=jnp.float32
    )
    key_weight_grad = jnp.einsum(
        "rd,re->de", tok_rows, key_grad, preferred_element_type=jnp.float32
    )
    value_weight_grad = jnp.einsum(
        "rd,re->de", tok_rows, value_grad, preferred_element_type=jnp.float32
    )
    token_grad = grad_sum_first + jnp.einsum(
        "re,de->rd", query_grad, query_weight, preferred_element_type=jnp.float32
    )
    token_grad = token_grad + jnp.einsum(
        "re,de->rd", key_grad, key_weight, preferred_element_type=jnp.float32
    )
    token_grad = token_grad + jnp.einsum(
        "re,de->rd", value_grad, value_weight, preferred_element_type=jnp.float32
    )
    gradients = (
        query_weight_grad,
        key_weight_grad,
        value_weight_grad,
        out_weight_grad,
        up_weight_grad,
        down_weight_grad,
        query_bias_grad,
        value_bias_grad,
        out_bias_grad,
        up_bias_grad,
        down_bias_grad,
        first_gain_grad,
        first_shift_grad,
        second_gain_grad,
        second_shift_grad,
    )
    return (token_grad.astype(jnp.bfloat16), gradients)


def local(
    tokens,
    cotangent,
    lengths,
    dealing,
    query_weight,
    key_weight,
    value_weight,
    out_weight,
    up_weight,
    down_weight,
    query_bias,
    value_bias,
    out_bias,
    up_bias,
    down_bias,
    first_gain,
    first_shift,
    second_gain,
    second_shift,
):
    devices = lax.axis_size("dp")
    own_index = lax.axis_index("dp")
    tok_dev, model_width = tokens.shape
    blocks = tok_dev // devices
    micro_rows = tok_dev // MICRO
    shards = (
        query_weight,
        key_weight,
        value_weight,
        out_weight,
        up_weight,
        down_weight,
        query_bias,
        value_bias,
        out_bias,
        up_bias,
        down_bias,
        first_gain,
        first_shift,
        second_gain,
        second_shift,
    )
    spread_tokens, spread_cotangent = (
        lax.all_to_all(
            tokens.reshape(blocks, devices, model_width),
            "dp",
            split_axis=1,
            concat_axis=1,
            tiled=True,
        ),
        lax.all_to_all(
            cotangent.reshape(blocks, devices, model_width),
            "dp",
            split_axis=1,
            concat_axis=1,
            tiled=True,
        ),
    )
    send_order, target, segment_ids = route_tables(lengths, dealing, tok_dev, devices, own_index)
    send_tokens = spread_tokens.reshape(blocks * devices, model_width)[send_order].reshape(
        blocks, devices, model_width
    )
    send_cotangent = spread_cotangent.reshape(blocks * devices, model_width)[send_order].reshape(
        blocks, devices, model_width
    )
    dealt_tokens, dealt_cotangent = (
        lax.all_to_all(send_tokens, "dp", split_axis=1, concat_axis=1, tiled=True),
        lax.all_to_all(send_cotangent, "dp", split_axis=1, concat_axis=1, tiled=True),
    )
    dealt_tokens = dealt_tokens.reshape(tok_dev, model_width)
    dealt_cotangent = dealt_cotangent.reshape(tok_dev, model_width)
    outputs_list = []
    token_grads = []
    totals = None
    for micro_index in range(MICRO):
        row_start = micro_index * micro_rows
        tok_rows = dealt_tokens[row_start : row_start + micro_rows]
        grad_rows = dealt_cotangent[row_start : row_start + micro_rows]
        segments = segment_ids[row_start : row_start + micro_rows]
        forward_weights = (
            lax.all_gather(shards[0], "dp", axis=0, tiled=True),
            lax.all_gather(shards[1], "dp", axis=0, tiled=True),
            lax.all_gather(shards[2], "dp", axis=0, tiled=True),
            lax.all_gather(shards[3], "dp", axis=0, tiled=True),
            lax.all_gather(shards[4], "dp", axis=0, tiled=True),
            lax.all_gather(shards[5], "dp", axis=0, tiled=True),
            lax.all_gather(shards[6], "dp", axis=0, tiled=True),
            lax.all_gather(shards[7], "dp", axis=0, tiled=True),
            lax.all_gather(shards[8], "dp", axis=0, tiled=True),
            lax.all_gather(shards[9], "dp", axis=0, tiled=True),
            lax.all_gather(shards[10], "dp", axis=0, tiled=True),
            lax.all_gather(shards[11], "dp", axis=0, tiled=True),
            lax.all_gather(shards[12], "dp", axis=0, tiled=True),
            lax.all_gather(shards[13], "dp", axis=0, tiled=True),
            lax.all_gather(shards[14], "dp", axis=0, tiled=True),
        )
        output, kept_state = forward_pass(forward_weights, tok_rows, segments)
        backward_weights = (
            lax.all_gather(shards[0], "dp", axis=0, tiled=True),
            lax.all_gather(shards[1], "dp", axis=0, tiled=True),
            lax.all_gather(shards[2], "dp", axis=0, tiled=True),
            lax.all_gather(shards[3], "dp", axis=0, tiled=True),
            lax.all_gather(shards[4], "dp", axis=0, tiled=True),
            lax.all_gather(shards[5], "dp", axis=0, tiled=True),
            lax.all_gather(shards[6], "dp", axis=0, tiled=True),
            lax.all_gather(shards[7], "dp", axis=0, tiled=True),
            lax.all_gather(shards[8], "dp", axis=0, tiled=True),
            lax.all_gather(shards[9], "dp", axis=0, tiled=True),
            lax.all_gather(shards[10], "dp", axis=0, tiled=True),
            lax.all_gather(shards[11], "dp", axis=0, tiled=True),
            lax.all_gather(shards[12], "dp", axis=0, tiled=True),
            lax.all_gather(shards[13], "dp", axis=0, tiled=True),
            lax.all_gather(shards[14], "dp", axis=0, tiled=True),
        )
        token_grad, gradients = backward_pass(
            backward_weights, tok_rows, grad_rows, segments, kept_state
        )
        outputs_list.append(output.astype(jnp.bfloat16))
        token_grads.append(token_grad)
        totals = gradients if micro_index == 0 else jax.tree.map(jnp.add, totals, gradients)
    final_shares = lax.psum_scatter(totals, "dp", scatter_dimension=0, tiled=True)
    layer_out = jnp.concatenate(outputs_list, axis=0)
    token_gradient = jnp.concatenate(token_grads, axis=0)
    back_out, back_grad = (
        lax.all_to_all(
            layer_out.reshape(blocks, devices, model_width),
            "dp",
            split_axis=1,
            concat_axis=1,
            tiled=True,
        ),
        lax.all_to_all(
            token_gradient.reshape(blocks, devices, model_width),
            "dp",
            split_axis=1,
            concat_axis=1,
            tiled=True,
        ),
    )
    held_out = back_out.reshape(blocks * devices, model_width)[target].reshape(
        blocks, devices, model_width
    )
    held_grad = back_grad.reshape(blocks * devices, model_width)[target].reshape(
        blocks, devices, model_width
    )
    home_out, home_grad = (
        lax.all_to_all(held_out, "dp", split_axis=1, concat_axis=1, tiled=True),
        lax.all_to_all(held_grad, "dp", split_axis=1, concat_axis=1, tiled=True),
    )
    return (
        home_out.reshape(tok_dev, model_width),
        home_grad.reshape(tok_dev, model_width),
    ) + tuple(final_shares)


def solution(mesh):
    return jax.shard_map(
        local,
        mesh=mesh,
        in_specs=(
            P("dp", None),
            P("dp", None),
            P(),
            P(),
            P("dp", None),
            P("dp", None),
            P("dp", None),
            P("dp", None),
            P("dp", None),
            P("dp", None),
            P("dp"),
            P("dp"),
            P("dp"),
            P("dp"),
            P("dp"),
            P("dp"),
            P("dp"),
            P("dp"),
            P("dp"),
        ),
        out_specs=(
            P("dp", None),
            P("dp", None),
            P("dp", None),
            P("dp", None),
            P("dp", None),
            P("dp", None),
            P("dp", None),
            P("dp", None),
            P("dp"),
            P("dp"),
            P("dp"),
            P("dp"),
            P("dp"),
            P("dp"),
            P("dp"),
            P("dp"),
            P("dp"),
        ),
        check_vma=False,
    )
```

profile of v0, /device:TPU:0, one launch (start us, length us, event | category | flops | bytes accessed | tf_op | source)
XLA Modules:
  0.0 1535.2 jit_solution(429070514995806762)
XLA Ops:
  26.1 54.7 %all-to-all-done = bf16[32,32,1024]{2,0,1:T(8,128)(2,1)S(1)} async-done(((bf16[32,32,1024]{2,0,1:T(8,128)(2,1)}), bf16[32,32,1024]{2,0,1:T(8,128)(2,1)S(1)}, u32[]{:S(2)}, u32[]{:S(2)}) %all-to-all-start) | async-done | bytes 2097184 | tf_op jit(solution)/shard_map/all_to_all | solution.py:332
  103.8 36.8 %all-to-all-done.4 = bf16[32,32,1024]{2,0,1:T(8,128)(2,1)} async-done(((bf16[32,32,1024]{2,0,1:T(8,128)(2,1)}), bf16[32,32,1024]{2,0,1:T(8,128)(2,1)}, u32[]{:S(2)}, u32[]{:S(2)}) %all-to-all-start.4) | async-done | bytes 2097184 | tf_op jit(solution)/shard_map/all_to_all | solution.py:339
  157.7 40.7 %all-to-all-done.1 = bf16[32,32,1024]{2,0,1:T(8,128)(2,1)} async-done(((bf16[32,32,1024]{2,0,1:T(8,128)(2,1)}), bf16[32,32,1024]{2,0,1:T(8,128)(2,1)}, u32[]{:S(2)}, u32[]{:S(2)}) %all-to-all-start.1) | async-done | bytes 2097184 | tf_op jit(solution)/shard_map/all_to_all | solution.py:355
  205.4 73.5 %all-reduce.18 = (bf16[1024]{0:T(1024)(128)(2,1)S(1)}, bf16[1024]{0:T(1024)(128)(2,1)S(1)}, bf16[1024]{0:T(1024)(128)(2,1)S(1)}, bf16[1024]{0:T(1024)(128)(2,1)S...) all-reduce(bf16[1024]{0:T(1024)(128)(2,1)S(1)} %dynamic-update-slic, ...), channel_id=1, replica_groups=mesh['dp'=32] {'dp'}, use_global_device_ids=true, to_apply=%add | all-reduce | flops 8192 | bytes 32768
  280.7 40.3 %all-gather = bf16[32,1,128]{2,1,0:T(2,128)(2,1)S(1)} all-gather(bf16[1,1,128]{2,1,0:T(2,128)(2,1)S(1)} %bitcast.238), channel_id=1, replica_groups=mesh['dp'=32] {'dp'}, dimensions={0}, use_global_device_ids=true | all-gather | bytes 8448 | tf_op jit(solution)/shard_map/all_gather | solution.py:378
  440.3 49.4 %multiply_convert_fusion.3 = (bf16[512,4096]{1,0:T(8,128)(2,1)}, f32[512,4096]{1,0:T(8,128)}, bf16[512,4096]{1,0:T(8,128)(2,1)}, f32[512,4096]{1,0:T(8,128)}, f32[512,4096]{1,0:T(8,128)}) fusion(f32[4096]{0:T(1024)S(1)} %bitcast.233, f32[512,4096]{1,0:T(8,128)S(1)} %fusion.42, bf16[1024,4096]{1,0:T(8,128)(2,1)S(1)} %copy-done.102, ...), kind=kOutput, calls=%fused_computation.40 | convolution fusion | flops 4574412800 | bytes 52457472 | tf_op jit(solution)/shard_map/dot_general | solution.py:126
  489.8 10.0 fusion.60
  520.2 26.9 %convert_reduce_fusion.1 = (f32[4096]{0:T(1024)}, bf16[512,4096]{1,0:T(8,128)(2,1)}, f32[4096]{0:T(1024)}, bf16[512,4096]{1,0:T(8,128)(2,1)}) fusion(f32[512,4096]{1,0:T(8,128)} %get-tuple-element.67, f32[512,4096]{1,0:T(8,128)} %get-tuple-element.105, f32[4096]{0:T(1024)S(1)} %bitcast.234, f32[512,4096]{1,0:T(8,128)} %fusion.64, ...), kind=kOutput, calls=%fused_computation.24 | convolution fusion | flops 4366262272 | bytes 59817984 | tf_op jit(solution)/shard_map/rd,fd->rf/dot_general | solution.py:195
  557.0 12.7 multiply_reduce_fusion.3
  616.1 14.5 multiply_reduce_fusion.1
  630.6 12.4 multiply_convert_fusion.1
  648.9 12.0 multiply_reduce_fusion
  660.9 12.6 multiply_convert_fusion
  700.2 13.5 fusion.44
  713.7 11.9 convolution_add_fusion
  726.8 10.6 fusion.71
  737.4 11.7 convolution_add_fusion.1
  771.2 41.3 %all-to-all-done.2 = bf16[32,32,1024]{2,0,1:T(8,128)(2,1)S(1)} async-done(((bf16[32,32,1024]{2,0,1:T(8,128)(2,1)}), bf16[32,32,1024]{2,0,1:T(8,128)(2,1)S(1)}, u32[]{:S(2)}, u32[]{:S(2)}) %all-to-all-start.2) | async-done | bytes 2097184 | tf_op jit(solution)/shard_map/all_to_all | solution.py:413
  828.5 41.8 %all-to-all-done.6 = bf16[32,32,1024]{2,0,1:T(8,128)(2,1)} async-done(((bf16[32,32,1024]{2,0,1:T(8,128)(2,1)}), bf16[32,32,1024]{2,0,1:T(8,128)(2,1)}, u32[]{:S(2)}, u32[]{:S(2)}) %all-to-all-start.6) | async-done | bytes 2097184 | tf_op jit(solution)/shard_map/all_to_all | solution.py:420
  886.7 44.0 %all-to-all-done.3 = bf16[32,32,1024]{2,0,1:T(8,128)(2,1)} async-done(((bf16[32,32,1024]{2,0,1:T(8,128)(2,1)}), bf16[32,32,1024]{2,0,1:T(8,128)(2,1)}, u32[]{:S(2)}, u32[]{:S(2)}) %all-to-all-start.3) | async-done | bytes 2097184 | tf_op jit(solution)/shard_map/all_to_all | solution.py:435
  934.9 76.3 %all-reduce.17 = (f32[1024]{0:T(1024)S(1)}, f32[1024]{0:T(1024)S(1)}, f32[1024]{0:T(1024)S(1)}, f32[4096]{0:T(1024)S(1)}, f32[1024]{0:T(1024)S(1)}, /*index=5*/f...) all-reduce(f32[1024]{0:T(1024)S(1)} %add.457, ...), channel_id=8, replica_groups=mesh['dp'=32] {'dp'}, use_global_device_ids=true, to_apply=%region_39.40.clone | all-reduce | flops 12288 | bytes 98304
  1024.6 134.6 %reduce-scatter.9.cloned.1.call-done = f32[32,1024]{1,0:T(8,128)} async-done(((f32[1024,1024]{1,0:T(8,128)}), f32[32,1024]{1,0:T(8,128)}) %reduce-scatter.9.cloned.1.call-update) | async-done | bytes 131088 | tf_op jit(solution)/shard_map/reduce_scatter | solution.py:409
  1159.2 181.6 %reduce-scatter.15.cloned.1.call-done = f32[32,4096]{1,0:T(8,128)} async-done(((f32[1024,4096]{1,0:T(8,128)}), f32[32,4096]{1,0:T(8,128)}) %reduce-scatter.15.cloned.1.call-update) | async-done | bytes 524304 | tf_op jit(solution)/shard_map/reduce_scatter | solution.py:409
  1340.8 187.4 %reduce-scatter.17.cloned.1.call-done = f32[128,1024]{1,0:T(8,128)} async-done(((f32[4096,1024]{1,0:T(8,128)}), f32[128,1024]{1,0:T(8,128)}) %reduce-scatter.17.cloned.1.call-update) | async-done | bytes 524304 | tf_op jit(solution)/shard_map/reduce_scatter | solution.py:409
  (454 shorter events, 367.9 us)
Async XLA Ops:
  7.2 318.8 %all-gather.12.cloned.1.call-start = ((), (), s32[]{:S(2)}) async-start(), calls=%async_computation.16 | async-start | bytes 2162688 | tf_op jit(solution)/shard_map/all_gather | solution.py:370
  7.9 324.5 %all-gather.10.cloned.1.call-start = ((), (), s32[]{:S(2)}) async-start(), calls=%async_computation.15 | async-start | bytes 2162688 | tf_op jit(solution)/shard_map/all_gather | solution.py:369
  8.7 329.9 %all-gather.8.cloned.1.call-start = ((), (), s32[]{:S(2)}) async-start(), calls=%async_computation.14 | async-start | bytes 2162688 | tf_op jit(solution)/shard_map/all_gather | solution.py:371
  9.4 387.6 %all-gather.14.cloned.1.call-start = ((), (), s32[]{:S(2)}) async-start(), calls=%async_computation.17 | async-start | bytes 2162688 | tf_op jit(solution)/shard_map/all_gather | solution.py:372
  10.0 419.7 %all-gather.16.cloned.1.call-start = ((), (), s32[]{:S(2)}) async-start(), calls=%async_computation.18 | async-start | bytes 8650752 | tf_op jit(solution)/shard_map/all_gather | solution.py:373
  14.6 66.1 %all-to-all-start = ((bf16[32,32,1024]{2,0,1:T(8,128)(2,1)}), bf16[32,32,1024]{2,0,1:T(8,128)(2,1)S(1)}, u32[]{:S(2)}, u32[]{:S(2)}) async-start(bf16[32,32,1024]{2,0,1:T(8,128)(2,1)} %copy.140), calls=%async_computation | async-start | bytes 4194304 | tf_op jit(solution)/shard_map/all_to_all | solution.py:332
  21.9 63.0 %copy-start.99 = (s32[256]{0:T(256)S(1)}, s32[256]{0:T(256)}, u32[]{:S(2)}) copy-start(s32[256]{0:T(256)} %param.22) | copy-start | bytes 3076
  80.7 59.9 %all-to-all-start.4 = ((bf16[32,32,1024]{2,0,1:T(8,128)(2,1)}), bf16[32,32,1024]{2,0,1:T(8,128)(2,1)}, u32[]{:S(2)}, u32[]{:S(2)}) async-start(bf16[32,32,1024]{2,0,1:T(8,128)(2,1)} %copy.157), calls=%async_computation.4 | async-start | bytes 4194304 | tf_op jit(solution)/shard_map/all_to_all | solution.py:339
  140.6 57.8 %all-to-all-start.1 = ((bf16[32,32,1024]{2,0,1:T(8,128)(2,1)}), bf16[32,32,1024]{2,0,1:T(8,128)(2,1)}, u32[]{:S(2)}, u32[]{:S(2)}) async-start(bf16[32,32,1024]{2,0,1:T(8,128)(2,1)} %copy.142), calls=%async_computation.1 | async-start | bytes 4194304 | tf_op jit(solution)/shard_map/all_to_all | solution.py:355
  153.6 127.1 %copy-start.101 = (bf16[128]{0:T(256)(128)(2,1)S(1)}, bf16[128]{0:T(256)(128)(2,1)}, u32[]{:S(2)}) copy-start(bf16[128]{0:T(256)(128)(2,1)} %param.32) | copy-start | bytes 772
  198.4 167.0 %all-to-all-start.5 = ((bf16[32,32,1024]{2,0,1:T(8,128)(2,1)}), bf16[32,32,1024]{2,0,1:T(8,128)(2,1)S(1)}, u32[]{:S(2)}, u32[]{:S(2)}) async-start(bf16[32,32,1024]{2,0,1:T(8,128)(2,1)} %copy.159), calls=%async_computation.5 | async-start | bytes 4194304 | tf_op jit(solution)/shard_map/all_to_all | solution.py:356
  202.5 287.2 %all-gather.18.cloned.1.call-start = ((), (), s32[]{:S(2)}) async-start(), calls=%async_computation.19 | async-start | bytes 8650752 | tf_op jit(solution)/shard_map/all_gather | solution.py:374
  203.1 821.6 %reduce-scatter.13.cloned.1.call-start = ((), (), s32[]{:S(2)}) async-start(), calls=%async_computation.23 | async-start | bytes 4325376 | tf_op jit(solution)/shard_map/reduce_scatter | solution.py:409
  278.9 221.2 %copy-start.70 = (f32[1024]{0:T(1024)}, f32[1024]{0:T(1024)S(1)}, u32[]{:S(2)}) copy-start(f32[1024]{0:T(1024)S(1)} %convert_element_type.233) | copy-start | bytes 12292
  322.5 65.4 %copy-start.31 = (pred[512,512]{0,1:T(8,128)(4,1)}, pred[512,512]{0,1:T(8,128)(4,1)S(1)}, u32[]{:S(2)}) copy-start(pred[512,512]{0,1:T(8,128)(4,1)S(1)} %get-tuple-element.125) | copy-start | bytes 786436
  579.4 445.2 %reduce-scatter.11.cloned.1.call-start = ((), (), s32[]{:S(2)}) async-start(), calls=%async_computation.22 | async-start | bytes 4325376 | tf_op jit(solution)/shard_map/reduce_scatter | solution.py:409
  615.9 408.7 %reduce-scatter.7.cloned.1.call-start = ((), (), s32[]{:S(2)}) async-start(), calls=%async_computation.20 | async-start | bytes 4325376 | tf_op jit(solution)/shard_map/reduce_scatter | solution.py:409
  681.1 478.1 %reduce-scatter.9.cloned.1.call-start = ((), (), s32[]{:S(2)}) async-start(), calls=%async_computation.21 | async-start | bytes 4325376 | tf_op jit(solution)/shard_map/reduce_scatter | solution.py:409
  699.6 641.2 %reduce-scatter.15.cloned.1.call-start = ((), (), s32[]{:S(2)}) async-start(), calls=%async_computation.24 | async-start | bytes 17301504 | tf_op jit(solution)/shard_map/reduce_scatter | solution.py:409
  725.6 802.5 %reduce-scatter.17.cloned.1.call-start = ((), (), s32[]{:S(2)}) async-start(), calls=%async_computation.25 | async-start | bytes 17301504 | tf_op jit(solution)/shard_map/reduce_scatter | solution.py:409
  753.3 59.2 %all-to-all-start.2 = ((bf16[32,32,1024]{2,0,1:T(8,128)(2,1)}), bf16[32,32,1024]{2,0,1:T(8,128)(2,1)S(1)}, u32[]{:S(2)}, u32[]{:S(2)}) async-start(bf16[32,32,1024]{2,0,1:T(8,128)(2,1)} %copy.153), calls=%async_computation.2 | async-start | bytes 4194304 | tf_op jit(solution)/shard_map/all_to_all | solution.py:413
  812.5 57.8 %all-to-all-start.6 = ((bf16[32,32,1024]{2,0,1:T(8,128)(2,1)}), bf16[32,32,1024]{2,0,1:T(8,128)(2,1)}, u32[]{:S(2)}, u32[]{:S(2)}) async-start(bf16[32,32,1024]{2,0,1:T(8,128)(2,1)} %copy.170), calls=%async_computation.6 | async-start | bytes 4194304 | tf_op jit(solution)/shard_map/all_to_all | solution.py:420
  870.3 60.4 %all-to-all-start.3 = ((bf16[32,32,1024]{2,0,1:T(8,128)(2,1)}), bf16[32,32,1024]{2,0,1:T(8,128)(2,1)}, u32[]{:S(2)}, u32[]{:S(2)}) async-start(bf16[32,32,1024]{2,0,1:T(8,128)(2,1)} %copy.155), calls=%async_computation.3 | async-start | bytes 4194304 | tf_op jit(solution)/shard_map/all_to_all | solution.py:435
  930.7 89.9 %all-to-all-start.7 = ((bf16[32,32,1024]{2,0,1:T(8,128)(2,1)}), bf16[32,32,1024]{2,0,1:T(8,128)(2,1)}, u32[]{:S(2)}, u32[]{:S(2)}) async-start(bf16[32,32,1024]{2,0,1:T(8,128)(2,1)} %copy.172), calls=%async_computation.7 | async-start | bytes 4194304 | tf_op jit(solution)/shard_map/all_to_all | solution.py:436
  (114 other events, 1794.5 us)
Sparse Core Ops, SparseCore 0:
  10.9 71.6 all-gather.11
  85.4 60.9 all-gather.9
  149.3 65.8 all-gather.7
  217.9 62.0 all-gather.13
  282.8 76.2 all-gather.15
  361.8 76.0 all-gather.17
  579.6 136.7 reduce-scatter.12
  719.2 147.4 reduce-scatter.10
  869.6 148.9 reduce-scatter.6
  1021.3 137.8 reduce-scatter.8
  1162.1 178.6 reduce-scatter.14
  1343.5 184.6 reduce-scatter.16
where the time goes:
time: 1550 us; the launch traced here: 1540 us
  waiting for transfers between devices  767 us (49%)
  matrix products  333 us (21%)
  blocking collectives  190 us (12%)
  local copies, waits for them, and re-layouts  129 us (8%)
  other arithmetic  63.8 us (4%)
  starting transfers between devices  36.1 us (2%)
  between operations  16.1 us (1%)
    reduce_scatter x6, waiting for transfers between devices, local(): lax.psum_scatter(totals, 'dp', scatter_dimension=0, tiled=True)  504 us
    unnamed x2, blocking collectives  150 us
    dot_general x2, matrix products, forward_pass(): jnp.dot(first_low, up_weight, preferred_element_type=jnp.float32)  56.7 us
    all_to_all x1, waiting for transfers between devices, local(): lax.all_to_all(tokens.reshape(blocks, devices, model_width), 'dp', split_...  54.7 us
    all_to_all x1, waiting for transfers between devices, local(): lax.all_to_all(held_out, 'dp', split_axis=1, concat_axis=1, tiled=True)  44 us
    all_to_all x1, waiting for transfers between devices, local(): lax.all_to_all(token_gradient.reshape(blocks, devices, model_width), 'dp'...  41.8 us
    all_to_all x1, waiting for transfers between devices, local(): lax.all_to_all(layer_out.reshape(blocks, devices, model_width), 'dp', spl...  41.3 us
    all_to_all x1, waiting for transfers between devices, local(): lax.all_to_all(send_tokens, 'dp', split_axis=1, concat_axis=1, tiled=True)  40.7 us
  transfers between devices with their start and end apart: 20, of which 9 were waited for; matrix products, arithmetic and copies ran while one was open for 27% of the time, Pallas kernels for 0%

commit v1 on v0

v1 whole, which is shorter than its diff:
```python
import functools

import jax
import jax.numpy as jnp
from jax import lax
from jax.experimental import pallas as pl
from jax.experimental.pallas import tpu as pltpu
from jax.sharding import PartitionSpec as P

HD = 64
GRAN = 128
HALO = 384
EPS = 1e-12
F32 = jnp.float32
BF16 = jnp.bfloat16
NT = (((1,), (1,)), ((), ()))
ANY = pl.BlockSpec(memory_space=pl.ANY)


def params(limit=56):
    return pltpu.CompilerParams(vmem_limit_bytes=limit << 20)


def whole(shape):
    return pl.BlockSpec(shape, lambda *_: (0,) * len(shape))


def dot(a, b):
    return jnp.dot(a, b, preferred_element_type=F32)


def dot_nt(a, b):
    return lax.dot_general(a, b, NT, preferred_element_type=F32)


def cost(flops, nbytes, trans=0):
    return pl.CostEstimate(flops=flops, bytes_accessed=nbytes, transcendentals=trans)


def qkv_kernel(xl, xo, xr, wq, wk, wv, vec, q, k, v):
    rows = xo.shape[0]
    for w, out, b in ((wq, q, vec[0:1, :]), (wk, k, None), (wv, v, vec[1:2, :])):
        def put(x, start, size):
            r = dot(x, w[...])
            if b is not None:
                r = r + b
            out[pl.ds(start, size), :] = r.astype(BF16)

        put(xl[...], 0, HALO)
        put(xr[...], HALO + rows, HALO)

        def step(i, c):
            s = pl.multiple_of(i * 256, 256)
            put(xo[pl.ds(s, 256), :], pl.multiple_of(HALO + s, 128), 256)
            return c

        lax.fori_loop(0, rows // 256, step, 0)


def qkv_call(xl, xo, xr, wq, wk, wv, vec):
    rows, d = xo.shape
    win = rows + 2 * HALO
    tn = 512
    wspec = pl.BlockSpec((d, tn), lambda j: (0, j))
    ospec = pl.BlockSpec((win, tn), lambda j: (0, j))
    out = jax.ShapeDtypeStruct((win, d), BF16)
    return pl.pallas_call(
        qkv_kernel,
        grid=(d // tn,),
        in_specs=[whole(xl.shape), whole(xo.shape), whole(xr.shape), wspec, wspec, wspec,
                  pl.BlockSpec((8, tn), lambda j: (0, j))],
        out_specs=[ospec] * 3,
        out_shape=[out] * 3,
        compiler_params=params(),
        cost_estimate=cost(6 * win * d * d, 2 * (4 * win * d + 3 * d * d)),
        name="qkv",
    )(xl, xo, xr, wq, wk, wv, vec)


def probs_t(k, qh):
    st = dot_nt(k, qh)
    e = jnp.exp(st - jnp.max(st, axis=0, keepdims=True))
    return e * (1.0 / jnp.sum(e, axis=0, keepdims=True))


def attn_fwd_kernel(tab, q_ref, k_ref, v_ref, o_ref, ctx):
    blocks = o_ref.shape[0] // GRAN

    def one(b, c):
        n = tab[1, b]
        s0 = tab[0, b]
        for nn in range(1, 5):
            @pl.when(n == nn)
            def _():
                size = nn * GRAN
                rows = pl.ds(pl.multiple_of(s0 * GRAN, GRAN), size)
                q = q_ref[rows, :] * jnp.asarray(0.125, BF16)
                k = k_ref[rows, :]
                vt = v_ref[rows, :].T
                low = lax.broadcasted_iota(jnp.int32, q.shape, 1) < HD
                parts = []
                for h in range(2):
                    qh = jnp.where(low if h == 0 else ~low, q, jnp.zeros_like(q))
                    p = probs_t(k, qh).astype(BF16)
                    parts.append(dot(vt[h * HD:(h + 1) * HD, :], p))
                ctx[rows, :] = jnp.concatenate(parts, axis=0).T.astype(BF16)
        return c

    lax.fori_loop(0, blocks, one, 0)
    o_ref[...] = ctx[pl.ds(HALO, o_ref.shape[0]), :]


def attn_fwd_call(tab, q, k, v, rows):
    win, d = q.shape
    spec = pl.BlockSpec((win, 2 * HD), lambda h, t: (0, h))
    return pl.pallas_call(
        attn_fwd_kernel,
        grid_spec=pltpu.PrefetchScalarGridSpec(
            num_scalar_prefetch=1,
            grid=(d // (2 * HD),),
            in_specs=[spec] * 3,
            out_specs=pl.BlockSpec((rows, 2 * HD), lambda h, t: (0, h)),
            scratch_shapes=[pltpu.VMEM((win, 2 * HD), BF16)],
        ),
        out_shape=jax.ShapeDtypeStruct((rows, d), BF16),
        compiler_params=params(),
        cost_estimate=cost(8 * rows * 512 * d, 8 * win * d, rows * 512 * 16),
        name="attn_fwd",
    )(tab, q, k, v)


def attn_bwd_kernel(tab, q_ref, k_ref, v_ref, gl, go, gr, dq_o, dk_o, dv_o, g_s, dq_s, dk_s, dv_s):
    rows_own = go.shape[0]
    blocks = rows_own // GRAN
    g_s[pl.ds(0, HALO), :] = gl[...]
    g_s[pl.ds(HALO, rows_own), :] = go[...]
    g_s[pl.ds(HALO + rows_own, HALO), :] = gr[...]

    def one(b, c):
        n = tab[1, b]
        s0 = tab[0, b]
        for nn in range(1, 5):
            @pl.when(n == nn)
            def _():
                size = nn * GRAN
                rows = pl.ds(pl.multiple_of(s0 * GRAN, GRAN), size)
                q = q_ref[rows, :] * jnp.asarray(0.125, BF16)
                k = k_ref[rows, :]
                v = v_ref[rows, :]
                g = g_s[rows, :]
                kt = (k * jnp.asarray(0.125, BF16)).T
                low = lax.broadcasted_iota(jnp.int32, q.shape, 1) < HD
                zero = jnp.zeros_like(q)
                dqs, dks, dvs = [], [], []
                for h in range(2):
                    mine = low if h == 0 else ~low
                    p = probs_t(k, jnp.where(mine, q, zero))
                    dp = dot_nt(v, jnp.where(mine, g, zero))
                    delta = jnp.sum(p * dp, axis=0, keepdims=True)
                    ds = (p * (dp - delta)).astype(BF16)
                    dvs.append(dot(p.astype(BF16), g))
                    dks.append(dot(ds, q))
                    dqs.append(dot(kt[h * HD:(h + 1) * HD, :], ds))
                dq_s[rows, :] = jnp.concatenate(dqs, axis=0).T.astype(BF16)
                dk_s[rows, :] = jnp.where(low, dks[0], dks[1]).astype(BF16)
                dv_s[rows, :] = jnp.where(low, dvs[0], dvs[1]).astype(BF16)
        return c

    lax.fori_loop(0, blocks, one, 0)
    own = pl.ds(HALO, rows_own)
    dq_o[...] = dq_s[own, :]
    dk_o[...] = dk_s[own, :]
    dv_o[...] = dv_s[own, :]


def attn_bwd_call(tab, q, k, v, gl, go, gr):
    win, d = q.shape
    rows = go.shape[0]
    spec = pl.BlockSpec((win, 2 * HD), lambda h, t: (0, h))
    own = pl.BlockSpec((rows, 2 * HD), lambda h, t: (0, h))
    halo = pl.BlockSpec((HALO, 2 * HD), lambda h, t: (0, h))
    out = jax.ShapeDtypeStruct((rows, d), BF16)
    return pl.pallas_call(
        attn_bwd_kernel,
        grid_spec=pltpu.PrefetchScalarGridSpec(
            num_scalar_prefetch=1,
            grid=(d // (2 * HD),),
            in_specs=[spec] * 3 + [halo, own, halo],
            out_specs=[own] * 3,
            scratch_shapes=[pltpu.VMEM((win, 2 * HD), BF16)] * 4,
        ),
        out_shape=[out] * 3,
        compiler_params=params(),
        cost_estimate=cost(20 * rows * 512 * d, 14 * win * d, rows * 512 * 16),
        name="attn_bwd",
    )(tab, q, k, v, gl, go, gr)


def norm_stats(z):
    cen = z - jnp.mean(z, axis=-1, keepdims=True)
    r = lax.rsqrt(jnp.mean(cen * cen, axis=-1, keepdims=True) + EPS)
    return cen * r, r


def norm_back(e, n, r):
    return r * (e - jnp.mean(e, axis=-1, keepdims=True) - n * jnp.mean(e * n, axis=-1, keepdims=True))


def out_proj_kernel(ctx, w, x, vec, xhat, low, r_o):
    z = x[...].astype(F32) + (dot(ctx[...], w[...]) + vec[2:3, :])
    n, r = norm_stats(z)
    xhat[...] = n
    r_o[...] = jnp.broadcast_to(r, r_o.shape)
    low[...] = (n * vec[4:5, :] + vec[5:6, :]).astype(BF16)


def out_proj_call(ctx, w, x, vec):
    rows, d = x.shape
    tm = 256
    t = pl.BlockSpec((tm, d), lambda i: (i, 0))
    return pl.pallas_call(
        out_proj_kernel,
        grid=(rows // tm,),
        in_specs=[t, whole(w.shape), t, whole(vec.shape)],
        out_specs=[t, t, pl.BlockSpec((tm, 128), lambda i: (i, 0))],
        out_shape=[jax.ShapeDtypeStruct((rows, d), F32), jax.ShapeDtypeStruct((rows, d), BF16),
                   jax.ShapeDtypeStruct((rows, 128), F32)],
        compiler_params=params(),
        cost_estimate=cost(2 * rows * d * d, rows * d * 10 + 2 * d * d),
        name="out_proj",
    )(ctx, w, x, vec)


RC = 256


def chunks(rows, fn):
    def step(i, c):
        fn(pl.ds(pl.multiple_of(i * RC, RC), RC))
        return c

    lax.fori_loop(0, rows // RC, step, 0)


def ffn_fwd_kernel(low, wu, bu, wd, xhat, g, vec, hid, dg, out, gs, sums, acc):
    rows = low.shape[0]
    t = pl.program_id(0)

    @pl.when(t == 0)
    def _():
        acc[...] = jnp.zeros_like(acc)

    def up(r):
        u = dot(low[r, :], wu[...]) + bu[...]
        phi = 0.5 * (1.0 + lax.erf(u * (0.5 ** 0.5)))
        h = (u * phi).astype(BF16)
        hid[r, :] = h
        dg[r, :] = (phi + u * (0.3989422804014327 * jnp.exp(-0.5 * u * u))).astype(BF16)
        acc[r, :] += dot(h, wd[...])

    chunks(rows, up)

    @pl.when(t == pl.num_programs(0) - 1)
    def _():
        sums[...] = jnp.zeros_like(sums)

        def fin(r):
            z = (xhat[r, :] * vec[4:5, :] + vec[5:6, :]) + (acc[r, :] + vec[3:4, :])
            n, rr = norm_stats(z)
            out[r, :] = (n * vec[6:7, :] + vec[7:8, :]).astype(BF16)
            gv = g[r, :].astype(F32)
            sums[0:1, :] += jnp.sum(gv * n, axis=0, keepdims=True)
            sums[1:2, :] += jnp.sum(gv, axis=0, keepdims=True)
            grad = norm_back(gv * vec[6:7, :], n, rr)
            gs[r, :] = grad
            sums[2:3, :] += jnp.sum(grad.astype(BF16).astype(F32), axis=0, keepdims=True)

        chunks(rows, fin)


def ffn_fwd_call(low, wu, bu, wd, xhat, g, vec):
    rows, d = low.shape
    ff = wu.shape[1]
    tf = 512
    col = pl.BlockSpec((rows, tf), lambda t: (0, t))
    return pl.pallas_call(
        ffn_fwd_kernel,
        grid=(ff // tf,),
        in_specs=[whole(low.shape), pl.BlockSpec((d, tf), lambda t: (0, t)), pl.BlockSpec((1, tf), lambda t: (0, t)),
                  pl.BlockSpec((tf, d), lambda t: (t, 0)), whole(xhat.shape), whole(g.shape), whole(vec.shape)],
        out_specs=[col, col, whole((rows, d)), whole((rows, d)), whole((8, d))],
        out_shape=[jax.ShapeDtypeStruct((rows, ff), BF16), jax.ShapeDtypeStruct((rows, ff), BF16),
                   jax.ShapeDtypeStruct((rows, d), BF16), jax.ShapeDtypeStruct((rows, d), F32),
                   jax.ShapeDtypeStruct((8, d), F32)],
        scratch_shapes=[pltpu.VMEM((rows, d), F32)],
        compiler_params=params(),
        cost_estimate=cost(4 * rows * d * ff, 4 * d * ff + 4 * rows * ff + rows * d * 14, 2 * rows * ff),
        name="ffn_fwd",
    )(low, wu, bu, wd, xhat, g, vec)


def ffn_bwd_kernel(low, gs, hid, dg, wu, wd, xhat, r1, vec, dwd, dwu, gsf, sums, sumu, acc, gd, lowt, gu):
    rows = low.shape[0]
    t = pl.program_id(0)
    tf = hid.shape[1]

    @pl.when(t == 0)
    def _():
        acc[...] = gs[...]
        gd[...] = gs[...].astype(BF16)
        lowt[...] = low[...].T

    sumu[...] = jnp.zeros_like(sumu)

    def back(r):
        gh = dot_nt(gd[r, :], wd[...])
        g = (gh * dg[r, :].astype(F32)).astype(BF16)
        gu[r, :] = g
        sumu[...] += jnp.sum(g.astype(F32), axis=0, keepdims=True)
        acc[r, :] += dot_nt(g, wu[...])

    chunks(rows, back)
    for j in range(tf // 256):
        c = slice(j * 256, (j + 1) * 256)
        dwd[c, :] = dot(hid[:, c].T, gd[...]).astype(BF16)

    def wgrad(r):
        dwu[r, :] = dot(lowt[r, :], gu[...]).astype(BF16)

    chunks(lowt.shape[0], wgrad)

    @pl.when(t == pl.num_programs(0) - 1)
    def _():
        sums[...] = jnp.zeros_like(sums)

        def fin(r):
            gf = acc[r, :]
            n = xhat[r, :]
            sums[0:1, :] += jnp.sum(gf * n, axis=0, keepdims=True)
            sums[1:2, :] += jnp.sum(gf, axis=0, keepdims=True)
            grad = norm_back(gf * vec[4:5, :], n, r1[r, 0:1])
            gsf[r, :] = grad
            sums[2:3, :] += jnp.sum(grad.astype(BF16).astype(F32), axis=0, keepdims=True)

        chunks(rows, fin)


def ffn_bwd_call(low, gs, hid, dg, wu, wd, xhat, r1, vec):
    rows, d = low.shape
    ff = wu.shape[1]
    tf = 512
    col = pl.BlockSpec((rows, tf), lambda t: (0, t))
    wus = pl.BlockSpec((d, tf), lambda t: (0, t))
    wds = pl.BlockSpec((tf, d), lambda t: (t, 0))
    once = dict(pipeline_mode=pl.Buffered(1))

    def one(shape):
        return pl.BlockSpec(shape, lambda *_: (0,) * len(shape), **once)

    return pl.pallas_call(
        ffn_bwd_kernel,
        grid=(ff // tf,),
        in_specs=[one(low.shape), one(gs.shape), col, col, wus, wds, one(xhat.shape), one(r1.shape), one(vec.shape)],
        out_specs=[wds, wus, whole((rows, d)), whole((8, d)), pl.BlockSpec((1, tf), lambda t: (0, t))],
        out_shape=[jax.ShapeDtypeStruct((ff, d), BF16), jax.ShapeDtypeStruct((d, ff), BF16),
                   jax.ShapeDtypeStruct((rows, d), F32), jax.ShapeDtypeStruct((8, d), F32),
                   jax.ShapeDtypeStruct((1, ff), F32)],
        scratch_shapes=[pltpu.VMEM((rows, d), F32), pltpu.VMEM((rows, d), BF16), pltpu.VMEM((d, rows), BF16),
                        pltpu.VMEM((rows, tf), BF16)],
        compiler_params=params(),
        cost_estimate=cost(8 * rows * d * ff, 8 * d * ff + 4 * rows * ff + rows * d * 18),
        name="ffn_bwd",
    )(low, gs, hid, dg, wu, wd, xhat, r1, vec)


def out_bwd_kernel(gsf, ctx, w, gc, dwo, ga, ctxt):
    rows = gsf.shape[0]

    def cast(r):
        ga[r, :] = gsf[r, :].astype(BF16)
        gc[r, :] = dot_nt(ga[r, :], w[...]).astype(BF16)

    chunks(rows, cast)
    ctxt[...] = ctx[...].T

    def wgrad(r):
        dwo[r, :] = dot(ctxt[r, :], ga[...]).astype(BF16)

    chunks(ctxt.shape[0], wgrad)


def out_bwd_call(gsf, ctx, w):
    rows, d = gsf.shape
    return pl.pallas_call(
        out_bwd_kernel,
        grid=(1,),
        in_specs=[whole(gsf.shape), whole(ctx.shape), whole(w.shape)],
        out_specs=[whole((rows, d)), whole((d, d))],
        out_shape=[jax.ShapeDtypeStruct((rows, d), BF16), jax.ShapeDtypeStruct((d, d), BF16)],
        scratch_shapes=[pltpu.VMEM((rows, d), BF16), pltpu.VMEM((d, rows), BF16)],
        compiler_params=params(),
        cost_estimate=cost(4 * rows * d * d, rows * d * 8 + 4 * d * d),
        name="out_bwd",
    )(gsf, ctx, w)


def in_bwd_kernel(x, gsf, dq, dk, dv, wq, wk, wv, tg, dwq, dwk, dwv, sums, xt):
    rows = x.shape[0]
    xt[...] = x[...].T
    sums[...] = jnp.zeros_like(sums)

    def tok(r):
        g = gsf[r, :] + dot_nt(dq[r, :], wq[...]) + dot_nt(dk[r, :], wk[...]) + dot_nt(dv[r, :], wv[...])
        tg[r, :] = g.astype(BF16)
        sums[0:1, :] += jnp.sum(dq[r, :].astype(F32), axis=0, keepdims=True)
        sums[1:2, :] += jnp.sum(dv[r, :].astype(F32), axis=0, keepdims=True)

    chunks(rows, tok)

    def wgrad(r):
        dwq[r, :] = dot(xt[r, :], dq[...]).astype(BF16)
        dwk[r, :] = dot(xt[r, :], dk[...]).astype(BF16)
        dwv[r, :] = dot(xt[r, :], dv[...]).astype(BF16)

    chunks(xt.shape[0], wgrad)


def in_bwd_call(x, gsf, dq, dk, dv, wq, wk, wv):
    rows, d = x.shape
    once = dict(pipeline_mode=pl.Buffered(1))

    def one(shape):
        return pl.BlockSpec(shape, lambda *_: (0,) * len(shape), **once)

    return pl.pallas_call(
        in_bwd_kernel,
        grid=(1,),
        in_specs=[one((rows, d))] * 5 + [one((d, d))] * 3,
        out_specs=[one((rows, d))] + [one((d, d))] * 3 + [one((8, d))],
        out_shape=[jax.ShapeDtypeStruct((rows, d), BF16)] + [jax.ShapeDtypeStruct((d, d), BF16)] * 3
        + [jax.ShapeDtypeStruct((8, d), F32)],
        scratch_shapes=[pltpu.VMEM((d, rows), BF16)],
        compiler_params=params(),
        cost_estimate=cost(12 * rows * d * d, rows * d * 14 + 12 * d * d),
        name="in_bwd",
    )(x, gsf, dq, dk, dv, wq, wk, wv)


def sequence_table(lengths, own, rows):
    ids = jnp.arange(lengths.shape[0], dtype=jnp.int32)
    starts = jnp.sum(jnp.where(ids[None, :] < ids[:, None], lengths[None, :], 0), axis=1)
    blocks = rows // GRAN
    at = own * rows + jnp.arange(blocks, dtype=jnp.int32) * GRAN
    inside = (starts[None, :] <= at[:, None]) & (at[:, None] < (starts + lengths)[None, :])
    first = jnp.sum(jnp.where(inside, starts[None, :], 0), axis=1)
    length = jnp.sum(jnp.where(inside, lengths[None, :], 0), axis=1)
    lead = (first == at) | (jnp.arange(blocks) == 0)
    return jnp.stack([(first - own * rows + HALO) // GRAN, jnp.where(lead, length // GRAN, 0)]).astype(jnp.int32)


def halo(x, n):
    right = [(i, i + 1) for i in range(n - 1)]
    left = [(i + 1, i) for i in range(n - 1)]
    return lax.ppermute(x[-HALO:], "dp", right), lax.ppermute(x[:HALO], "dp", left)


def local(tokens, cotangent, lengths, dealing, *shards):
    n = lax.axis_size("dp")
    own = lax.axis_index("dp")
    rows, d = tokens.shape
    part = d // n
    wq, wk, wv, wo, wu, wd = (lax.all_gather(s, "dp", axis=0, tiled=True) for s in shards[:6])
    qb, vb, ob, ub, db, fg, fs, sg, ss = shards[6:]
    packed = jnp.concatenate([qb, vb, ob, db, fg, fs, sg, ss, ub])
    gathered = lax.all_gather(packed, "dp", axis=0, tiled=False)
    vec = gathered[:, : 8 * part].reshape(n, 8, part).transpose(1, 0, 2).reshape(8, d).astype(F32)
    bu = gathered[:, 8 * part:].reshape(1, -1).astype(F32)
    tab = sequence_table(lengths, own, rows)
    xl, xr = halo(tokens, n)
    q, k, v = qkv_call(xl, tokens, xr, wq, wk, wv, vec)
    ctx = attn_fwd_call(tab, q, k, v, rows)
    xhat, low, r1 = out_proj_call(ctx, wo, tokens, vec)
    hid, dg, layer_out, gs, sums2 = ffn_fwd_call(low, wu, bu, wd, xhat, cotangent, vec)
    dwd, dwu, gsf, sums1, sumu = ffn_bwd_call(low, gs, hid, dg, wu, wd, xhat, r1, vec)
    gc, dwo = out_bwd_call(gsf, ctx, wo)
    gl, gr = halo(gc, n)
    dq, dk, dv = attn_bwd_call(tab, q, k, v, gl, gc, gr)
    tg, dwq, dwk, dwv, sums0 = in_bwd_call(tokens, gsf, dq, dk, dv, wq, wk, wv)
    big = jnp.concatenate([w.reshape(n, -1, d) for w in (dwq, dwk, dwv, dwo)]
                          + [dwu.reshape(n, part, -1, d).transpose(0, 2, 1, 3).reshape(n, -1, d), dwd.reshape(n, -1, d)], axis=1)
    share = lax.psum_scatter(big, "dp", scatter_dimension=0, tiled=False).astype(F32)
    small = jnp.stack([sums0[0], sums0[1], sums1[2], sums2[2], sums1[0], sums1[1], sums2[0], sums2[1]])
    small = jnp.concatenate([small.reshape(8, n, part).transpose(1, 0, 2).reshape(n, -1), sumu.reshape(n, -1)], axis=1)
    tiny = lax.psum_scatter(small, "dp", scatter_dimension=0, tiled=False)
    gq, gk, gv, go = (share[i * part:(i + 1) * part] for i in range(4))
    gu = share[4 * part:8 * part].reshape(-1, part, d).transpose(1, 0, 2).reshape(part, -1)
    gd = share[8 * part:]
    t = [tiny[i * part:(i + 1) * part] for i in range(8)] + [tiny[8 * part:]]
    return (layer_out, tg, gq, gk, gv, go, gu, gd, t[0], t[1], t[2], t[8], t[3], t[4], t[5], t[6], t[7])


def solution(mesh):
    mat = P("dp", None)
    vec = P("dp")
    return jax.shard_map(
        local,
        mesh=mesh,
        in_specs=(mat, mat, P(), P()) + (mat,) * 6 + (vec,) * 9,
        out_specs=(mat,) * 8 + (vec,) * 9,
        check_vma=False,
    )
```

time: 1550 us -> 925 us (0.60)
  matrix products: 333 us -> 0 us
  waiting for transfers between devices: 767 us -> 463 us
  Pallas kernels: 0 us -> 268 us
  blocking collectives: 190 us -> 98.9 us
  local copies, waits for them, and re-layouts: 129 us -> 68.8 us
  other arithmetic: 63.8 us -> 4.24 us
  starting transfers between devices: 36.1 us -> 7.47 us
    dot_general x48 -> x0, matrix products: 333 us -> none  [the longest x2 56.7 us: forward_pass(): jnp.dot(first_low, up_weight, preferred_element_type=jnp.float32)]
    reduce_scatter x6 -> x1, waiting for transfers between devices: 504 us -> 200 us  [local(): lax.psum_scatter(big, 'dp', scatter_dimension=0, tiled=False).astype(F32)]
    pallas_call x0 -> x8, Pallas kernels: none -> 268 us  [the longest x1 63.7 us: ffn_bwd_call(): pl.pallas_call(ffn_bwd_kernel, grid=(ff // tf,), in_specs=[one(low.shape)...]
    all_gather x6, waiting for transfers between devices: 0.07 us -> 260 us  [local(): lax.all_gather(s, 'dp', axis=0, tiled=True)]
    all_to_all x8 -> x0, waiting for transfers between devices: 259 us -> none  [the longest x1 54.7 us: local(): lax.all_to_all(tokens.reshape(blocks, devices, model_width), 'dp', split_...]
    unnamed x2 -> x1, blocking collectives: 150 us -> 52.1 us
    all_to_all x8 -> x0, starting transfers between devices: 34 us -> none  [the longest x1 7.3 us: local(): lax.all_to_all(tokens.reshape(blocks, devices, model_width), 'dp', split_...]
    reduce_sum x18 -> x2, other arithmetic: 34 us -> 0.98 us  [the longest x1 0.8 us: sequence_table(): jnp.sum(jnp.where(ids[None, :] < ids[:, None], lengths[None, :], 0), axis=1)]
  transfers between devices with their start and end apart: 20 -> 11, of which waited for: 9 -> 6; matrix products, arithmetic and copies ran while one was open for 27% -> 4% of each run, Pallas kernels for 0% -> 8%
where the time goes in v1:
time: 925 us
  waiting for transfers between devices  463 us (50%)
  Pallas kernels  268 us (29%)
  blocking collectives  98.9 us (11%)
  local copies, waits for them, and re-layouts  68.8 us (7%)
  between operations  14.3 us (2%)
    all_gather x6, waiting for transfers between devices, local(): lax.all_gather(s, 'dp', axis=0, tiled=True)  260 us
    reduce_scatter x1, waiting for transfers between devices, local(): lax.psum_scatter(big, 'dp', scatter_dimension=0, tiled=False).astype(F32)  200 us
    pallas_call x1, Pallas kernels, ffn_bwd_call(): pl.pallas_call(ffn_bwd_kernel, grid=(ff // tf,), in_specs=[one(low.shape)...  63.7 us
    pallas_call x1, Pallas kernels, attn_bwd_call(): pl.pallas_call(attn_bwd_kernel, grid_spec=pltpu.PrefetchScalarGridSpec(nu...  53.6 us
    unnamed x1, blocking collectives  52.1 us
    all_gather x1, blocking collectives, local(): gathered = lax.all_gather(packed, 'dp', axis=0, tiled=False)  46.8 us
    pallas_call x1, Pallas kernels, attn_fwd_call(): pl.pallas_call(attn_fwd_kernel, grid_spec=pltpu.PrefetchScalarGridSpec(nu...  43 us
    pallas_call x1, Pallas kernels, ffn_fwd_call(): pl.pallas_call(ffn_fwd_kernel, grid=(ff // tf,), in_specs=[whole(low.shap...  42.3 us
  transfers between devices with their start and end apart: 11, of which 6 were waited for; matrix products, arithmetic and copies ran while one was open for 4% of the time, Pallas kernels for 8%

profile of v1, /device:TPU:0, one launch (start us, length us, event | category | flops | bytes accessed | tf_op | source)
XLA Modules:
  0.0 925.4 jit_solution(13503201871954126800)
XLA Ops:
  12.7 2.4 collective-permute-start
  17.9 6.1 concatenate.9
  24.0 46.8 %all-gather.1 = bf16[32,1,384]{2,1,0:T(2,128)(2,1)S(1)} all-gather(bf16[1,1,384]{2,1,0:T(2,128)(2,1)S(1)} %reshape.266), channel_id=2, replica_groups=mesh['dp'=32] {'dp'}, dimensions={0}, use_global_device_ids=true | all-gather | bytes 25344 | tf_op jit(solution)/shard_map/all_gather | solution.py:475
  73.4 58.1 %all-gather.13.cloned.1.call-done.wv = bf16[1024,1024]{1,0:T(8,128)(2,1)} async-done(((bf16[32,1024]{1,0:T(8,128)(2,1)}), bf16[1024,1024]{1,0:T(8,128)(2,1)}) %all-gather.13.cloned.1.call-update) | async-done | bytes 2097168 | tf_op jit(solution)/shard_map/all_gather | solution.py:472
  131.5 58.1 %all-gather.9.cloned.1.call-done.wq = bf16[1024,1024]{1,0:T(8,128)(2,1)} async-done(((bf16[32,1024]{1,0:T(8,128)(2,1)}), bf16[1024,1024]{1,0:T(8,128)(2,1)}) %all-gather.9.cloned.1.call-update) | async-done | bytes 2097168 | tf_op jit(solution)/shard_map/all_gather | solution.py:472
  189.6 22.4 %qkv.1 = (bf16[1792,1024]{1,0:T(8,128)(2,1)}, bf16[1792,1024]{1,0:T(8,128)(2,1)}, bf16[1792,1024]{1,0:T(8,128)(2,1)}) custom-call(bf16[384,1024]{1,0:T(8,128)(2,1)} %copy-done.6, bf16[1024,1024]{1,0:T(8,128)(2,1)} %x.3, bf16[384,1024]{1,0:T(8,128)(2,1)} %copy-done.7, bf16[1024,1024]{1,0:T(8,128)(2,1)} %all-gather.9.cloned.1.call-done.wq, ...), custom_call_target="tpu_custom_call" | custom-call | flops 11274289152 | bytes 20971520 | tf_op jit(solution)/shard_map/qkv/pallas_call | solution.py:67
  212.1 43.0 %attn_fwd.1.ctx = bf16[1024,1024]{1,0:T(8,128)(2,1)} custom-call(s32[2,8]{1,0:T(2,128)} %pad_add_fusion.tab, bf16[1792,1024]{1,0:T(8,128)(2,1)} %get-tuple-element.43.q_ref, bf16[1792,1024]{1,0:T(8,128)(2,1)} %get-tuple-element.44.k_ref, bf16[1792,1024]{1,0:T(8,128)(2,1)} %get-tuple-element.45.v_ref), custom_call_target="tpu_custom_call" | custom-call | flops 4294967296 | bytes 14680064 | tf_op jit(solution)/shard_map/attn_fwd/pallas_call | solution.py:116
  255.1 8.1 out_proj.1
  263.2 64.5 %all-gather.17.cloned.1.call-done.wu = bf16[1024,4096]{1,0:T(8,128)(2,1)} async-done(((bf16[32,4096]{1,0:T(8,128)(2,1)}), bf16[1024,4096]{1,0:T(8,128)(2,1)}) %all-gather.17.cloned.1.call-update) | async-done | bytes 8388624 | tf_op jit(solution)/shard_map/all_gather | solution.py:472
  327.7 78.8 %all-gather.19.cloned.1.call-done.wd = bf16[4096,1024]{1,0:T(8,128)(2,1)} async-done(((bf16[128,1024]{1,0:T(8,128)(2,1)}), bf16[4096,1024]{1,0:T(8,128)(2,1)}) %all-gather.19.cloned.1.call-update) | async-done | bytes 8388624 | tf_op jit(solution)/shard_map/all_gather | solution.py:472
  406.5 42.3 %ffn_fwd.1 = (bf16[1024,4096]{1,0:T(8,128)(2,1)}, bf16[1024,4096]{1,0:T(8,128)(2,1)}, bf16[1024,1024]{1,0:T(8,128)(2,1)}, f32[1024,1024]{1,0:T(8,128)}, f32[8,1024]{1,0:T(8,128)}) custom-call(bf16[1024,1024]{1,0:T(8,128)(2,1)} %get-tuple-element.46.low, bf16[1024,4096]{1,0:T(8,128)(2,1)} %all-gather.17.cloned.1.call-done.wu, f32[1,4096]{1,0:T(1,128)} %bitcast.75, ...), custom_call_target="tpu_custom_call" | custom-call | flops 17179869184 | bytes 48234496 | tf_op jit(solution)/shard_map/ffn_fwd/pallas_call | solution.py:286
  448.8 63.7 %ffn_bwd.1 = (bf16[4096,1024]{1,0:T(8,128)(2,1)}, bf16[1024,4096]{1,0:T(8,128)(2,1)}, f32[1024,1024]{1,0:T(8,128)}, f32[8,1024]{1,0:T(8,128)}, f32[1,4096]{1,0:T(1,128)}) custom-call(bf16[1024,1024]{1,0:T(8,128)(2,1)} %get-tuple-element.46.low, f32[1024,1024]{1,0:T(8,128)} %get-tuple-element.49.gs, bf16[1024,4096]{1,0:T(8,128)(2,1)} %get-tuple-element.50.hid, ...), custom_call_target="tpu_custom_call" | custom-call | flops 34359738368 | bytes 69206016 | tf_op jit(solution)/shard_map/ffn_bwd/pallas_call | solution.py:360
  512.5 11.3 %out_bwd.1 = (bf16[1024,1024]{1,0:T(8,128)(2,1)}, bf16[1024,1024]{1,0:T(8,128)(2,1)}) custom-call(f32[1024,1024]{1,0:T(8,128)} %get-tuple-element.53.gsf, bf16[1024,1024]{1,0:T(8,128)(2,1)} %attn_fwd.1.ctx, bf16[1024,1024]{1,0:T(8,128)(2,1)} %all-gather.15.cloned.1.call-done.w), custom_call_target="tpu_custom_call" | custom-call | flops 4294967296 | bytes 12582912 | tf_op jit(solution)/shard_map/out_bwd/pallas_call | solution.py:394
  525.3 2.2 collective-permute-start.2
  528.8 14.6 %reshape.254 = bf16[32,32,4,1024]{3,2,1,0:T(4,128)(2,1)} reshape(bf16[1024,4096]{1,0:T(8,128)(2,1)} %get-tuple-element.63) | data formatting | bytes 16777216 | tf_op jit(solution)/shard_map/reshape | solution.py:490
  543.4 10.3 %copy.51 = bf16[32,4,32,1024]{3,2,1,0:T(8,128)(2,1)} copy(bf16[32,4,32,1024]{3,1,2,0:T(4,128)(2,1)} %bitcast.63) | data formatting | bytes 16777216 | tf_op jit(solution)/shard_map/transpose | solution.py:490
  555.5 53.6 %attn_bwd.1 = (bf16[1024,1024]{1,0:T(8,128)(2,1)}, bf16[1024,1024]{1,0:T(8,128)(2,1)}, bf16[1024,1024]{1,0:T(8,128)(2,1)}) custom-call(s32[2,8]{1,0:T(2,128)} %pad_add_fusion.tab, bf16[1792,1024]{1,0:T(8,128)(2,1)} %get-tuple-element.43.q_ref, bf16[1792,1024]{1,0:T(8,128)(2,1)} %get-tuple-element.44.k_ref, bf16[1792,1024]{1,0:T(8,128)(2,1)} %get-tuple-element.45.v_ref, ...), custom_call_target="tpu_custom_call" | custom-call | flops 10737418240 | bytes 25690112 | tf_op jit(solution)/shard_map/attn_bwd/pallas_call | solution.py:183
  609.0 23.8 %in_bwd.1 = (bf16[1024,1024]{1,0:T(8,128)(2,1)}, bf16[1024,1024]{1,0:T(8,128)(2,1)}, bf16[1024,1024]{1,0:T(8,128)(2,1)}, bf16[1024,1024]{1,0:T(8,128)(2,1)}, f32[8,1024]{1,0:T(8,128)}) custom-call(bf16[1024,1024]{1,0:T(8,128)(2,1)} %x.3, f32[1024,1024]{1,0:T(8,128)} %get-tuple-element.53.gsf, bf16[1024,1024]{1,0:T(8,128)(2,1)} %get-tuple-element.55.dq, ...), custom_call_target="tpu_custom_call" | custom-call | flops 12884901888 | bytes 27262976 | tf_op jit(solution)/shard_map/in_bwd/pallas_call | solution.py:435
  632.8 3.3 constant_dynamic-update-slice_fusion.5
  636.1 1.5 constant_dynamic-update-slice_fusion.4
  640.6 8.3 constant_dynamic-update-slice_fusion.1
  648.9 8.2 constant_dynamic-update-slice_fusion
  661.4 52.1 %all-reduce = f32[32,384]{1,0:T(8,128)S(1)} all-reduce(f32[32,384]{1,0:T(8,128)S(1)} %pad_maximum_fusion), channel_id=4, replica_groups=mesh['dp'=32] {'dp'}, use_global_device_ids=true, to_apply=%region_4.5.clone | all-reduce | flops 12288 | bytes 98304
  714.7 200.0 %reduce-scatter.2.cloned.1.call-done = bf16[1,384,1024]{2,1,0:T(8,128)(2,1)} async-done(((bf16[32,384,1024]{2,1,0:T(8,128)(2,1)}), bf16[1,384,1024]{2,1,0:T(8,128)(2,1)}) %reduce-scatter.2.cloned.1.call-update) | async-done | bytes 786448 | tf_op jit(solution)/shard_map/reduce_scatter | solution.py:491
  (76 shorter events, 27.5 us)
Async XLA Ops:
  7.2 64.5 %copy-start.5 = (s32[256]{0:T(256)S(1)}, s32[256]{0:T(256)}, u32[]{:S(2)}) copy-start(s32[256]{0:T(256)} %param.21) | copy-start | bytes 3076
  7.2 66.2 %all-gather.11.cloned.1.call-start = ((), (), s32[]{:S(2)}) async-start(), calls=%async_computation.2 | async-start | bytes 2162688 | tf_op jit(solution)/shard_map/all_gather | solution.py:472
  7.9 123.6 %all-gather.13.cloned.1.call-start = ((), (), s32[]{:S(2)}) async-start(), calls=%async_computation.3 | async-start | bytes 2162688 | tf_op jit(solution)/shard_map/all_gather | solution.py:472
  8.7 180.9 %all-gather.9.cloned.1.call-start = ((), (), s32[]{:S(2)}) async-start(), calls=%async_computation.1 | async-start | bytes 2162688 | tf_op jit(solution)/shard_map/all_gather | solution.py:472
  9.4 245.7 %all-gather.15.cloned.1.call-start = ((), (), s32[]{:S(2)}) async-start(), calls=%async_computation.4 | async-start | bytes 2162688 | tf_op jit(solution)/shard_map/all_gather | solution.py:472
  10.0 317.7 %all-gather.17.cloned.1.call-start = ((), (), s32[]{:S(2)}) async-start(), calls=%async_computation.5 | async-start | bytes 8650752 | tf_op jit(solution)/shard_map/all_gather | solution.py:472
  10.6 395.9 %all-gather.19.cloned.1.call-start = ((), (), s32[]{:S(2)}) async-start(), calls=%async_computation.6 | async-start | bytes 8650752 | tf_op jit(solution)/shard_map/all_gather | solution.py:472
  11.2 903.5 %reduce-scatter.2.cloned.1.call-start = ((), (), s32[]{:S(2)}) async-start(), calls=%async_computation.7 | async-start | bytes 25952256 | tf_op jit(solution)/shard_map/reduce_scatter | solution.py:491
  12.7 60.4 %collective-permute-start = (bf16[384,1024]{1,0:T(8,128)(2,1)S(1)}, bf16[384,1024]{1,0:T(8,128)(2,1)S(1)}, u32[]{:S(2)}, u32[]{:S(2)}) collective-permute-start(bf16[384,1024]{1,0:T(8,128)(2,1)S(1)} %get-tuple-element.74), channel_id=1, source_target_pairs={{0,1},{1,2},{2,3},{3,4},{4,5},{5,6},{6,7},{7,8},{8,9},{9,10},{10,1... | collective-permute-start | bytes 2359304 | tf_op jit(solution)/shard_map/ppermute | solution.py:464
  15.1 58.0 %collective-permute-start.1 = (bf16[384,1024]{1,0:T(8,128)(2,1)S(1)}, bf16[384,1024]{1,0:T(8,128)(2,1)S(1)}, u32[]{:S(2)}, u32[]{:S(2)}) collective-permute-start(bf16[384,1024]{1,0:T(8,128)(2,1)S(1)} %get-tuple-element.73), channel_id=1, source_target_pairs={{1,0},{2,1},{3,2},{4,3},{5,4},{6,5},{7,6},{8,7},{9,8},{10,9},{11,1... | collective-permute-start | bytes 2359304 | tf_op jit(solution)/shard_map/ppermute | solution.py:464
  73.1 116.5 %copy-start.6 = (bf16[384,1024]{1,0:T(8,128)(2,1)}, bf16[384,1024]{1,0:T(8,128)(2,1)S(1)}, u32[]{:S(2)}) copy-start(bf16[384,1024]{1,0:T(8,128)(2,1)S(1)} %collective-permute-done.xl) | copy-start | bytes 2359300
  73.1 116.5 %copy-start.7 = (bf16[384,1024]{1,0:T(8,128)(2,1)}, bf16[384,1024]{1,0:T(8,128)(2,1)S(1)}, u32[]{:S(2)}) copy-start(bf16[384,1024]{1,0:T(8,128)(2,1)S(1)} %collective-permute-done.1.xr) | copy-start | bytes 2359300
  525.3 28.4 %collective-permute-start.2 = (bf16[384,1024]{1,0:T(8,128)(2,1)S(1)}, bf16[384,1024]{1,0:T(8,128)(2,1)S(1)}, u32[]{:S(2)}, u32[]{:S(2)}) collective-permute-start(bf16[384,1024]{1,0:T(8,128)(2,1)S(1)} %get-tuple-element.72), channel_id=1, source_target_pairs={{0,1},{1,2},{2,3},{3,4},{4,5},{5,6},{6,7},{7,8},{8,9},{9,10},{10,1... | collective-permute-start | bytes 2359304 | tf_op jit(solution)/shard_map/ppermute | solution.py:464
  527.5 26.2 %collective-permute-start.3 = (bf16[384,1024]{1,0:T(8,128)(2,1)S(1)}, bf16[384,1024]{1,0:T(8,128)(2,1)S(1)}, u32[]{:S(2)}, u32[]{:S(2)}) collective-permute-start(bf16[384,1024]{1,0:T(8,128)(2,1)S(1)} %get-tuple-element.71), channel_id=1, source_target_pairs={{1,0},{2,1},{3,2},{4,3},{5,4},{6,5},{7,6},{8,7},{9,8},{10,9},{11,1... | collective-permute-start | bytes 2359304 | tf_op jit(solution)/shard_map/ppermute | solution.py:464
  553.7 0.9 copy-start.8
  554.6 0.9 copy-start.9
  632.8 3.3 copy-start.3
  632.8 4.8 copy-start.2
  636.1 3.0 copy-start.1
  657.2 4.2 copy-start.4
  914.6 3.0 copy-start
Sparse Core Ops, SparseCore 0:
  10.9 62.4 all-gather.10
  76.2 55.2 all-gather.12
  134.4 55.2 all-gather.8
  192.3 56.2 all-gather.14
  251.3 76.3 all-gather.16
  330.4 76.0 all-gather.18
  657.3 257.2 reduce-scatter.1

commit v2 on v1

--- a/solution.py
+++ b/solution.py
@@ -14,6 +14,7 @@
 F32 = jnp.float32
 BF16 = jnp.bfloat16
 NT = (((1,), (1,)), ((), ()))
+MESH = pl.DeviceIdType.MESH
 ANY = pl.BlockSpec(memory_space=pl.ANY)
 
 
@@ -446,6 +447,325 @@
     )(x, gsf, dq, dk, dv, wq, wk, wv)
 
 
+def grid_of(n):
+    chips = n // 2
+    return {16: (4, 2, 2), 64: (4, 4, 4)}.get(chips, (chips, 1, 1))
+
+
+class Place:
+    def __init__(self, n):
+        self.n = n
+        self.size = grid_of(n)
+        me = lax.axis_index("dp")
+        nz, ny, nx = self.size
+        self.me = me
+        self.c = lax.rem(me, 2)
+        self.x = lax.rem(me // 2, nx)
+        self.y = lax.rem(me // (2 * nx), ny)
+        self.z = me // (2 * nx * ny)
+
+    def at(self, axis, k):
+        nz, ny, nx = self.size
+        z, y, x, c = self.z, self.y, self.x, self.c
+        if axis == "z":
+            z = lax.rem(z + k, nz)
+        elif axis == "y":
+            y = lax.rem(y + k, ny)
+        elif axis == "x":
+            x = lax.rem(x + k, nx)
+        else:
+            c = lax.rem(c + k, 2)
+        pos = {"z": z, "y": y, "x": x, "c": c}[axis]
+        return ((z * ny + y) * nx + x) * 2 + c, pos
+
+    def steps(self, axis):
+        nz, ny, nx = self.size
+        return range(1, {"z": nz, "y": ny, "x": nx, "c": 2}[axis])
+
+    def peers(self):
+        return [self.at(a, k)[0] for a in "zyxc" for k in self.steps(a)]
+
+
+def enter(peers):
+    sem = pltpu.get_barrier_semaphore()
+    for p in peers:
+        pl.semaphore_signal(sem, inc=1, device_id=(p,), device_id_type=MESH)
+    pl.semaphore_wait(sem, len(peers))
+
+
+def gather_slots(n):
+    nz, ny, nx = grid_of(n)
+    return (nz - 1) + 2 * (ny - 1) + 2 * (nx - 1) + 1
+
+
+class Gather:
+    def __init__(self, place, src, dst, rows, cols, ssem, rsem, lsem, index):
+        self.p, self.index = place, index
+        self.src, self.dst, self.rows, self.cols = src, dst, rows, cols
+        self.ssem, self.rsem, self.lsem = ssem, rsem, lsem
+        p = place
+        r0, nr = rows
+        c0, nc = cols
+        rs = pl.ds(r0, nr)
+        full = pl.ds(c0, nc)
+        halves = (pl.ds(c0, nc // 2), pl.ds(c0 + nc // 2, nc // 2))
+        al = pl.ds(0, p.size[0])
+        self.local = pltpu.make_async_copy(src.at[rs, full], dst.at[p.z, p.y, p.x, p.c, rs, full], lsem.at[index])
+        slot = 0
+
+        def copy(s, d, dev):
+            nonlocal slot
+            cp = pltpu.make_async_remote_copy(src_ref=s, dst_ref=d, send_sem=ssem.at[index, slot], recv_sem=rsem.at[index, slot],
+                                              device_id=(dev,), device_id_type=MESH)
+            slot += 1
+            return cp
+
+        mine = dst.at[p.z, p.y, p.x, p.c, rs, full]
+        self.ph = [[], [], [], []]
+        for k in p.steps("z"):
+            self.ph[0].append(copy(src.at[rs, full], mine, p.at("z", k)[0]))
+        for h, axis in ((0, "y"), (1, "x")):
+            s = dst.at[:, p.y, p.x, p.c, rs, halves[h]]
+            for k in p.steps(axis):
+                self.ph[1].append(copy(s, s, p.at(axis, k)[0]))
+        for h, axis in ((0, "x"), (1, "y")):
+            s = dst.at[:, :, p.x, p.c, rs, halves[0]] if h == 0 else dst.at[:, p.y, :, p.c, rs, halves[1]]
+            for k in p.steps(axis):
+                self.ph[2].append(copy(s, s, p.at(axis, k)[0]))
+        s = dst.at[:, :, :, p.c, rs, full]
+        self.ph[3].append(copy(s, s, p.at("c", 1)[0]))
+
+    def start(self, i):
+        if i == 0:
+            self.local.start()
+        for cp in self.ph[i]:
+            cp.start()
+
+    def wait(self, i):
+        if i == 0:
+            self.local.wait()
+        for cp in self.ph[i]:
+            cp.wait_recv()
+
+    def sent(self):
+        for ph in self.ph:
+            for cp in ph:
+                cp.wait_send()
+
+
+def gather_kernel(n, plan, nsrc, *refs):
+    srcs, xsrc, outs = refs[:nsrc], refs[nsrc], refs[nsrc + 1:2 * nsrc + 1]
+    xl, xr = refs[2 * nsrc + 1:2 * nsrc + 3]
+    ssem, rsem, lsem, hs, hr = refs[2 * nsrc+3:]
+    p = Place(n)
+    right, left = lax.rem(p.me + 1, n), lax.rem(p.me + n - 1, n)
+    enter(p.peers() + [left, right])
+    rows = xsrc.shape[0]
+    halo = [pltpu.make_async_remote_copy(src_ref=xsrc.at[pl.ds(rows-HALO,HALO),:], dst_ref=xl, send_sem=hs.at[0], recv_sem=hr.at[0], device_id=(right,), device_id_type=MESH),
+            pltpu.make_async_remote_copy(src_ref=xsrc.at[pl.ds(0,HALO),:], dst_ref=xr, send_sem=hs.at[1], recv_sem=hr.at[1], device_id=(left,), device_id_type=MESH)]
+    for h in halo: h.start()
+    g = [Gather(p, srcs[a], outs[a], r, c, ssem, rsem, lsem, i) for i, (a, r, c) in enumerate(plan)]
+    for s in range(len(g) + 4):
+        for ph in (0, 1, 2, 3, 4):
+            i = s - ph
+            if 0 <= i < len(g):
+                if ph > 0:
+                    g[i].wait(ph - 1)
+                if ph < 4:
+                    g[i].start(ph)
+    for c in g:
+        c.sent()
+    for h in halo: h.wait()
+
+
+def gather_plan(shards, d):
+    least = min(s.shape[0] for s in shards if s.shape[-1] >= d)
+    plan = []
+    for a, s in enumerate(shards):
+        if s.shape[1] < d:
+            plan.append((a, (0, s.shape[0]), (0, s.shape[1])))
+            continue
+        for j in range(s.shape[1] // d):
+            for i in range(s.shape[0] // least):
+                plan.append((a, (i * least, least), (j * d, d)))
+    return plan
+
+
+def gather_call(n, shards, tokens, order=None):
+    d = tokens.shape[1]
+    plan = gather_plan(shards, d)
+    k = gather_slots(n)
+    outs = [jax.ShapeDtypeStruct(grid_of(n) + (2,) + s.shape, s.dtype) for s in shards]
+    halo = jax.ShapeDtypeStruct((HALO, d), tokens.dtype)
+    res = pl.pallas_call(
+        functools.partial(gather_kernel, n, plan, len(shards)),
+        in_specs=[ANY] * (len(shards)+1),
+        out_specs=[ANY] * (len(shards)+2),
+        out_shape=outs+[halo,halo],
+        scratch_shapes=[pltpu.SemaphoreType.DMA((len(plan), k)), pltpu.SemaphoreType.DMA((len(plan), k)),
+                        pltpu.SemaphoreType.DMA((len(plan),)),pltpu.SemaphoreType.DMA((2,)),pltpu.SemaphoreType.DMA((2,))],
+        compiler_params=pltpu.CompilerParams(collective_id=1, has_side_effects=True),
+        name="gather",
+    )(*shards, tokens)
+    return [r.reshape((n * s.shape[0],) + s.shape[1:]) for r, s in zip(res, shards)] + list(res[-2:])
+
+
+def reduce_slots(n):
+    nz, ny, nx = grid_of(n)
+    return (nz - 1) + 2 * (ny - 1) + 2 * (nx - 1) + 1
+
+
+def landing(n, r, cols, dtype):
+    nz, ny, nx = grid_of(n)
+    h = cols // 2
+    return [pltpu.VMEM((nz, ny, nx, r, cols), dtype),
+            pltpu.VMEM((max(nx - 1, 1), nz, ny, r, h), dtype), pltpu.VMEM((max(ny - 1, 1), nz, nx, r, h), dtype),
+            pltpu.VMEM((max(ny - 1, 1), nz, r, h), dtype), pltpu.VMEM((max(nx - 1, 1), nz, r, h), dtype),
+            pltpu.VMEM((max(nz - 1, 1), r, cols), dtype)]
+
+
+def partial(n, r, cols, dtype):
+    nz, ny, nx = grid_of(n)
+    h = cols // 2
+    return [pltpu.VMEM((nz, ny, nx, r, cols), dtype), pltpu.VMEM((nz, ny, r, h), dtype), pltpu.VMEM((nz, nx, r, h), dtype),
+            pltpu.VMEM((nz, r, cols), dtype), pltpu.VMEM((r, cols), F32)]
+
+
+class Reduce:
+    def __init__(self, place, src, land, part, out, ssem, rsem, lsem, index):
+        self.p, self.src, self.land, self.part, self.out = place, src, land, part, out
+        p = place
+        self.h = part[3].shape[-1] // 2
+        self.ca, self.cb = pl.ds(0, self.h), pl.ds(self.h, self.h)
+        self.get = pltpu.make_async_copy(src.at[:, :, :, p.c], part[0], lsem.at[index, 0])
+        self.put = pltpu.make_async_copy(part[4], out, lsem.at[index, 1])
+        slot = 0
+
+        def copy(s, d, dev):
+            nonlocal slot
+            cp = pltpu.make_async_remote_copy(src_ref=s, dst_ref=d, send_sem=ssem.at[index, slot], recv_sem=rsem.at[index, slot],
+                                              device_id=(dev,), device_id_type=MESH)
+            slot += 1
+            return cp
+
+        self.ph = [[], [], [], []]
+        dev, oc = p.at("c", 1)
+        self.ph[0].append(copy(src.at[:, :, :, oc], land[0], dev))
+        for k in p.steps("x"):
+            dev, o = p.at("x", k)
+            self.ph[1].append(copy(part[0].at[:, :, o, :, self.ca], land[1].at[k - 1], dev))
+        for k in p.steps("y"):
+            dev, o = p.at("y", k)
+            self.ph[1].append(copy(part[0].at[:, o, :, :, self.cb], land[2].at[k - 1], dev))
+        for k in p.steps("y"):
+            dev, o = p.at("y", k)
+            self.ph[2].append(copy(part[1].at[:, o], land[3].at[k - 1], dev))
+        for k in p.steps("x"):
+            dev, o = p.at("x", k)
+            self.ph[2].append(copy(part[2].at[:, o], land[4].at[k - 1], dev))
+        for k in p.steps("z"):
+            dev, o = p.at("z", k)
+            self.ph[3].append(copy(part[3].at[o], land[5].at[k - 1], dev))
+
+    def begin(self):
+        self.get.start()
+        self.ph[0][0].start()
+
+    def go(self, i):
+        p, land, part = self.p, self.land, self.part
+        nz, ny, nx = p.size
+        dt = part[0].dtype
+        for cp in self.ph[i - 1]:
+            cp.wait_recv()
+        if i == 1:
+            self.get.wait()
+
+            def add(z, c):
+                part[0][z] = (part[0][z].astype(F32) + land[0][z].astype(F32)).astype(dt)
+                return c
+
+            lax.fori_loop(0, nz, add, 0)
+        elif i == 2:
+            def add(z, c):
+                a = part[0][z, :, pl.ds(p.x, 1), :, self.ca].astype(F32)[:, 0]
+                for k in range(nx - 1):
+                    a += land[1][k, z].astype(F32)
+                part[1][z] = a.astype(dt)
+                b = part[0][z, pl.ds(p.y, 1), :, :, self.cb].astype(F32)[0]
+                for k in range(ny - 1):
+                    b += land[2][k, z].astype(F32)
+                part[2][z] = b.astype(dt)
+                return c
+
+            lax.fori_loop(0, nz, add, 0)
+        elif i == 3:
+            a = part[1][:, pl.ds(p.y, 1)].astype(F32)[:, 0]
+            for k in range(ny - 1):
+                a += land[3][k].astype(F32)
+            part[3][:, :, self.ca] = a.astype(dt)
+            b = part[2][:, pl.ds(p.x, 1)].astype(F32)[:, 0]
+            for k in range(nx - 1):
+                b += land[4][k].astype(F32)
+            part[3][:, :, self.cb] = b.astype(dt)
+        else:
+            a = part[3][pl.ds(p.z, 1)].astype(F32)[0]
+            for k in range(nz - 1):
+                a += land[5][k].astype(F32)
+            part[4][...] = a
+            self.put.start()
+            return
+        for cp in self.ph[i]:
+            cp.start()
+
+    def finish(self):
+        self.put.wait()
+        for ph in self.ph:
+            for cp in ph:
+                cp.wait_send()
+
+
+def reduce_kernel(n, plan, nsrc, *refs):
+    srcs, outs = refs[:nsrc], refs[nsrc:2 * nsrc]
+    scratch = refs[2 * nsrc:]
+    ssem, rsem, lsem = scratch[-3:]
+    p = Place(n)
+    enter(p.peers())
+    red = []
+    for i, (a, (r0, nr), (c0, nc)) in enumerate(plan):
+        land, part = scratch[11 * i:11 * i + 6], scratch[11 * i + 6:11 * i + 11]
+        rs, cs = pl.ds(r0, nr), pl.ds(c0, nc)
+        red.append(Reduce(p, srcs[a].at[:, :, :, :, rs, cs], land, part, outs[a].at[rs, cs], ssem, rsem, lsem, i))
+    for s in range(len(red) + 5):
+        for ph in (0, 1, 2, 3, 4, 5):
+            i = s - ph
+            if 0 <= i < len(red):
+                if ph == 0:
+                    red[i].begin()
+                elif ph < 5:
+                    red[i].go(ph)
+                else:
+                    red[i].finish()
+
+
+def reduce_call(n, grads, d):
+    views = [g.reshape(grid_of(n) + (2, g.shape[0] // n) + g.shape[1:]) for g in grads]
+    plan = gather_plan([jax.ShapeDtypeStruct(v.shape[4:], v.dtype) for v in views], d)
+    k = reduce_slots(n)
+    scratch = []
+    for a, r, c in plan:
+        scratch += landing(n, r[1], c[1], grads[a].dtype) + partial(n, r[1], c[1], grads[a].dtype)
+    return pl.pallas_call(
+        functools.partial(reduce_kernel, n, plan, len(grads)),
+        in_specs=[ANY] * len(grads),
+        out_specs=[ANY] * len(grads),
+        out_shape=[jax.ShapeDtypeStruct(v.shape[4:], F32) for v in views],
+        scratch_shapes=scratch + [pltpu.SemaphoreType.DMA((len(plan), k)), pltpu.SemaphoreType.DMA((len(plan), k)),
+                                  pltpu.SemaphoreType.DMA((len(plan), 2))],
+        compiler_params=pltpu.CompilerParams(collective_id=2, has_side_effects=True, vmem_limit_bytes=60 << 20),
+        name="reduce",
+    )(*views)
+
+
 def sequence_table(lengths, own, rows):
     ids = jnp.arange(lengths.shape[0], dtype=jnp.int32)
     starts = jnp.sum(jnp.where(ids[None, :] < ids[:, None], lengths[None, :], 0), axis=1)
@@ -464,19 +784,28 @@
     return lax.ppermute(x[-HALO:], "dp", right), lax.ppermute(x[:HALO], "dp", left)
 
 
+def pack(values, n, rows, dtype):
+    cols = [v.reshape(n, -1) for v in values]
+    flat = jnp.concatenate(cols, axis=1)
+    return jnp.pad(flat, ((0, 0), (0, rows * 256 - flat.shape[1]))).astype(dtype).reshape(n * rows, 256)
+
+
+def unpack(packed, n, part):
+    flat = packed.reshape(n, -1)
+    vec = flat[:, : 8 * part].reshape(n, 8, part).transpose(1, 0, 2).reshape(8, n * part)
+    return vec, flat[:, 8 * part:12 * part].reshape(1, -1)
+
+
 def local(tokens, cotangent, lengths, dealing, *shards):
     n = lax.axis_size("dp")
     own = lax.axis_index("dp")
     rows, d = tokens.shape
     part = d // n
-    wq, wk, wv, wo, wu, wd = (lax.all_gather(s, "dp", axis=0, tiled=True) for s in shards[:6])
     qb, vb, ob, ub, db, fg, fs, sg, ss = shards[6:]
-    packed = jnp.concatenate([qb, vb, ob, db, fg, fs, sg, ss, ub])
-    gathered = lax.all_gather(packed, "dp", axis=0, tiled=False)
-    vec = gathered[:, : 8 * part].reshape(n, 8, part).transpose(1, 0, 2).reshape(8, d).astype(F32)
-    bu = gathered[:, 8 * part:].reshape(1, -1).astype(F32)
+    packed = pack([qb, vb, ob, db, fg, fs, sg, ss, ub], 1, 16, BF16)
+    packed, wq, wk, wv, wo, wu, wd, xl, xr = gather_call(n, [packed] + list(shards[:6]), tokens)
+    vec, bu = unpack(packed.astype(F32), n, part)
     tab = sequence_table(lengths, own, rows)
-    xl, xr = halo(tokens, n)
     q, k, v = qkv_call(xl, tokens, xr, wq, wk, wv, vec)
     ctx = attn_fwd_call(tab, q, k, v, rows)
     xhat, low, r1 = out_proj_call(ctx, wo, tokens, vec)
@@ -486,17 +815,11 @@
     gl, gr = halo(gc, n)
     dq, dk, dv = attn_bwd_call(tab, q, k, v, gl, gc, gr)
     tg, dwq, dwk, dwv, sums0 = in_bwd_call(tokens, gsf, dq, dk, dv, wq, wk, wv)
-    big = jnp.concatenate([w.reshape(n, -1, d) for w in (dwq, dwk, dwv, dwo)]
-                          + [dwu.reshape(n, part, -1, d).transpose(0, 2, 1, 3).reshape(n, -1, d), dwd.reshape(n, -1, d)], axis=1)
-    share = lax.psum_scatter(big, "dp", scatter_dimension=0, tiled=False).astype(F32)
-    small = jnp.stack([sums0[0], sums0[1], sums1[2], sums2[2], sums1[0], sums1[1], sums2[0], sums2[1]])
-    small = jnp.concatenate([small.reshape(8, n, part).transpose(1, 0, 2).reshape(n, -1), sumu.reshape(n, -1)], axis=1)
-    tiny = lax.psum_scatter(small, "dp", scatter_dimension=0, tiled=False)
-    gq, gk, gv, go = (share[i * part:(i + 1) * part] for i in range(4))
-    gu = share[4 * part:8 * part].reshape(-1, part, d).transpose(1, 0, 2).reshape(part, -1)
-    gd = share[8 * part:]
-    t = [tiny[i * part:(i + 1) * part] for i in range(8)] + [tiny[8 * part:]]
-    return (layer_out, tg, gq, gk, gv, go, gu, gd, t[0], t[1], t[2], t[8], t[3], t[4], t[5], t[6], t[7])
+    small = pack([sums0[0], sums0[1], sums1[2], sums2[2], sums1[0], sums1[1], sums2[0], sums2[1], sumu], n, 8, F32)
+    tiny, gd, gu, go, gq, gk, gv = reduce_call(n, [small, dwd, dwu, dwo, dwq, dwk, dwv], d)
+    vecs, ubg = unpack(tiny, 1, part)
+    t = [vecs[i] for i in range(8)]
+    return (layer_out, tg, gq, gk, gv, go, gu, gd, t[0], t[1], t[2], ubg[0], t[3], t[4], t[5], t[6], t[7])
 
 
 def solution(mesh):

time: 925 us -> 567 us (0.61); the launches traced: 925 us -> 558 us
  waiting for transfers between devices: 463 us -> 0.47 us
  Pallas kernels: 268 us -> 531 us
  blocking collectives: 98.9 us -> 0 us
  local copies, waits for them, and re-layouts: 68.8 us -> 20.9 us
  between operations: 14.3 us -> 0.8 us
    pallas_call x0 -> x2, Pallas kernels: none -> 273 us  [the longest x1 142 us: reduce_call(): pl.pallas_call(functools.partial(reduce_kernel, n, plan, len(grads)), in_...]
    all_gather x6 -> x0, waiting for transfers between devices: 260 us -> none  [local(): lax.all_gather(s, 'dp', axis=0, tiled=True)]
    reduce_scatter x1 -> x0, waiting for transfers between devices: 200 us -> none  [local(): lax.psum_scatter(big, 'dp', scatter_dimension=0, tiled=False).astype(F32)]
    unnamed x1 -> x0, blocking collectives: 52.1 us -> none
    all_gather x1 -> x0, blocking collectives: 46.8 us -> none  [local(): gathered = lax.all_gather(packed, 'dp', axis=0, tiled=False)]
    reshape x4 -> x3, local copies, waits for them, and re-layouts: 15.6 us -> 1.42 us  [the longest x2 0.81 us: unpack(): flat[:, :8 * part].reshape(n, 8, part).transpose(1, 0, 2)]
    concatenate x2, local copies, waits for them, and re-layouts: 14.3 us -> 0.97 us  [pack(): flat = jnp.concatenate(cols, axis=1)]
    transpose x2 -> x1, local copies, waits for them, and re-layouts: 10.4 us -> 0.03 us  [unpack(): flat[:, :8 * part].reshape(n, 8, part).transpose(1, 0, 2)]
  transfers between devices with their start and end apart: 11 -> 2, of which waited for: 6 -> 1; matrix products, arithmetic and copies ran while one was open for 4% -> 0% of each run, Pallas kernels for 8% -> 0%
where the time goes in v2:
time: 567 us; the launch traced here: 558 us
  Pallas kernels  531 us (94%)
  local copies, waits for them, and re-layouts  20.9 us (4%)
    pallas_call x1, Pallas kernels, reduce_call(): pl.pallas_call(functools.partial(reduce_kernel, n, plan, len(grads)), in_...  142 us
    pallas_call x1, Pallas kernels, gather_call(): pl.pallas_call(functools.partial(gather_kernel, n, plan, len(shards)), in...  131 us
    pallas_call x1, Pallas kernels, ffn_bwd_call(): pl.pallas_call(ffn_bwd_kernel, grid=(ff // tf,), in_specs=[one(low.shape)...  63.6 us
    pallas_call x1, Pallas kernels, attn_bwd_call(): pl.pallas_call(attn_bwd_kernel, grid_spec=pltpu.PrefetchScalarGridSpec(nu...  46 us
    pallas_call x1, Pallas kernels, ffn_fwd_call(): pl.pallas_call(ffn_fwd_kernel, grid=(ff // tf,), in_specs=[whole(low.shap...  42.3 us
    pallas_call x1, Pallas kernels, attn_fwd_call(): pl.pallas_call(attn_fwd_kernel, grid_spec=pltpu.PrefetchScalarGridSpec(nu...  40.9 us
    pallas_call x1, Pallas kernels, in_bwd_call(): pl.pallas_call(in_bwd_kernel, grid=(1,), in_specs=[one((rows, d))] * 5 +...  23.6 us
    pallas_call x1, Pallas kernels, qkv_call(): pl.pallas_call(qkv_kernel, grid=(d // tn,), in_specs=[whole(xl.shape), wh...  22.4 us
  transfers between devices with their start and end apart: 2, of which 1 were waited for; matrix products, arithmetic and copies ran while one was open for 0% of the time, Pallas kernels for 0%

profile of v2, /device:TPU:0, one launch (start us, length us, event | category | flops | bytes accessed | tf_op | source)
XLA Modules:
  0.0 558.1 jit_solution(17926799220356418191)
XLA Ops:
  0.7 0.9 concatenate.6
  2.2 131.0 %gather.1 = (bf16[4,2,2,2,16,256]{5,4,3,2,1,0:T(8,128)(2,1)}, bf16[4,2,2,2,32,1024]{5,4,3,2,1,0:T(8,128)(2,1)}, bf16[4,2,2,2,32,1024]{5,4,3,2,1,0:T(8,128)(2,1)}...) custom-call(bf16[16,256]{1,0:T(8,128)(2,1)} %reshape.287.refs_0_, ...), custom_call_target="tpu_custom_call" | custom-call | tf_op jit(solution)/shard_map/gather/pallas_call | solution.py:600
  133.2 1.0 copy.37
  136.6 22.4 %qkv.1 = (bf16[1792,1024]{1,0:T(8,128)(2,1)}, bf16[1792,1024]{1,0:T(8,128)(2,1)}, bf16[1792,1024]{1,0:T(8,128)(2,1)}) custom-call(bf16[384,1024]{1,0:T(8,128)(2,1)} %get-tuple-element.59.xl, bf16[1024,1024]{1,0:T(8,128)(2,1)} %x.7, bf16[384,1024]{1,0:T(8,128)(2,1)} %get-tuple-element.60.xr, bf16[1024,1024]{1,0:T(8,128)(2,1)} %bitcast.97, ...), custom_call_target="tpu_custom_call" | custom-call | flops 11274289152 | bytes 20971520 | tf_op jit(solution)/shard_map/qkv/pallas_call | solution.py:68
  159.0 40.9 %attn_fwd.1.ctx = bf16[1024,1024]{1,0:T(8,128)(2,1)} custom-call(s32[2,8]{1,0:T(2,128)} %pad_add_fusion.tab, bf16[1792,1024]{1,0:T(8,128)(2,1)} %get-tuple-element.65.q_ref, bf16[1792,1024]{1,0:T(8,128)(2,1)} %get-tuple-element.66.k_ref, bf16[1792,1024]{1,0:T(8,128)(2,1)} %get-tuple-element.67.v_ref), custom_call_target="tpu_custom_call" | custom-call | flops 4294967296 | bytes 14680064 | tf_op jit(solution)/shard_map/attn_fwd/pallas_call | solution.py:117
  199.9 8.1 %out_proj.1 = (f32[1024,1024]{1,0:T(8,128)}, bf16[1024,1024]{1,0:T(8,128)(2,1)}, f32[1024,128]{1,0:T(8,128)}) custom-call(bf16[1024,1024]{1,0:T(8,128)(2,1)} %attn_fwd.1.ctx, bf16[1024,1024]{1,0:T(8,128)(2,1)} %bitcast.103, bf16[1024,1024]{1,0:T(8,128)(2,1)} %x.7, f32[8,1024]{1,0:T(8,128)} %reshape.292.vec), custom_call_target="tpu_custom_call" | custom-call | flops 2147483648 | bytes 12582912 | tf_op jit(solution)/shard_map/out_proj/pallas_call | solution.py:222
  208.0 42.3 %ffn_fwd.1 = (bf16[1024,4096]{1,0:T(8,128)(2,1)}, bf16[1024,4096]{1,0:T(8,128)(2,1)}, bf16[1024,1024]{1,0:T(8,128)(2,1)}, f32[1024,1024]{1,0:T(8,128)}, f32[8,1024]{1,0:T(8,128)}) custom-call(bf16[1024,1024]{1,0:T(8,128)(2,1)} %get-tuple-element.69.low, bf16[1024,4096]{1,0:T(8,128)(2,1)} %bitcast.93, f32[1,4096]{1,0:T(1,128)} %bitcast.82, ...), custom_call_target="tpu_custom_call" | custom-call | flops 17179869184 | bytes 48234496 | tf_op jit(solution)/shard_map/ffn_fwd/pallas_call | solution.py:287
  250.4 63.6 %ffn_bwd.1 = (bf16[4096,1024]{1,0:T(8,128)(2,1)}, bf16[1024,4096]{1,0:T(8,128)(2,1)}, f32[1024,1024]{1,0:T(8,128)}, f32[8,1024]{1,0:T(8,128)}, f32[1,4096]{1,0:T(1,128)}) custom-call(bf16[1024,1024]{1,0:T(8,128)(2,1)} %get-tuple-element.69.low, f32[1024,1024]{1,0:T(8,128)} %get-tuple-element.74.gs, bf16[1024,4096]{1,0:T(8,128)(2,1)} %get-tuple-element.75.hid, ...), custom_call_target="tpu_custom_call" | custom-call | flops 34359738368 | bytes 69206016 | tf_op jit(solution)/shard_map/ffn_bwd/pallas_call | solution.py:361
  314.0 11.2 %out_bwd.1 = (bf16[1024,1024]{1,0:T(8,128)(2,1)}, bf16[1024,1024]{1,0:T(8,128)(2,1)}) custom-call(f32[1024,1024]{1,0:T(8,128)} %get-tuple-element.78.gsf, bf16[1024,1024]{1,0:T(8,128)(2,1)} %attn_fwd.1.ctx, bf16[1024,1024]{1,0:T(8,128)(2,1)} %bitcast.104), custom_call_target="tpu_custom_call" | custom-call | flops 4294967296 | bytes 12582912 | tf_op jit(solution)/shard_map/out_bwd/pallas_call | solution.py:395
  325.2 1.5 fusion.1
  326.7 1.3 collective-permute-start.1
  328.0 3.1 collective-permute-start
  331.1 0.9 slice_reduce_fusion
  333.4 0.9 copy-done.4
  334.2 46.0 %attn_bwd.1 = (bf16[1024,1024]{1,0:T(8,128)(2,1)}, bf16[1024,1024]{1,0:T(8,128)(2,1)}, bf16[1024,1024]{1,0:T(8,128)(2,1)}) custom-call(s32[2,8]{1,0:T(2,128)} %pad_add_fusion.tab, bf16[1792,1024]{1,0:T(8,128)(2,1)} %get-tuple-element.65.q_ref, bf16[1792,1024]{1,0:T(8,128)(2,1)} %get-tuple-element.66.k_ref, bf16[1792,1024]{1,0:T(8,128)(2,1)} %get-tuple-element.67.v_ref, ...), custom_call_target="tpu_custom_call" | custom-call | flops 10737418240 | bytes 25690112 | tf_op jit(solution)/shard_map/attn_bwd/pallas_call | solution.py:184
  380.2 23.6 %in_bwd.1 = (bf16[1024,1024]{1,0:T(8,128)(2,1)}, bf16[1024,1024]{1,0:T(8,128)(2,1)}, bf16[1024,1024]{1,0:T(8,128)(2,1)}, bf16[1024,1024]{1,0:T(8,128)(2,1)}, f32[8,1024]{1,0:T(8,128)}) custom-call(bf16[1024,1024]{1,0:T(8,128)(2,1)} %x.7, f32[1024,1024]{1,0:T(8,128)} %get-tuple-element.78.gsf, bf16[1024,1024]{1,0:T(8,128)(2,1)} %get-tuple-element.80.dq, ...), custom_call_target="tpu_custom_call" | custom-call | flops 12884901888 | bytes 27262976 | tf_op jit(solution)/shard_map/in_bwd/pallas_call | solution.py:436
  403.8 0.9 slice_reduce_fusion.6
  405.7 141.6 %reduce.35 = (f32[8,256]{1,0:T(8,128)}, f32[128,1024]{1,0:T(8,128)}, f32[32,4096]{1,0:T(8,128)}, f32[32,1024]{1,0:T(8,128)}, f32[32,1024]{1,0:T(8,128)}, /*index=5*/f32[32,1024]{1,0:T(8,128)}, f32[32,1024]{1,0:T(8,128)}) custom-call(f32[4,2,2,2,8,256]{5,4,3,2,1,0:T(8,128)} %bitcast.73, bf16[4,2,2,2,128,1024]{5,4,3,2,1,0:T(8,128)(2,1)} %bitcast.67, ...), custom_call_target="tpu_custom_call" | custom-call | tf_op jit(solution)/shard_map/reduce/pallas_call | solution.py:757
  549.2 1.6 copy.46
  550.7 1.6 copy.47
  552.3 1.6 copy.48
  553.9 1.6 copy.49
  555.4 1.9 copy.50
  557.3 0.8 copy.51
  (38 shorter events, 7.2 us)
Async XLA Ops:
  0.7 134.2 %copy-start.2 = (s32[256]{0:T(256)S(1)}, s32[256]{0:T(256)}, u32[]{:S(2)}) copy-start(s32[256]{0:T(256)} %param.21) | copy-start | bytes 3076
  326.7 5.8 %collective-permute-start.1 = (bf16[384,1024]{1,0:T(8,128)(2,1)S(1)}, bf16[384,1024]{1,0:T(8,128)(2,1)S(1)}, u32[]{:S(2)}, u32[]{:S(2)}) collective-permute-start(bf16[384,1024]{1,0:T(8,128)(2,1)S(1)} %get-tuple-element.111), channel_id=1, source_target_pairs={{1,0},{2,1},{3,2},{4,3},{5,4},{6,5},{7,6},{8,7},{9,8},{10,9},{11,1... | collective-permute-start | bytes 2359304 | tf_op jit(solution)/shard_map/ppermute | solution.py:784
  328.0 4.9 collective-permute-start
  332.5 0.9 copy-start.3
  333.4 0.9 copy-start.4
  380.2 24.6 %copy-start.1 = (f32[1,4096]{1,0:T(1,128)S(1)}, f32[1,4096]{1,0:T(1,128)}, u32[]{:S(2)}) copy-start(f32[1,4096]{1,0:T(1,128)} %get-tuple-element.87) | copy-start | bytes 49156
  547.3 10.0 %copy-start = (f32[128,1024]{1,0:T(8,128)S(1)}, f32[128,1024]{1,0:T(8,128)}, u32[]{:S(2)}) copy-start(f32[128,1024]{1,0:T(8,128)} %get-tuple-element.150) | copy-start | bytes 1572868

commit v3 on v2

--- a/solution.py
+++ b/solution.py
@@ -38,30 +38,24 @@
     return pl.CostEstimate(flops=flops, bytes_accessed=nbytes, transcendentals=trans)
 
 
-def qkv_kernel(xl, xo, xr, wq, wk, wv, vec, q, k, v):
+def qkv_kernel(xl, xo, xr, wq, wk, wv, vec, q, k, v, x):
     rows = xo.shape[0]
-    for w, out, b in ((wq, q, vec[0:1, :]), (wk, k, None), (wv, v, vec[1:2, :])):
-        def put(x, start, size):
-            r = dot(x, w[...])
-            if b is not None:
-                r = r + b
-            out[pl.ds(start, size), :] = r.astype(BF16)
-
-        put(xl[...], 0, HALO)
-        put(xr[...], HALO + rows, HALO)
-
-        def step(i, c):
-            s = pl.multiple_of(i * 256, 256)
-            put(xo[pl.ds(s, 256), :], pl.multiple_of(HALO + s, 128), 256)
-            return c
-
-        lax.fori_loop(0, rows // 256, step, 0)
+
+    @pl.when(pl.program_id(0) == 0)
+    def _():
+        x[pl.ds(0, HALO), :] = xl[...]
+        x[pl.ds(HALO, rows), :] = xo[...]
+        x[pl.ds(HALO + rows, HALO), :] = xr[...]
+
+    q[...] = (dot(x[...], wq[...]) + vec[0:1, :]).astype(BF16)
+    k[...] = dot(x[...], wk[...]).astype(BF16)
+    v[...] = (dot(x[...], wv[...]) + vec[1:2, :]).astype(BF16)
 
 
 def qkv_call(xl, xo, xr, wq, wk, wv, vec):
     rows, d = xo.shape
     win = rows + 2 * HALO
-    tn = 512
+    tn = 256
     wspec = pl.BlockSpec((d, tn), lambda j: (0, j))
     ospec = pl.BlockSpec((win, tn), lambda j: (0, j))
     out = jax.ShapeDtypeStruct((win, d), BF16)
@@ -72,129 +66,146 @@
                   pl.BlockSpec((8, tn), lambda j: (0, j))],
         out_specs=[ospec] * 3,
         out_shape=[out] * 3,
+        scratch_shapes=[pltpu.VMEM((win, d), BF16)],
         compiler_params=params(),
         cost_estimate=cost(6 * win * d * d, 2 * (4 * win * d + 3 * d * d)),
         name="qkv",
     )(xl, xo, xr, wq, wk, wv, vec)
 
 
-def probs_t(k, qh):
-    st = dot_nt(k, qh)
-    e = jnp.exp(st - jnp.max(st, axis=0, keepdims=True))
-    return e * (1.0 / jnp.sum(e, axis=0, keepdims=True))
-
-
-def attn_fwd_kernel(tab, q_ref, k_ref, v_ref, o_ref, ctx):
-    blocks = o_ref.shape[0] // GRAN
-
+LANES = 512
+TOGETHER = {1: 4, 2: 2, 3: 1, 4: 1}
+
+
+def sequences(tab, blocks, fn):
     def one(b, c):
         n = tab[1, b]
         s0 = tab[0, b]
         for nn in range(1, 5):
             @pl.when(n == nn)
             def _():
-                size = nn * GRAN
-                rows = pl.ds(pl.multiple_of(s0 * GRAN, GRAN), size)
-                q = q_ref[rows, :] * jnp.asarray(0.125, BF16)
-                k = k_ref[rows, :]
-                vt = v_ref[rows, :].T
-                low = lax.broadcasted_iota(jnp.int32, q.shape, 1) < HD
-                parts = []
-                for h in range(2):
-                    qh = jnp.where(low if h == 0 else ~low, q, jnp.zeros_like(q))
-                    p = probs_t(k, qh).astype(BF16)
-                    parts.append(dot(vt[h * HD:(h + 1) * HD, :], p))
-                ctx[rows, :] = jnp.concatenate(parts, axis=0).T.astype(BF16)
+                rows = pl.ds(pl.multiple_of(s0 * GRAN, GRAN), nn * GRAN)
+                per = TOGETHER[nn]
+
+                def group(i, c):
+                    pairs = [i * per + j for j in range(per)]
+                    fn(rows, [(pl.ds(pl.multiple_of(p * 2 * HD, 2 * HD), 2 * HD), 2 * p) for p in pairs])
+                    return c
+
+                lax.fori_loop(0, LANES // (2 * HD) // per, group, 0)
         return c
 
     lax.fori_loop(0, blocks, one, 0)
+
+
+def masks(shape):
+    low = lax.broadcasted_iota(jnp.int32, shape, 1) < HD
+    return low, ~low
+
+
+def eighth(x):
+    return x * jnp.asarray(0.125, BF16)
+
+
+def attn_fwd_kernel(tab, q_ref, k_ref, v_ref, o_ref, lse_ref, ctx):
+    def work(rows, pairs):
+        mine = masks((rows.size, 2 * HD))
+        st = []
+        for c, h in pairs:
+            q, k = eighth(q_ref[rows, c]), k_ref[rows, c]
+            st += [dot_nt(k, jnp.where(m, q, jnp.zeros_like(q))) for m in mine]
+        top = [jnp.max(s, axis=0, keepdims=True) for s in st]
+        e = [jnp.exp(s - m) for s, m in zip(st, top)]
+        total = [jnp.sum(x, axis=0, keepdims=True) for x in e]
+        for i, (c, h) in enumerate(pairs):
+            vt = v_ref[rows, c].T
+            parts = []
+            for j in range(2):
+                x = 2 * i + j
+                parts.append(dot(vt[j * HD:(j + 1) * HD, :], e[x].astype(BF16)) * (1.0 / total[x]))
+                lse_ref[pl.ds(h + j, 1), rows] = top[x] + jnp.log(total[x])
+            ctx[rows, c] = jnp.concatenate(parts, axis=0).T.astype(BF16)
+
+    sequences(tab, o_ref.shape[0] // GRAN, work)
     o_ref[...] = ctx[pl.ds(HALO, o_ref.shape[0]), :]
 
 
 def attn_fwd_call(tab, q, k, v, rows):
     win, d = q.shape
-    spec = pl.BlockSpec((win, 2 * HD), lambda h, t: (0, h))
+    spec = pl.BlockSpec((win, LANES), lambda h, t: (0, h))
     return pl.pallas_call(
         attn_fwd_kernel,
         grid_spec=pltpu.PrefetchScalarGridSpec(
             num_scalar_prefetch=1,
-            grid=(d // (2 * HD),),
+            grid=(d // LANES,),
             in_specs=[spec] * 3,
-            out_specs=pl.BlockSpec((rows, 2 * HD), lambda h, t: (0, h)),
-            scratch_shapes=[pltpu.VMEM((win, 2 * HD), BF16)],
+            out_specs=[pl.BlockSpec((rows, LANES), lambda h, t: (0, h)), pl.BlockSpec((LANES // HD, win), lambda h, t: (h, 0))],
+            scratch_shapes=[pltpu.VMEM((win, LANES), BF16)],
         ),
-        out_shape=jax.ShapeDtypeStruct((rows, d), BF16),
+        out_shape=[jax.ShapeDtypeStruct((rows, d), BF16), jax.ShapeDtypeStruct((d // HD, win), F32)],
         compiler_params=params(),
         cost_estimate=cost(8 * rows * 512 * d, 8 * win * d, rows * 512 * 16),
         name="attn_fwd",
     )(tab, q, k, v)
 
 
-def attn_bwd_kernel(tab, q_ref, k_ref, v_ref, gl, go, gr, dq_o, dk_o, dv_o, g_s, dq_s, dk_s, dv_s):
+def attn_bwd_kernel(tab, q_ref, k_ref, v_ref, lse_ref, gl, go, gr, dq_o, dk_o, dv_o, g_s, dq_s, dk_s, dv_s):
     rows_own = go.shape[0]
-    blocks = rows_own // GRAN
     g_s[pl.ds(0, HALO), :] = gl[...]
     g_s[pl.ds(HALO, rows_own), :] = go[...]
     g_s[pl.ds(HALO + rows_own, HALO), :] = gr[...]
 
-    def one(b, c):
-        n = tab[1, b]
-        s0 = tab[0, b]
-        for nn in range(1, 5):
-            @pl.when(n == nn)
-            def _():
-                size = nn * GRAN
-                rows = pl.ds(pl.multiple_of(s0 * GRAN, GRAN), size)
-                q = q_ref[rows, :] * jnp.asarray(0.125, BF16)
-                k = k_ref[rows, :]
-                v = v_ref[rows, :]
-                g = g_s[rows, :]
-                kt = (k * jnp.asarray(0.125, BF16)).T
-                low = lax.broadcasted_iota(jnp.int32, q.shape, 1) < HD
-                zero = jnp.zeros_like(q)
-                dqs, dks, dvs = [], [], []
-                for h in range(2):
-                    mine = low if h == 0 else ~low
-                    p = probs_t(k, jnp.where(mine, q, zero))
-                    dp = dot_nt(v, jnp.where(mine, g, zero))
-                    delta = jnp.sum(p * dp, axis=0, keepdims=True)
-                    ds = (p * (dp - delta)).astype(BF16)
-                    dvs.append(dot(p.astype(BF16), g))
-                    dks.append(dot(ds, q))
-                    dqs.append(dot(kt[h * HD:(h + 1) * HD, :], ds))
-                dq_s[rows, :] = jnp.concatenate(dqs, axis=0).T.astype(BF16)
-                dk_s[rows, :] = jnp.where(low, dks[0], dks[1]).astype(BF16)
-                dv_s[rows, :] = jnp.where(low, dvs[0], dvs[1]).astype(BF16)
-        return c
-
-    lax.fori_loop(0, blocks, one, 0)
+    def work(rows, pairs):
+        mine = masks((rows.size, 2 * HD))
+        qs, gs, p, dp = [], [], [], []
+        for c, h in pairs:
+            q, k, v, g = eighth(q_ref[rows, c]), k_ref[rows, c], v_ref[rows, c], g_s[rows, c]
+            zero = jnp.zeros_like(q)
+            for j, m in enumerate(mine):
+                st = dot_nt(k, jnp.where(m, q, zero))
+                p.append(jnp.exp(st - lse_ref[pl.ds(h + j, 1), rows]))
+                dp.append(dot_nt(v, jnp.where(m, g, zero)))
+            qs.append(q)
+            gs.append(g)
+        delta = [jnp.sum(a * b, axis=0, keepdims=True) for a, b in zip(p, dp)]
+        ds = [(a * (b - d)).astype(BF16) for a, b, d in zip(p, dp, delta)]
+        for i, (c, h) in enumerate(pairs):
+            kt = eighth(k_ref[rows, c]).T
+            dq = [dot(kt[j * HD:(j + 1) * HD, :], ds[2 * i + j]) for j in range(2)]
+            dk = [dot(ds[2 * i + j], qs[i]) for j in range(2)]
+            dv = [dot(p[2 * i + j].astype(BF16), gs[i]) for j in range(2)]
+            dq_s[rows, c] = jnp.concatenate(dq, axis=0).T.astype(BF16)
+            dk_s[rows, c] = jnp.where(mine[0], dk[0], dk[1]).astype(BF16)
+            dv_s[rows, c] = jnp.where(mine[0], dv[0], dv[1]).astype(BF16)
+
+    sequences(tab, rows_own // GRAN, work)
     own = pl.ds(HALO, rows_own)
     dq_o[...] = dq_s[own, :]
     dk_o[...] = dk_s[own, :]
     dv_o[...] = dv_s[own, :]
 
 
-def attn_bwd_call(tab, q, k, v, gl, go, gr):
+def attn_bwd_call(tab, q, k, v, lse, gl, go, gr):
     win, d = q.shape
     rows = go.shape[0]
-    spec = pl.BlockSpec((win, 2 * HD), lambda h, t: (0, h))
-    own = pl.BlockSpec((rows, 2 * HD), lambda h, t: (0, h))
-    halo = pl.BlockSpec((HALO, 2 * HD), lambda h, t: (0, h))
+    spec = pl.BlockSpec((win, LANES), lambda h, t: (0, h))
+    own = pl.BlockSpec((rows, LANES), lambda h, t: (0, h))
+    halo = pl.BlockSpec((HALO, LANES), lambda h, t: (0, h))
     out = jax.ShapeDtypeStruct((rows, d), BF16)
     return pl.pallas_call(
         attn_bwd_kernel,
         grid_spec=pltpu.PrefetchScalarGridSpec(
             num_scalar_prefetch=1,
-            grid=(d // (2 * HD),),
-            in_specs=[spec] * 3 + [halo, own, halo],
+            grid=(d // LANES,),
+            in_specs=[spec] * 3 + [pl.BlockSpec((LANES // HD, win), lambda h, t: (h, 0)), halo, own, halo],
             out_specs=[own] * 3,
-            scratch_shapes=[pltpu.VMEM((win, 2 * HD), BF16)] * 4,
+            scratch_shapes=[pltpu.VMEM((win, LANES), BF16)] * 4,
         ),
         out_shape=[out] * 3,
         compiler_params=params(),
         cost_estimate=cost(20 * rows * 512 * d, 14 * win * d, rows * 512 * 16),
         name="attn_bwd",
-    )(tab, q, k, v, gl, go, gr)
+    )(tab, q, k, v, lse, gl, go, gr)
 
 
 def norm_stats(z):
@@ -207,32 +218,9 @@
     return r * (e - jnp.mean(e, axis=-1, keepdims=True) - n * jnp.mean(e * n, axis=-1, keepdims=True))
 
 
-def out_proj_kernel(ctx, w, x, vec, xhat, low, r_o):
-    z = x[...].astype(F32) + (dot(ctx[...], w[...]) + vec[2:3, :])
-    n, r = norm_stats(z)
-    xhat[...] = n
-    r_o[...] = jnp.broadcast_to(r, r_o.shape)
-    low[...] = (n * vec[4:5, :] + vec[5:6, :]).astype(BF16)
-
-
-def out_proj_call(ctx, w, x, vec):
-    rows, d = x.shape
-    tm = 256
-    t = pl.BlockSpec((tm, d), lambda i: (i, 0))
-    return pl.pallas_call(
-        out_proj_kernel,
-        grid=(rows // tm,),
-        in_specs=[t, whole(w.shape), t, whole(vec.shape)],
-        out_specs=[t, t, pl.BlockSpec((tm, 128), lambda i: (i, 0))],
-        out_shape=[jax.ShapeDtypeStruct((rows, d), F32), jax.ShapeDtypeStruct((rows, d), BF16),
-                   jax.ShapeDtypeStruct((rows, 128), F32)],
-        compiler_params=params(),
-        cost_estimate=cost(2 * rows * d * d, rows * d * 10 + 2 * d * d),
-        name="out_proj",
-    )(ctx, w, x, vec)
-
-
 RC = 256
+TF = 512
+TC = 256
 
 
 def chunks(rows, fn):
@@ -243,201 +231,209 @@
     lax.fori_loop(0, rows // RC, step, 0)
 
 
-def ffn_fwd_kernel(low, wu, bu, wd, xhat, g, vec, hid, dg, out, gs, sums, acc):
-    rows = low.shape[0]
+def clip(t, first, count):
+    return jnp.clip(t - first, 0, count - 1)
+
+
+def lanes(t, size):
+    return pl.ds(pl.multiple_of(t * size, size), size)
+
+
+def colsum(v):
+    return jnp.sum(v, axis=0, keepdims=True)
+
+
+def gelu_parts(u):
+    phi = 0.5 * (1.0 + lax.erf(u * (0.5 ** 0.5)))
+    return u * phi, phi + u * (0.3989422804014327 * jnp.exp(-0.5 * u * u))
+
+
+def fwd_kernel(nu, nc, ctx, wo, x, wu, bu, wd, g, vec, xhat, low, r1, hidt, dg, out, gs, sums, z, hid):
     t = pl.program_id(0)
-
-    @pl.when(t == 0)
-    def _():
-        acc[...] = jnp.zeros_like(acc)
-
-    def up(r):
-        u = dot(low[r, :], wu[...]) + bu[...]
-        phi = 0.5 * (1.0 + lax.erf(u * (0.5 ** 0.5)))
-        h = (u * phi).astype(BF16)
-        hid[r, :] = h
-        dg[r, :] = (phi + u * (0.3989422804014327 * jnp.exp(-0.5 * u * u))).astype(BF16)
-        acc[r, :] += dot(h, wd[...])
-
-    chunks(rows, up)
-
-    @pl.when(t == pl.num_programs(0) - 1)
+    rows = x.shape[0]
+
+    @pl.when(t < nc)
+    def _():
+        c = lanes(t, TC)
+        z[:, c] = dot(ctx[...], wo[...]) + x[:, c].astype(F32)
+
+    @pl.when(t == nc - 1)
+    def _():
+        def fin(r):
+            n, rr = norm_stats(z[r, :] + vec[2:3, :])
+            xhat[r, :] = n
+            r1[r, :] = jnp.broadcast_to(rr, (RC, r1.shape[1]))
+            low[r, :] = (n * vec[4:5, :] + vec[5:6, :]).astype(BF16)
+
+        chunks(rows, fin)
+
+    @pl.when((t >= nc) & (t < nc + nu))
+    def _():
+        for j in range(TF // TC):
+            c = slice(j * TC, (j + 1) * TC)
+            h, s = gelu_parts(dot(low[...], wu[:, c]) + bu[:, c])
+            h = h.astype(BF16)
+            dg[:, c] = s.astype(BF16)
+            hid[:, lanes((t - nc) * (TF // TC) + j, TC)] = h
+            hidt[c, :] = h.T
+
+    @pl.when(t >= nc + nu)
+    def _():
+        c = lanes(t - nc - nu, TC)
+        z[:, c] = dot(hid[...], wd[...])
+
+    @pl.when(t == 2 * nc + nu - 1)
     def _():
         sums[...] = jnp.zeros_like(sums)
 
         def fin(r):
-            z = (xhat[r, :] * vec[4:5, :] + vec[5:6, :]) + (acc[r, :] + vec[3:4, :])
-            n, rr = norm_stats(z)
+            v = (xhat[r, :] * vec[4:5, :] + vec[5:6, :]) + (z[r, :] + vec[3:4, :])
+            n, rr = norm_stats(v)
             out[r, :] = (n * vec[6:7, :] + vec[7:8, :]).astype(BF16)
             gv = g[r, :].astype(F32)
-            sums[0:1, :] += jnp.sum(gv * n, axis=0, keepdims=True)
-            sums[1:2, :] += jnp.sum(gv, axis=0, keepdims=True)
+            sums[0:1, :] += colsum(gv * n)
+            sums[1:2, :] += colsum(gv)
             grad = norm_back(gv * vec[6:7, :], n, rr)
             gs[r, :] = grad
-            sums[2:3, :] += jnp.sum(grad.astype(BF16).astype(F32), axis=0, keepdims=True)
+            sums[2:3, :] += colsum(grad.astype(BF16).astype(F32))
 
         chunks(rows, fin)
 
 
-def ffn_fwd_call(low, wu, bu, wd, xhat, g, vec):
+def single(shape):
+    return pl.BlockSpec(shape, lambda *_: (0,) * len(shape), pipeline_mode=pl.Buffered(1))
+
+
+def fwd_call(ctx, wo, x, wu, bu, wd, g, vec):
+    rows, d = x.shape
+    ff = wu.shape[1]
+    nu, nc = ff // TF, d // TC
+    return pl.pallas_call(
+        functools.partial(fwd_kernel, nu, nc),
+        grid=(2 * nc + nu,),
+        in_specs=[single(ctx.shape), pl.BlockSpec((d, TC), lambda t: (0, clip(t, 0, nc))), single(x.shape),
+                  pl.BlockSpec((d, TF), lambda t: (0, clip(t, nc, nu))), pl.BlockSpec((1, TF), lambda t: (0, clip(t, nc, nu))),
+                  pl.BlockSpec((ff, TC), lambda t: (0, clip(t, nc + nu, nc))), single(g.shape), single(vec.shape)],
+        out_specs=[single((rows, d)), single((rows, d)), single((rows, 128)),
+                   pl.BlockSpec((TF, rows), lambda t: (clip(t, nc, nu), 0)), pl.BlockSpec((rows, TF), lambda t: (0, clip(t, nc, nu))),
+                   single((rows, d)), single((rows, d)), single((8, d))],
+        out_shape=[jax.ShapeDtypeStruct((rows, d), F32), jax.ShapeDtypeStruct((rows, d), BF16),
+                   jax.ShapeDtypeStruct((rows, 128), F32), jax.ShapeDtypeStruct((ff, rows), BF16),
+                   jax.ShapeDtypeStruct((rows, ff), BF16), jax.ShapeDtypeStruct((rows, d), BF16),
+                   jax.ShapeDtypeStruct((rows, d), F32), jax.ShapeDtypeStruct((8, d), F32)],
+        scratch_shapes=[pltpu.VMEM((rows, d), F32), pltpu.VMEM((rows, ff), BF16)],
+        compiler_params=params(60),
+        cost_estimate=cost(4 * rows * d * ff, 4 * d * ff + 4 * rows * ff + rows * d * 14, 2 * rows * ff),
+        name="fwd",
+    )(ctx, wo, x, wu, bu, wd, g, vec)
+
+
+def bwd_kernel(nu, nc, low, gs, hidt, dg, wu, wd, xhat, r1, ctx, wo, vec, dwd, dwu, gsf, sums, sumu, gc, dwo, gd, lowt, gu, z, ctxt, ga):
+    t = pl.program_id(0)
+    rows = low.shape[0]
+
+    @pl.when(t == 0)
+    def _():
+        gd[...] = gs[...].astype(BF16)
+        lowt[...] = low[...].T
+        ctxt[...] = ctx[...].T
+
+    @pl.when(t < nu)
+    def _():
+        for j in range(TF // TC):
+            c = slice(j * TC, (j + 1) * TC)
+            g = (dot_nt(gd[...], wd[c, :]) * dg[:, c].astype(F32)).astype(BF16)
+            gu[:, lanes(t * (TF // TC) + j, TC)] = g
+            sumu[:, c] = colsum(g.astype(F32))
+            dwu[:, c] = dot(lowt[...], g).astype(BF16)
+        dwd[...] = dot(hidt[...], gd[...]).astype(BF16)
+
+    @pl.when((t >= nu) & (t < nu + nc))
+    def _():
+        c = lanes(t - nu, TC)
+        z[:, c] = gs[:, c] + dot_nt(gu[...], wu[...])
+
+    @pl.when(t == nu + nc - 1)
+    def _():
+        sums[...] = jnp.zeros_like(sums)
+
+        def fin(r):
+            gf = z[r, :]
+            n = xhat[r, :]
+            sums[0:1, :] += colsum(gf * n)
+            sums[1:2, :] += colsum(gf)
+            grad = norm_back(gf * vec[4:5, :], n, r1[r, 0:1])
+            gsf[r, :] = grad
+            low_g = grad.astype(BF16)
+            ga[r, :] = low_g
+            sums[2:3, :] += colsum(low_g.astype(F32))
+
+        chunks(rows, fin)
+
+    @pl.when(t >= nu + nc)
+    def _():
+        c = lanes(t - nu - nc, TC)
+        gc[...] = dot_nt(ga[...], wo[...]).astype(BF16)
+        dwo[...] = dot(ctxt[...], ga[:, c]).astype(BF16)
+
+
+def bwd_call(low, gs, hidt, dg, wu, wd, xhat, r1, ctx, wo, vec):
     rows, d = low.shape
     ff = wu.shape[1]
-    tf = 512
-    col = pl.BlockSpec((rows, tf), lambda t: (0, t))
+    nu, nc = ff // TF, d // TC
+
+    def up(t):
+        return clip(t, 0, nu)
+
+    def last(t):
+        return clip(t, nu + nc, nc)
+
     return pl.pallas_call(
-        ffn_fwd_kernel,
-        grid=(ff // tf,),
-        in_specs=[whole(low.shape), pl.BlockSpec((d, tf), lambda t: (0, t)), pl.BlockSpec((1, tf), lambda t: (0, t)),
-                  pl.BlockSpec((tf, d), lambda t: (t, 0)), whole(xhat.shape), whole(g.shape), whole(vec.shape)],
-        out_specs=[col, col, whole((rows, d)), whole((rows, d)), whole((8, d))],
-        out_shape=[jax.ShapeDtypeStruct((rows, ff), BF16), jax.ShapeDtypeStruct((rows, ff), BF16),
-                   jax.ShapeDtypeStruct((rows, d), BF16), jax.ShapeDtypeStruct((rows, d), F32),
-                   jax.ShapeDtypeStruct((8, d), F32)],
-        scratch_shapes=[pltpu.VMEM((rows, d), F32)],
-        compiler_params=params(),
-        cost_estimate=cost(4 * rows * d * ff, 4 * d * ff + 4 * rows * ff + rows * d * 14, 2 * rows * ff),
-        name="ffn_fwd",
-    )(low, wu, bu, wd, xhat, g, vec)
-
-
-def ffn_bwd_kernel(low, gs, hid, dg, wu, wd, xhat, r1, vec, dwd, dwu, gsf, sums, sumu, acc, gd, lowt, gu):
-    rows = low.shape[0]
-    t = pl.program_id(0)
-    tf = hid.shape[1]
-
-    @pl.when(t == 0)
-    def _():
-        acc[...] = gs[...]
-        gd[...] = gs[...].astype(BF16)
-        lowt[...] = low[...].T
-
-    sumu[...] = jnp.zeros_like(sumu)
-
-    def back(r):
-        gh = dot_nt(gd[r, :], wd[...])
-        g = (gh * dg[r, :].astype(F32)).astype(BF16)
-        gu[r, :] = g
-        sumu[...] += jnp.sum(g.astype(F32), axis=0, keepdims=True)
-        acc[r, :] += dot_nt(g, wu[...])
-
-    chunks(rows, back)
-    for j in range(tf // 256):
-        c = slice(j * 256, (j + 1) * 256)
-        dwd[c, :] = dot(hid[:, c].T, gd[...]).astype(BF16)
-
-    def wgrad(r):
-        dwu[r, :] = dot(lowt[r, :], gu[...]).astype(BF16)
-
-    chunks(lowt.shape[0], wgrad)
-
-    @pl.when(t == pl.num_programs(0) - 1)
-    def _():
-        sums[...] = jnp.zeros_like(sums)
-
-        def fin(r):
-            gf = acc[r, :]
-            n = xhat[r, :]
-            sums[0:1, :] += jnp.sum(gf * n, axis=0, keepdims=True)
-            sums[1:2, :] += jnp.sum(gf, axis=0, keepdims=True)
-            grad = norm_back(gf * vec[4:5, :], n, r1[r, 0:1])
-            gsf[r, :] = grad
-            sums[2:3, :] += jnp.sum(grad.astype(BF16).astype(F32), axis=0, keepdims=True)
-
-        chunks(rows, fin)
-
-
-def ffn_bwd_call(low, gs, hid, dg, wu, wd, xhat, r1, vec):
-    rows, d = low.shape
-    ff = wu.shape[1]
-    tf = 512
-    col = pl.BlockSpec((rows, tf), lambda t: (0, t))
-    wus = pl.BlockSpec((d, tf), lambda t: (0, t))
-    wds = pl.BlockSpec((tf, d), lambda t: (t, 0))
-    once = dict(pipeline_mode=pl.Buffered(1))
-
-    def one(shape):
-        return pl.BlockSpec(shape, lambda *_: (0,) * len(shape), **once)
-
-    return pl.pallas_call(
-        ffn_bwd_kernel,
-        grid=(ff // tf,),
-        in_specs=[one(low.shape), one(gs.shape), col, col, wus, wds, one(xhat.shape), one(r1.shape), one(vec.shape)],
-        out_specs=[wds, wus, whole((rows, d)), whole((8, d)), pl.BlockSpec((1, tf), lambda t: (0, t))],
+        functools.partial(bwd_kernel, nu, nc),
+        grid=(nu + 2 * nc,),
+        in_specs=[single(low.shape), single(gs.shape), pl.BlockSpec((TF, rows), lambda t: (up(t), 0)),
+                  pl.BlockSpec((rows, TF), lambda t: (0, up(t))), pl.BlockSpec((TC, ff), lambda t: (clip(t, nu, nc), 0)),
+                  pl.BlockSpec((TF, d), lambda t: (up(t), 0)), single(xhat.shape), single(r1.shape), single(ctx.shape),
+                  pl.BlockSpec((TC, d), lambda t: (last(t), 0)), single(vec.shape)],
+        out_specs=[pl.BlockSpec((TF, d), lambda t: (up(t), 0)), pl.BlockSpec((d, TF), lambda t: (0, up(t))), single((rows, d)),
+                   single((8, d)), pl.BlockSpec((1, TF), lambda t: (0, up(t))), pl.BlockSpec((rows, TC), lambda t: (0, last(t))),
+                   pl.BlockSpec((d, TC), lambda t: (0, last(t)))],
         out_shape=[jax.ShapeDtypeStruct((ff, d), BF16), jax.ShapeDtypeStruct((d, ff), BF16),
                    jax.ShapeDtypeStruct((rows, d), F32), jax.ShapeDtypeStruct((8, d), F32),
-                   jax.ShapeDtypeStruct((1, ff), F32)],
-        scratch_shapes=[pltpu.VMEM((rows, d), F32), pltpu.VMEM((rows, d), BF16), pltpu.VMEM((d, rows), BF16),
-                        pltpu.VMEM((rows, tf), BF16)],
-        compiler_params=params(),
+                   jax.ShapeDtypeStruct((1, ff), F32), jax.ShapeDtypeStruct((rows, d), BF16), jax.ShapeDtypeStruct((d, d), BF16)],
+        scratch_shapes=[pltpu.VMEM((rows, d), BF16), pltpu.VMEM((d, rows), BF16), pltpu.VMEM((rows, ff), BF16),
+                        pltpu.VMEM((rows, d), F32), pltpu.VMEM((d, rows), BF16), pltpu.VMEM((rows, d), BF16)],
+        compiler_params=params(60),
         cost_estimate=cost(8 * rows * d * ff, 8 * d * ff + 4 * rows * ff + rows * d * 18),
-        name="ffn_bwd",
-    )(low, gs, hid, dg, wu, wd, xhat, r1, vec)
-
-
-def out_bwd_kernel(gsf, ctx, w, gc, dwo, ga, ctxt):
-    rows = gsf.shape[0]
-
-    def cast(r):
-        ga[r, :] = gsf[r, :].astype(BF16)
-        gc[r, :] = dot_nt(ga[r, :], w[...]).astype(BF16)
-
-    chunks(rows, cast)
-    ctxt[...] = ctx[...].T
-
-    def wgrad(r):
-        dwo[r, :] = dot(ctxt[r, :], ga[...]).astype(BF16)
-
-    chunks(ctxt.shape[0], wgrad)
-
-
-def out_bwd_call(gsf, ctx, w):
-    rows, d = gsf.shape
-    return pl.pallas_call(
-        out_bwd_kernel,
-        grid=(1,),
-        in_specs=[whole(gsf.shape), whole(ctx.shape), whole(w.shape)],
-        out_specs=[whole((rows, d)), whole((d, d))],
-        out_shape=[jax.ShapeDtypeStruct((rows, d), BF16), jax.ShapeDtypeStruct((d, d), BF16)],
-        scratch_shapes=[pltpu.VMEM((rows, d), BF16), pltpu.VMEM((d, rows), BF16)],
-        compiler_params=params(),
-        cost_estimate=cost(4 * rows * d * d, rows * d * 8 + 4 * d * d),
-        name="out_bwd",
-    )(gsf, ctx, w)
+        name="bwd",
+    )(low, gs, hidt, dg, wu, wd, xhat, r1, ctx, wo, vec)
 
 
 def in_bwd_kernel(x, gsf, dq, dk, dv, wq, wk, wv, tg, dwq, dwk, dwv, sums, xt):
-    rows = x.shape[0]
-    xt[...] = x[...].T
-    sums[...] = jnp.zeros_like(sums)
-
-    def tok(r):
-        g = gsf[r, :] + dot_nt(dq[r, :], wq[...]) + dot_nt(dk[r, :], wk[...]) + dot_nt(dv[r, :], wv[...])
-        tg[r, :] = g.astype(BF16)
-        sums[0:1, :] += jnp.sum(dq[r, :].astype(F32), axis=0, keepdims=True)
-        sums[1:2, :] += jnp.sum(dv[r, :].astype(F32), axis=0, keepdims=True)
-
-    chunks(rows, tok)
-
-    def wgrad(r):
-        dwq[r, :] = dot(xt[r, :], dq[...]).astype(BF16)
-        dwk[r, :] = dot(xt[r, :], dk[...]).astype(BF16)
-        dwv[r, :] = dot(xt[r, :], dv[...]).astype(BF16)
-
-    chunks(xt.shape[0], wgrad)
+    t = pl.program_id(0)
+
+    @pl.when(t == 0)
+    def _():
+        xt[...] = x[...].T
+
+    c = lanes(t, TC)
+    g = gsf[...] + dot_nt(dq[...], wq[...]) + dot_nt(dk[...], wk[...]) + dot_nt(dv[...], wv[...])
+    tg[...] = g.astype(BF16)
+    sums[0:1, :] = colsum(dq[:, c].astype(F32))
+    sums[1:2, :] = colsum(dv[:, c].astype(F32))
+    for a, o in ((dq, dwq), (dk, dwk), (dv, dwv)):
+        o[...] = dot(xt[...], a[:, c]).astype(BF16)
 
 
 def in_bwd_call(x, gsf, dq, dk, dv, wq, wk, wv):
     rows, d = x.shape
-    once = dict(pipeline_mode=pl.Buffered(1))
-
-    def one(shape):
-        return pl.BlockSpec(shape, lambda *_: (0,) * len(shape), **once)
-
+    col = pl.BlockSpec((rows, TC), lambda t: (0, t))
+    wcol = pl.BlockSpec((d, TC), lambda t: (0, t))
     return pl.pallas_call(
         in_bwd_kernel,
-        grid=(1,),
-        in_specs=[one((rows, d))] * 5 + [one((d, d))] * 3,
-        out_specs=[one((rows, d))] + [one((d, d))] * 3 + [one((8, d))],
+        grid=(d // TC,),
+        in_specs=[single((rows, d)), col] + [single((rows, d))] * 3 + [pl.BlockSpec((TC, d), lambda t: (t, 0))] * 3,
+        out_specs=[col] + [wcol] * 3 + [pl.BlockSpec((8, TC), lambda t: (0, t))],
         out_shape=[jax.ShapeDtypeStruct((rows, d), BF16)] + [jax.ShapeDtypeStruct((d, d), BF16)] * 3
         + [jax.ShapeDtypeStruct((8, d), F32)],
         scratch_shapes=[pltpu.VMEM((d, rows), BF16)],
@@ -766,6 +762,20 @@
     )(*views)
 
 
+def hand_on_kernel(*refs):
+    half = len(refs) // 2
+    for a, b in zip(refs[:half], refs[half:]):
+        b[...] = a[...]
+
+
+def hand_on(arrays):
+    return pl.pallas_call(
+        hand_on_kernel,
+        out_shape=[jax.ShapeDtypeStruct(a.shape, a.dtype) for a in arrays],
+        name="hand_on",
+    )(*arrays)
+
+
 def sequence_table(lengths, own, rows):
     ids = jnp.arange(lengths.shape[0], dtype=jnp.int32)
     starts = jnp.sum(jnp.where(ids[None, :] < ids[:, None], lengths[None, :], 0), axis=1)
@@ -807,16 +817,15 @@
     vec, bu = unpack(packed.astype(F32), n, part)
     tab = sequence_table(lengths, own, rows)
     q, k, v = qkv_call(xl, tokens, xr, wq, wk, wv, vec)
-    ctx = attn_fwd_call(tab, q, k, v, rows)
-    xhat, low, r1 = out_proj_call(ctx, wo, tokens, vec)
-    hid, dg, layer_out, gs, sums2 = ffn_fwd_call(low, wu, bu, wd, xhat, cotangent, vec)
-    dwd, dwu, gsf, sums1, sumu = ffn_bwd_call(low, gs, hid, dg, wu, wd, xhat, r1, vec)
-    gc, dwo = out_bwd_call(gsf, ctx, wo)
+    ctx, lse = attn_fwd_call(tab, q, k, v, rows)
+    xhat, low, r1, hidt, dg, layer_out, gs, sums2 = fwd_call(ctx, wo, tokens, wu, bu, wd, cotangent, vec)
+    dwd, dwu, gsf, sums1, sumu, gc, dwo = bwd_call(low, gs, hidt, dg, wu, wd, xhat, r1, ctx, wo, vec)
     gl, gr = halo(gc, n)
-    dq, dk, dv = attn_bwd_call(tab, q, k, v, gl, gc, gr)
+    dq, dk, dv = attn_bwd_call(tab, q, k, v, lse, gl, gc, gr)
     tg, dwq, dwk, dwv, sums0 = in_bwd_call(tokens, gsf, dq, dk, dv, wq, wk, wv)
     small = pack([sums0[0], sums0[1], sums1[2], sums2[2], sums1[0], sums1[1], sums2[0], sums2[1], sumu], n, 8, F32)
     tiny, gd, gu, go, gq, gk, gv = reduce_call(n, [small, dwd, dwu, dwo, dwq, dwk, dwv], d)
+    gq, gk, gv, go, gu, gd = hand_on([gq, gk, gv, go, gu, gd])
     vecs, ubg = unpack(tiny, 1, part)
     t = [vecs[i] for i in range(8)]
     return (layer_out, tg, gq, gk, gv, go, gu, gd, t[0], t[1], t[2], ubg[0], t[3], t[4], t[5], t[6], t[7])

time: 567 us -> 515 us (0.908)
  Pallas kernels: 531 us -> 487 us
  local copies, waits for them, and re-layouts: 20.9 us -> 11.5 us
    pallas_call x1, Pallas kernels: 40.9 us -> 14.6 us  [attn_fwd_call(): pl.pallas_call(attn_fwd_kernel, grid_spec=pltpu.PrefetchScalarGridSpec(nu...]
    pallas_call x1, Pallas kernels: 46 us -> 19.7 us  [attn_bwd_call(): pl.pallas_call(attn_bwd_kernel, grid_spec=pltpu.PrefetchScalarGridSpec(nu...]
    pallas_call x1, Pallas kernels: 142 us -> 161 us  [reduce_call(): pl.pallas_call(functools.partial(reduce_kernel, n, plan, len(grads)), in_...]
    unnamed x19 -> x11, local copies, waits for them, and re-layouts: 12.9 us -> 3.42 us
    pallas_call x1, Pallas kernels: 22.4 us -> 16.7 us  [qkv_call(): pl.pallas_call(qkv_kernel, grid=(d // tn,), in_specs=[whole(xl.shape), wh...]
    pallas_call x5 -> x4, Pallas kernels: 149 us -> 144 us  [the longest x1 74.5 us: bwd_call(): pl.pallas_call(functools.partial(bwd_kernel, nu, nc), grid=(nu + 2 * nc,)...]
where the time goes in v3:
time: 515 us; the launch traced here: 510 us
  Pallas kernels  487 us (95%)
  local copies, waits for them, and re-layouts  11.5 us (2%)
  starting transfers between devices  9.36 us (2%)
    pallas_call x1, Pallas kernels, reduce_call(): pl.pallas_call(functools.partial(reduce_kernel, n, plan, len(grads)), in_...  161 us
    pallas_call x1, Pallas kernels, gather_call(): pl.pallas_call(functools.partial(gather_kernel, n, plan, len(shards)), in...  131 us
    pallas_call x1, Pallas kernels, bwd_call(): pl.pallas_call(functools.partial(bwd_kernel, nu, nc), grid=(nu + 2 * nc,)...  74.5 us
    pallas_call x1, Pallas kernels, fwd_call(): pl.pallas_call(functools.partial(fwd_kernel, nu, nc), grid=(2 * nc + nu,)...  46.4 us
    pallas_call x1, Pallas kernels, in_bwd_call(): pl.pallas_call(in_bwd_kernel, grid=(d // TC,), in_specs=[single((rows, d)...  20.3 us
    pallas_call x1, Pallas kernels, attn_bwd_call(): pl.pallas_call(attn_bwd_kernel, grid_spec=pltpu.PrefetchScalarGridSpec(nu...  19.7 us
    pallas_call x1, Pallas kernels, qkv_call(): pl.pallas_call(qkv_kernel, grid=(d // tn,), in_specs=[whole(xl.shape), wh...  16.7 us
    pallas_call x1, Pallas kernels, attn_fwd_call(): pl.pallas_call(attn_fwd_kernel, grid_spec=pltpu.PrefetchScalarGridSpec(nu...  14.6 us
  transfers between devices with their start and end apart: 2, of which 1 were waited for; matrix products, arithmetic and copies ran while one was open for 0% of the time, Pallas kernels for 0%

profile of v3, /device:TPU:0, one launch (start us, length us, event | category | flops | bytes accessed | tf_op | source)
XLA Modules:
  0.0 510.2 jit_solution(15805629506455655973)
XLA Ops:
  0.7 0.9 concatenate.6
  1.6 0.6 reshape.287.refs_0_
  2.2 131.0 %gather.1 = (bf16[4,2,2,2,16,256]{5,4,3,2,1,0:T(8,128)(2,1)}, bf16[4,2,2,2,32,1024]{5,4,3,2,1,0:T(8,128)(2,1)}, bf16[4,2,2,2,32,1024]{5,4,3,2,1,0:T(8,128)(2,1)}...) custom-call(bf16[16,256]{1,0:T(8,128)(2,1)} %reshape.287.refs_0_, ...), custom_call_target="tpu_custom_call" | custom-call | tf_op jit(solution)/shard_map/gather/pallas_call | solution.py:596
  133.2 1.0 copy.37
  134.3 0.6 slice.102
  135.1 0.7 reshape.292.vec
  136.6 16.7 %qkv.1 = (bf16[1792,1024]{1,0:T(8,128)(2,1)}, bf16[1792,1024]{1,0:T(8,128)(2,1)}, bf16[1792,1024]{1,0:T(8,128)(2,1)}) custom-call(bf16[384,1024]{1,0:T(8,128)(2,1)} %get-tuple-element.67.xl, bf16[1024,1024]{1,0:T(8,128)(2,1)} %x.7, bf16[384,1024]{1,0:T(8,128)(2,1)} %get-tuple-element.68.xr, bf16[1024,1024]{1,0:T(8,128)(2,1)} %bitcast.97, ...), custom_call_target="tpu_custom_call" | custom-call | flops 11274289152 | bytes 20971520 | tf_op jit(solution)/shard_map/qkv/pallas_call | solution.py:62
  153.3 14.6 %attn_fwd.1 = (bf16[1024,1024]{1,0:T(8,128)(2,1)}, f32[16,1792]{1,0:T(8,128)}) custom-call(s32[2,8]{1,0:T(2,128)} %pad_add_fusion.tab, bf16[1792,1024]{1,0:T(8,128)(2,1)} %get-tuple-element.73.q_ref, bf16[1792,1024]{1,0:T(8,128)(2,1)} %get-tuple-element.74.k_ref, bf16[1792,1024]{1,0:T(8,128)(2,1)} %get-tuple-element.75.v_ref), custom_call_target="tpu_custom_call" | custom-call | flops 4294967296 | bytes 14680064 | tf_op jit(solution)/shard_map/attn_fwd/pallas_call | solution.py:136
  167.9 46.4 %fwd.1 = (f32[1024,1024]{1,0:T(8,128)}, bf16[1024,1024]{1,0:T(8,128)(2,1)}, f32[1024,128]{1,0:T(8,128)}, bf16[4096,1024]{1,0:T(8,128)(2,1)}, bf16[1024,4096]{1,0...) custom-call(bf16[1024,1024]{1,0:T(8,128)(2,1)} %get-tuple-element.76.ctx, ...), custom_call_target="tpu_custom_call" | custom-call | flops 17179869184 | bytes 48234496 | tf_op jit(solution)/shard_map/fwd/pallas_call | solution.py:311
  214.3 74.5 %bwd.1 = (bf16[4096,1024]{1,0:T(8,128)(2,1)}, bf16[1024,4096]{1,0:T(8,128)(2,1)}, f32[1024,1024]{1,0:T(8,128)}, f32[8,1024]{1,0:T(8,128)}, f32[1,4096]{1,0:T(1,1...) custom-call(bf16[1024,1024]{1,0:T(8,128)(2,1)} %get-tuple-element.81.low, ...), custom_call_target="tpu_custom_call" | custom-call | flops 34359738368 | bytes 69206016 | tf_op jit(solution)/shard_map/bwd/pallas_call | solution.py:391
  288.8 1.5 fusion.1
  290.3 1.3 collective-permute-start.1
  291.6 8.1 %collective-permute-start = (bf16[384,1024]{1,0:T(8,128)(2,1)S(1)}, bf16[384,1024]{1,0:T(8,128)(2,1)S(1)}, u32[]{:S(2)}, u32[]{:S(2)}) collective-permute-start(bf16[384,1024]{1,0:T(8,128)(2,1)S(1)} %get-tuple-element.128), channel_id=1, source_target_pairs={{0,1},{1,2},{2,3},{3,4},{4,5},{5,6},{6,7},{7,8},{8,9},{9,10},{10,1... | collective-permute-start | bytes 2359304 | tf_op jit(solution)/shard_map/ppermute | solution.py:794
  299.6 0.9 slice_reduce_fusion.2
  300.8 0.7 collective-permute-done.gl
  301.7 0.7 copy-done.3
  302.4 19.7 %attn_bwd.1 = (bf16[1024,1024]{1,0:T(8,128)(2,1)}, bf16[1024,1024]{1,0:T(8,128)(2,1)}, bf16[1024,1024]{1,0:T(8,128)(2,1)}) custom-call(s32[2,8]{1,0:T(2,128)} %pad_add_fusion.tab, bf16[1792,1024]{1,0:T(8,128)(2,1)} %get-tuple-element.73.q_ref, bf16[1792,1024]{1,0:T(8,128)(2,1)} %get-tuple-element.74.k_ref, bf16[1792,1024]{1,0:T(8,128)(2,1)} %get-tuple-element.75.v_ref, ...), custom_call_target="tpu_custom_call" | custom-call | flops 10737418240 | bytes 25690112 | tf_op jit(solution)/shard_map/attn_bwd/pallas_call | solution.py:195
  322.0 20.3 %in_bwd.1 = (bf16[1024,1024]{1,0:T(8,128)(2,1)}, bf16[1024,1024]{1,0:T(8,128)(2,1)}, bf16[1024,1024]{1,0:T(8,128)(2,1)}, bf16[1024,1024]{1,0:T(8,128)(2,1)}, f32[8,1024]{1,0:T(8,128)}) custom-call(bf16[1024,1024]{1,0:T(8,128)(2,1)} %x.7, f32[1024,1024]{1,0:T(8,128)} %get-tuple-element.87.gsf, bf16[1024,1024]{1,0:T(8,128)(2,1)} %get-tuple-element.90.dq, ...), custom_call_target="tpu_custom_call" | custom-call | flops 12884901888 | bytes 27262976 | tf_op jit(solution)/shard_map/in_bwd/pallas_call | solution.py:432
  342.4 0.9 slice_reduce_fusion
  343.8 0.8 copy.38
  344.6 161.2 %reduce.35 = (f32[8,256]{1,0:T(8,128)}, f32[128,1024]{1,0:T(8,128)}, f32[32,4096]{1,0:T(8,128)}, f32[32,1024]{1,0:T(8,128)}, f32[32,1024]{1,0:T(8,128)}, /*index=5*/f32[32,1024]{1,0:T(8,128)}, f32[32,1024]{1,0:T(8,128)}) custom-call(f32[4,2,2,2,8,256]{5,4,3,2,1,0:T(8,128)} %bitcast.73, bf16[4,2,2,2,128,1024]{5,4,3,2,1,0:T(8,128)(2,1)} %bitcast.67, ...), custom_call_target="tpu_custom_call" | custom-call | tf_op jit(solution)/shard_map/reduce/pallas_call | solution.py:753
  505.8 0.7 copy.39
  507.0 0.6 slice_bitcast_fusion
  507.6 2.6 hand_on.1
  (29 shorter events, 2.4 us)
Async XLA Ops:
  0.7 134.2 %copy-start.1 = (s32[256]{0:T(256)S(1)}, s32[256]{0:T(256)}, u32[]{:S(2)}) copy-start(s32[256]{0:T(256)} %param.21) | copy-start | bytes 3076
  290.3 10.5 %collective-permute-start.1 = (bf16[384,1024]{1,0:T(8,128)(2,1)S(1)}, bf16[384,1024]{1,0:T(8,128)(2,1)S(1)}, u32[]{:S(2)}, u32[]{:S(2)}) collective-permute-start(bf16[384,1024]{1,0:T(8,128)(2,1)S(1)} %get-tuple-element.127), channel_id=1, source_target_pairs={{1,0},{2,1},{3,2},{4,3},{5,4},{6,5},{7,6},{8,7},{9,8},{10,9},{11,1... | collective-permute-start | bytes 2359304 | tf_op jit(solution)/shard_map/ppermute | solution.py:794
  291.6 9.9 %collective-permute-start = (bf16[384,1024]{1,0:T(8,128)(2,1)S(1)}, bf16[384,1024]{1,0:T(8,128)(2,1)S(1)}, u32[]{:S(2)}, u32[]{:S(2)}) collective-permute-start(bf16[384,1024]{1,0:T(8,128)(2,1)S(1)} %get-tuple-element.128), channel_id=1, source_target_pairs={{0,1},{1,2},{2,3},{3,4},{4,5},{5,6},{6,7},{7,8},{8,9},{9,10},{10,1... | collective-permute-start | bytes 2359304 | tf_op jit(solution)/shard_map/ppermute | solution.py:794
  300.8 0.9 copy-start.2
  301.5 0.9 copy-start.3
  322.0 21.6 %copy-start = (f32[1,4096]{1,0:T(1,128)S(1)}, f32[1,4096]{1,0:T(1,128)}, u32[]{:S(2)}) copy-start(f32[1,4096]{1,0:T(1,128)} %get-tuple-element.97) | copy-start | bytes 49156

commit v4 on v3

--- a/solution.py
+++ b/solution.py
@@ -149,7 +149,7 @@
     )(tab, q, k, v)
 
 
-def attn_bwd_kernel(tab, q_ref, k_ref, v_ref, lse_ref, gl, go, gr, dq_o, dk_o, dv_o, g_s, dq_s, dk_s, dv_s):
+def attn_bwd_kernel(tab, q_ref, k_ref, v_ref, lse_ref, gl, go, gr, dq_o, dk_o, dv_o, sums, g_s, dq_s, dk_s, dv_s):
     rows_own = go.shape[0]
     g_s[pl.ds(0, HALO), :] = gl[...]
     g_s[pl.ds(HALO, rows_own), :] = go[...]
@@ -183,6 +183,8 @@
     dq_o[...] = dq_s[own, :]
     dk_o[...] = dk_s[own, :]
     dv_o[...] = dv_s[own, :]
+    sums[0:1, :] = jnp.sum(dq_o[...].astype(F32), axis=0, keepdims=True)
+    sums[1:2, :] = jnp.sum(dv_o[...].astype(F32), axis=0, keepdims=True)
 
 
 def attn_bwd_call(tab, q, k, v, lse, gl, go, gr):
@@ -198,10 +200,10 @@
             num_scalar_prefetch=1,
             grid=(d // LANES,),
             in_specs=[spec] * 3 + [pl.BlockSpec((LANES // HD, win), lambda h, t: (h, 0)), halo, own, halo],
-            out_specs=[own] * 3,
+            out_specs=[own] * 3 + [pl.BlockSpec((8, LANES), lambda h, t: (0, h))],
             scratch_shapes=[pltpu.VMEM((win, LANES), BF16)] * 4,
         ),
-        out_shape=[out] * 3,
+        out_shape=[out] * 3 + [jax.ShapeDtypeStruct((8, d), F32)],
         compiler_params=params(),
         cost_estimate=cost(20 * rows * 512 * d, 14 * win * d, rows * 512 * 16),
         name="attn_bwd",
@@ -248,7 +250,7 @@
     return u * phi, phi + u * (0.3989422804014327 * jnp.exp(-0.5 * u * u))
 
 
-def fwd_kernel(nu, nc, ctx, wo, x, wu, bu, wd, g, vec, xhat, low, r1, hidt, dg, out, gs, sums, z, hid):
+def fwd_kernel(nu, nc, ctx, wo, x, wu, bu, wd, g, vec, xhat, lowt, ctxt, r1, hidt, dg, out, gs, gd, sums, z, hid, low):
     t = pl.program_id(0)
     rows = x.shape[0]
 
@@ -263,7 +265,10 @@
             n, rr = norm_stats(z[r, :] + vec[2:3, :])
             xhat[r, :] = n
             r1[r, :] = jnp.broadcast_to(rr, (RC, r1.shape[1]))
-            low[r, :] = (n * vec[4:5, :] + vec[5:6, :]).astype(BF16)
+            v = (n * vec[4:5, :] + vec[5:6, :]).astype(BF16)
+            low[r, :] = v
+            lowt[:, r] = v.T
+            ctxt[:, r] = ctx[r, :].T
 
         chunks(rows, fin)
 
@@ -295,7 +300,9 @@
             sums[1:2, :] += colsum(gv)
             grad = norm_back(gv * vec[6:7, :], n, rr)
             gs[r, :] = grad
-            sums[2:3, :] += colsum(grad.astype(BF16).astype(F32))
+            low_g = grad.astype(BF16)
+            gd[r, :] = low_g
+            sums[2:3, :] += colsum(low_g.astype(F32))
 
         chunks(rows, fin)
 
@@ -314,133 +321,18 @@
         in_specs=[single(ctx.shape), pl.BlockSpec((d, TC), lambda t: (0, clip(t, 0, nc))), single(x.shape),
                   pl.BlockSpec((d, TF), lambda t: (0, clip(t, nc, nu))), pl.BlockSpec((1, TF), lambda t: (0, clip(t, nc, nu))),
                   pl.BlockSpec((ff, TC), lambda t: (0, clip(t, nc + nu, nc))), single(g.shape), single(vec.shape)],
-        out_specs=[single((rows, d)), single((rows, d)), single((rows, 128)),
+        out_specs=[single((rows, d)), single((d, rows)), single((d, rows)), single((rows, 128)),
                    pl.BlockSpec((TF, rows), lambda t: (clip(t, nc, nu), 0)), pl.BlockSpec((rows, TF), lambda t: (0, clip(t, nc, nu))),
-                   single((rows, d)), single((rows, d)), single((8, d))],
-        out_shape=[jax.ShapeDtypeStruct((rows, d), F32), jax.ShapeDtypeStruct((rows, d), BF16),
+                   single((rows, d)), single((rows, d)), single((rows, d)), single((8, d))],
+        out_shape=[jax.ShapeDtypeStruct((rows, d), F32), jax.ShapeDtypeStruct((d, rows), BF16), jax.ShapeDtypeStruct((d, rows), BF16),
                    jax.ShapeDtypeStruct((rows, 128), F32), jax.ShapeDtypeStruct((ff, rows), BF16),
                    jax.ShapeDtypeStruct((rows, ff), BF16), jax.ShapeDtypeStruct((rows, d), BF16),
-                   jax.ShapeDtypeStruct((rows, d), F32), jax.ShapeDtypeStruct((8, d), F32)],
-        scratch_shapes=[pltpu.VMEM((rows, d), F32), pltpu.VMEM((rows, ff), BF16)],
+                   jax.ShapeDtypeStruct((rows, d), F32), jax.ShapeDtypeStruct((rows, d), BF16), jax.ShapeDtypeStruct((8, d), F32)],
+        scratch_shapes=[pltpu.VMEM((rows, d), F32), pltpu.VMEM((rows, ff), BF16), pltpu.VMEM((rows, d), BF16)],
         compiler_params=params(60),
         cost_estimate=cost(4 * rows * d * ff, 4 * d * ff + 4 * rows * ff + rows * d * 14, 2 * rows * ff),
         name="fwd",
     )(ctx, wo, x, wu, bu, wd, g, vec)
-
-
-def bwd_kernel(nu, nc, low, gs, hidt, dg, wu, wd, xhat, r1, ctx, wo, vec, dwd, dwu, gsf, sums, sumu, gc, dwo, gd, lowt, gu, z, ctxt, ga):
-    t = pl.program_id(0)
-    rows = low.shape[0]
-
-    @pl.when(t == 0)
-    def _():
-        gd[...] = gs[...].astype(BF16)
-        lowt[...] = low[...].T
-        ctxt[...] = ctx[...].T
-
-    @pl.when(t < nu)
-    def _():
-        for j in range(TF // TC):
-            c = slice(j * TC, (j + 1) * TC)
-            g = (dot_nt(gd[...], wd[c, :]) * dg[:, c].astype(F32)).astype(BF16)
-            gu[:, lanes(t * (TF // TC) + j, TC)] = g
-            sumu[:, c] = colsum(g.astype(F32))
-            dwu[:, c] = dot(lowt[...], g).astype(BF16)
-        dwd[...] = dot(hidt[...], gd[...]).astype(BF16)
-
-    @pl.when((t >= nu) & (t < nu + nc))
-    def _():
-        c = lanes(t - nu, TC)
-        z[:, c] = gs[:, c] + dot_nt(gu[...], wu[...])
-
-    @pl.when(t == nu + nc - 1)
-    def _():
-        sums[...] = jnp.zeros_like(sums)
-
-        def fin(r):
-            gf = z[r, :]
-            n = xhat[r, :]
-            sums[0:1, :] += colsum(gf * n)
-            sums[1:2, :] += colsum(gf)
-            grad = norm_back(gf * vec[4:5, :], n, r1[r, 0:1])
-            gsf[r, :] = grad
-            low_g = grad.astype(BF16)
-            ga[r, :] = low_g
-            sums[2:3, :] += colsum(low_g.astype(F32))
-
-        chunks(rows, fin)
-
-    @pl.when(t >= nu + nc)
-    def _():
-        c = lanes(t - nu - nc, TC)
-        gc[...] = dot_nt(ga[...], wo[...]).astype(BF16)
-        dwo[...] = dot(ctxt[...], ga[:, c]).astype(BF16)
-
-
-def bwd_call(low, gs, hidt, dg, wu, wd, xhat, r1, ctx, wo, vec):
-    rows, d = low.shape
-    ff = wu.shape[1]
-    nu, nc = ff // TF, d // TC
-
-    def up(t):
-        return clip(t, 0, nu)
-
-    def last(t):
-        return clip(t, nu + nc, nc)
-
-    return pl.pallas_call(
-        functools.partial(bwd_kernel, nu, nc),
-        grid=(nu + 2 * nc,),
-        in_specs=[single(low.shape), single(gs.shape), pl.BlockSpec((TF, rows), lambda t: (up(t), 0)),
-                  pl.BlockSpec((rows, TF), lambda t: (0, up(t))), pl.BlockSpec((TC, ff), lambda t: (clip(t, nu, nc), 0)),
-                  pl.BlockSpec((TF, d), lambda t: (up(t), 0)), single(xhat.shape), single(r1.shape), single(ctx.shape),
-                  pl.BlockSpec((TC, d), lambda t: (last(t), 0)), single(vec.shape)],
-        out_specs=[pl.BlockSpec((TF, d), lambda t: (up(t), 0)), pl.BlockSpec((d, TF), lambda t: (0, up(t))), single((rows, d)),
-                   single((8, d)), pl.BlockSpec((1, TF), lambda t: (0, up(t))), pl.BlockSpec((rows, TC), lambda t: (0, last(t))),
-                   pl.BlockSpec((d, TC), lambda t: (0, last(t)))],
-        out_shape=[jax.ShapeDtypeStruct((ff, d), BF16), jax.ShapeDtypeStruct((d, ff), BF16),
-                   jax.ShapeDtypeStruct((rows, d), F32), jax.ShapeDtypeStruct((8, d), F32),
-                   jax.ShapeDtypeStruct((1, ff), F32), jax.ShapeDtypeStruct((rows, d), BF16), jax.ShapeDtypeStruct((d, d), BF16)],
-        scratch_shapes=[pltpu.VMEM((rows, d), BF16), pltpu.VMEM((d, rows), BF16), pltpu.VMEM((rows, ff), BF16),
-                        pltpu.VMEM((rows, d), F32), pltpu.VMEM((d, rows), BF16), pltpu.VMEM((rows, d), BF16)],
-        compiler_params=params(60),
-        cost_estimate=cost(8 * rows * d * ff, 8 * d * ff + 4 * rows * ff + rows * d * 18),
-        name="bwd",
-    )(low, gs, hidt, dg, wu, wd, xhat, r1, ctx, wo, vec)
-
-
-def in_bwd_kernel(x, gsf, dq, dk, dv, wq, wk, wv, tg, dwq, dwk, dwv, sums, xt):
-    t = pl.program_id(0)
-
-    @pl.when(t == 0)
-    def _():
-        xt[...] = x[...].T
-
-    c = lanes(t, TC)
-    g = gsf[...] + dot_nt(dq[...], wq[...]) + dot_nt(dk[...], wk[...]) + dot_nt(dv[...], wv[...])
-    tg[...] = g.astype(BF16)
-    sums[0:1, :] = colsum(dq[:, c].astype(F32))
-    sums[1:2, :] = colsum(dv[:, c].astype(F32))
-    for a, o in ((dq, dwq), (dk, dwk), (dv, dwv)):
-        o[...] = dot(xt[...], a[:, c]).astype(BF16)
-
-
-def in_bwd_call(x, gsf, dq, dk, dv, wq, wk, wv):
-    rows, d = x.shape
-    col = pl.BlockSpec((rows, TC), lambda t: (0, t))
-    wcol = pl.BlockSpec((d, TC), lambda t: (0, t))
-    return pl.pallas_call(
-        in_bwd_kernel,
-        grid=(d // TC,),
-        in_specs=[single((rows, d)), col] + [single((rows, d))] * 3 + [pl.BlockSpec((TC, d), lambda t: (t, 0))] * 3,
-        out_specs=[col] + [wcol] * 3 + [pl.BlockSpec((8, TC), lambda t: (0, t))],
-        out_shape=[jax.ShapeDtypeStruct((rows, d), BF16)] + [jax.ShapeDtypeStruct((d, d), BF16)] * 3
-        + [jax.ShapeDtypeStruct((8, d), F32)],
-        scratch_shapes=[pltpu.VMEM((d, rows), BF16)],
-        compiler_params=params(),
-        cost_estimate=cost(12 * rows * d * d, rows * d * 14 + 12 * d * d),
-        name="in_bwd",
-    )(x, gsf, dq, dk, dv, wq, wk, wv)
 
 
 def grid_of(n):
@@ -611,30 +503,24 @@
     return (nz - 1) + 2 * (ny - 1) + 2 * (nx - 1) + 1
 
 
-def landing(n, r, cols, dtype):
+def reduce_buffers(n, r, cols, dtype):
     nz, ny, nx = grid_of(n)
     h = cols // 2
     return [pltpu.VMEM((nz, ny, nx, r, cols), dtype),
             pltpu.VMEM((max(nx - 1, 1), nz, ny, r, h), dtype), pltpu.VMEM((max(ny - 1, 1), nz, nx, r, h), dtype),
             pltpu.VMEM((max(ny - 1, 1), nz, r, h), dtype), pltpu.VMEM((max(nx - 1, 1), nz, r, h), dtype),
-            pltpu.VMEM((max(nz - 1, 1), r, cols), dtype)]
-
-
-def partial(n, r, cols, dtype):
-    nz, ny, nx = grid_of(n)
-    h = cols // 2
-    return [pltpu.VMEM((nz, ny, nx, r, cols), dtype), pltpu.VMEM((nz, ny, r, h), dtype), pltpu.VMEM((nz, nx, r, h), dtype),
-            pltpu.VMEM((nz, r, cols), dtype), pltpu.VMEM((r, cols), F32)]
+            pltpu.VMEM((max(nz - 1, 1), r, cols), dtype), pltpu.VMEM((nz, r, cols), dtype), pltpu.VMEM((r, cols), F32)]
 
 
 class Reduce:
-    def __init__(self, place, src, land, part, out, ssem, rsem, lsem, index):
-        self.p, self.src, self.land, self.part, self.out = place, src, land, part, out
+    def __init__(self, place, src, own, bufs, out, ssem, rsem, lsem, index):
+        self.p, self.src, self.own, self.bufs = place, src, own, bufs
         p = place
-        self.h = part[3].shape[-1] // 2
+        self.h = bufs[1].shape[-1]
         self.ca, self.cb = pl.ds(0, self.h), pl.ds(self.h, self.h)
-        self.get = pltpu.make_async_copy(src.at[:, :, :, p.c], part[0], lsem.at[index, 0])
-        self.put = pltpu.make_async_copy(part[4], out, lsem.at[index, 1])
+        if own is not None:
+            self.get = pltpu.make_async_copy(src.at[:, :, :, p.c], own, lsem.at[index, 0])
+        self.put = pltpu.make_async_copy(bufs[7], out, lsem.at[index, 1])
         slot = 0
 
         def copy(s, d, dev):
@@ -646,68 +532,72 @@
 
         self.ph = [[], [], [], []]
         dev, oc = p.at("c", 1)
-        self.ph[0].append(copy(src.at[:, :, :, oc], land[0], dev))
+        self.ph[0].append(copy(src.at[:, :, :, oc], bufs[0], dev))
         for k in p.steps("x"):
             dev, o = p.at("x", k)
-            self.ph[1].append(copy(part[0].at[:, :, o, :, self.ca], land[1].at[k - 1], dev))
+            self.ph[1].append(copy(bufs[0].at[:, :, o, :, self.ca], bufs[1].at[k - 1], dev))
         for k in p.steps("y"):
             dev, o = p.at("y", k)
-            self.ph[1].append(copy(part[0].at[:, o, :, :, self.cb], land[2].at[k - 1], dev))
+            self.ph[1].append(copy(bufs[0].at[:, o, :, :, self.cb], bufs[2].at[k - 1], dev))
         for k in p.steps("y"):
             dev, o = p.at("y", k)
-            self.ph[2].append(copy(part[1].at[:, o], land[3].at[k - 1], dev))
+            self.ph[2].append(copy(bufs[1].at[0, :, o], bufs[3].at[k - 1], dev))
         for k in p.steps("x"):
             dev, o = p.at("x", k)
-            self.ph[2].append(copy(part[2].at[:, o], land[4].at[k - 1], dev))
+            self.ph[2].append(copy(bufs[2].at[0, :, o], bufs[4].at[k - 1], dev))
         for k in p.steps("z"):
             dev, o = p.at("z", k)
-            self.ph[3].append(copy(part[3].at[o], land[5].at[k - 1], dev))
+            self.ph[3].append(copy(bufs[6].at[o], bufs[5].at[k - 1], dev))
 
     def begin(self):
-        self.get.start()
         self.ph[0][0].start()
+        if self.own is not None:
+            self.get.start()
 
     def go(self, i):
-        p, land, part = self.p, self.land, self.part
+        p, bufs = self.p, self.bufs
         nz, ny, nx = p.size
-        dt = part[0].dtype
+        dt = bufs[0].dtype
         for cp in self.ph[i - 1]:
             cp.wait_recv()
         if i == 1:
-            self.get.wait()
+            self.ph[0][0].wait_send()
+            if self.own is not None:
+                self.get.wait()
 
             def add(z, c):
-                part[0][z] = (part[0][z].astype(F32) + land[0][z].astype(F32)).astype(dt)
+                mine = self.own[z] if self.own is not None else self.src[z, :, :, pl.ds(p.c, 1)][:, :, 0]
+                bufs[0][z] = (mine.astype(F32) + bufs[0][z].astype(F32)).astype(dt)
                 return c
 
             lax.fori_loop(0, nz, add, 0)
         elif i == 2:
             def add(z, c):
-                a = part[0][z, :, pl.ds(p.x, 1), :, self.ca].astype(F32)[:, 0]
+                a = bufs[0][z, :, pl.ds(p.x, 1), :, self.ca].astype(F32)[:, 0]
                 for k in range(nx - 1):
-                    a += land[1][k, z].astype(F32)
-                part[1][z] = a.astype(dt)
-                b = part[0][z, pl.ds(p.y, 1), :, :, self.cb].astype(F32)[0]
+                    a += bufs[1][k, z].astype(F32)
+                bufs[1][0, z] = a.astype(dt)
+                b = bufs[0][z, pl.ds(p.y, 1), :, :, self.cb].astype(F32)[0]
                 for k in range(ny - 1):
-                    b += land[2][k, z].astype(F32)
-                part[2][z] = b.astype(dt)
+                    b += bufs[2][k, z].astype(F32)
+                bufs[2][0, z] = b.astype(dt)
                 return c
 
             lax.fori_loop(0, nz, add, 0)
         elif i == 3:
-            a = part[1][:, pl.ds(p.y, 1)].astype(F32)[:, 0]
+            a = bufs[1][0, :, pl.ds(p.y, 1)].astype(F32)[:, 0]
             for k in range(ny - 1):
-                a += land[3][k].astype(F32)
-            part[3][:, :, self.ca] = a.astype(dt)
-            b = part[2][:, pl.ds(p.x, 1)].astype(F32)[:, 0]
+                a += bufs[3][k].astype(F32)
+            bufs[6][:, :, self.ca] = a.astype(dt)
+            b = bufs[2][0, :, pl.ds(p.x, 1)].astype(F32)[:, 0]
             for k in range(nx - 1):
-                b += land[4][k].astype(F32)
-            part[3][:, :, self.cb] = b.astype(dt)
+                b += bufs[4][k].astype(F32)
+            bufs[6][:, :, self.cb] = b.astype(dt)
         else:
-            a = part[3][pl.ds(p.z, 1)].astype(F32)[0]
+            a = bufs[6][pl.ds(p.z, 1)].astype(F32)[0]
             for k in range(nz - 1):
-                a += land[5][k].astype(F32)
-            part[4][...] = a
+                a += bufs[5][k].astype(F32)
+            bufs[7][...] = a
             self.put.start()
             return
         for cp in self.ph[i]:
@@ -715,65 +605,271 @@
 
     def finish(self):
         self.put.wait()
-        for ph in self.ph:
+        for ph in self.ph[1:]:
             for cp in ph:
                 cp.wait_send()
 
 
-def reduce_kernel(n, plan, nsrc, *refs):
-    srcs, outs = refs[:nsrc], refs[nsrc:2 * nsrc]
-    scratch = refs[2 * nsrc:]
-    ssem, rsem, lsem = scratch[-3:]
+def run_at(t, events):
+    for step in sorted({e[0] for e in events}):
+        @pl.when(t == step)
+        def _():
+            for e in events:
+                if e[0] == step:
+                    e[1](*e[2:])
+
+
+EARLY = 3
+
+
+def bwd_kernel(n, nu, nc, nr, gd, lowt, hidt, dg, wd, wu, gs, xhat, r1, vec, gsf, ga, sums, sumu, dwd3, dwu3, rd, ru, gu, bufd, bufu, *rest):
+    t = pl.program_id(0)
+    d, rows = lowt.shape
+    ssem, rsem, lsem, wsem = rest[-4:]
     p = Place(n)
-    enter(p.peers())
+    r = d // n
     red = []
-    for i, (a, (r0, nr), (c0, nc)) in enumerate(plan):
-        land, part = scratch[11 * i:11 * i + 6], scratch[11 * i + 6:11 * i + 11]
-        rs, cs = pl.ds(r0, nr), pl.ds(c0, nc)
-        red.append(Reduce(p, srcs[a].at[:, :, :, :, rs, cs], land, part, outs[a].at[rs, cs], ssem, rsem, lsem, i))
-    for s in range(len(red) + 5):
-        for ph in (0, 1, 2, 3, 4, 5):
-            i = s - ph
-            if 0 <= i < len(red):
-                if ph == 0:
-                    red[i].begin()
-                elif ph < 5:
-                    red[i].go(ph)
-                else:
-                    red[i].finish()
-
-
-def reduce_call(n, grads, d):
-    views = [g.reshape(grid_of(n) + (2, g.shape[0] // n) + g.shape[1:]) for g in grads]
-    plan = gather_plan([jax.ShapeDtypeStruct(v.shape[4:], v.dtype) for v in views], d)
+    for i in range(2 * EARLY):
+        j = i // 2
+        out = rd.at[pl.ds(j * r, r), :] if i % 2 == 0 else ru.at[:, pl.ds(j * d, d)]
+        red.append(Reduce(p, (bufd, bufu)[i % 2], None, rest[8 * i:8 * i + 8], out, ssem, rsem, lsem, i))
+    late = [pltpu.make_async_copy(bufd, dwd3, wsem.at[0]), pltpu.make_async_copy(bufu, dwu3, wsem.at[1])]
+
+    @pl.when(t == 0)
+    def _():
+        enter(p.peers())
+
+    @pl.when(t < nu)
+    def _():
+        for j in range(TF // TC):
+            c = slice(j * TC, (j + 1) * TC)
+            g = (dot_nt(gd[...], wd[c, :]) * dg[:, c].astype(F32)).astype(BF16)
+            gu[:, lanes(t * (TF // TC) + j, TC)] = g
+            sumu[:, c] = colsum(g.astype(F32))
+
+    mid = []
+    for j in range(EARLY):
+        mid += [(2 * j + 2, red[2 * j].go, 1), (2 * j + 2, red[2 * j + 1].go, 1)]
+        if j > 0:
+            mid += [(2 * j + 2, red[2 * j - 1].go, 2)]
+        if j > 1:
+            mid += [(2 * j + 2, red[2 * j - 3].go, 4)]
+    run_at(t, mid)
+
+    @pl.when(t < nu)
+    def _():
+        half = lax.rem(t, d // TF)
+        for j in range(TF // TC):
+            c = lanes(half * (TF // TC) + j, TC)
+            bufu[..., c] = dot(lowt[...], gu[:, lanes(t * (TF // TC) + j, TC)]).astype(BF16).reshape(bufu.shape[:-1] + (TC,))
+            bufd[..., c] = dot(hidt[...].reshape(d, rows), gd[:, c]).astype(BF16).reshape(bufd.shape[:-1] + (TC,))
+
+    @pl.when((t >= nu) & (t < nu + nc))
+    def _():
+        gsf[:, lanes(t - nu, TC)] = gs[...] + dot_nt(gu[...], wu[...])
+
+    @pl.when(t == nu + nc)
+    def _():
+        sums[...] = jnp.zeros_like(sums)
+
+    @pl.when(t >= nu + nc)
+    def _():
+        at = lanes(t - nu - nc, RC)
+        gf = gsf[at, :]
+        nn = xhat[...]
+        sums[0:1, :] += colsum(gf * nn)
+        sums[1:2, :] += colsum(gf)
+        grad = norm_back(gf * vec[4:5, :], nn, r1[:, 0:1])
+        gsf[at, :] = grad
+        low_g = grad.astype(BF16)
+        ga[...] = low_g
+        sums[2:3, :] += colsum(low_g.astype(F32))
+
+    end = []
+    for j in range(EARLY):
+        s = 2 * j + 1
+        end += [(s, red[2 * j].begin), (s, red[2 * j + 1].begin)]
+    end += [(3, red[0].go, 2), (4, red[0].go, 3), (5, red[1].go, 3), (5, red[2].go, 2), (5, red[0].go, 4)]
+    end += [(6, red[2].go, 3), (7, late[0].start), (7, late[1].start), (7, red[3].go, 3), (7, red[4].go, 2), (8, red[2].go, 4),
+            (8, red[5].go, 2), (9, red[4].go, 3), (9, red[3].go, 4), (10, red[5].go, 3), (12, red[4].go, 4)]
+    last = nu + nc + nr - 1
+    end += [(last, red[5].go, 4)] + [(last, c.wait) for c in late] + [(last, c.finish) for c in red]
+    run_at(t, end)
+
+
+def bwd_call(n, gd, lowt, hidt, dg, wd, wu, gs, xhat, r1, vec):
+    d, rows = lowt.shape
+    ff = wu.shape[1]
+    nu, nc, nr = ff // TF, d // TC, rows // RC
+    r = d // n
+    parts = ff // d
+    z = grid_of(n) + (2, r)
+    per = d // TF
+    chunk = jax.ShapeDtypeStruct(z + (d,), BF16)
     k = reduce_slots(n)
-    scratch = []
-    for a, r, c in plan:
-        scratch += landing(n, r[1], c[1], grads[a].dtype) + partial(n, r[1], c[1], grads[a].dtype)
+    scratch = [pltpu.VMEM((rows, ff), BF16), pltpu.VMEM(z + (d,), BF16), pltpu.VMEM(z + (d,), BF16)]
+    for i in range(2 * EARLY):
+        scratch += reduce_buffers(n, r, d, BF16)
+    scratch += [pltpu.SemaphoreType.DMA((2 * EARLY, k)), pltpu.SemaphoreType.DMA((2 * EARLY, k)), pltpu.SemaphoreType.DMA((2 * EARLY, 2)),
+                pltpu.SemaphoreType.DMA((2,))]
     return pl.pallas_call(
-        functools.partial(reduce_kernel, n, plan, len(grads)),
-        in_specs=[ANY] * len(grads),
-        out_specs=[ANY] * len(grads),
-        out_shape=[jax.ShapeDtypeStruct(v.shape[4:], F32) for v in views],
-        scratch_shapes=scratch + [pltpu.SemaphoreType.DMA((len(plan), k)), pltpu.SemaphoreType.DMA((len(plan), k)),
-                                  pltpu.SemaphoreType.DMA((len(plan), 2))],
-        compiler_params=pltpu.CompilerParams(collective_id=2, has_side_effects=True, vmem_limit_bytes=60 << 20),
-        name="reduce",
-    )(*views)
-
-
-def hand_on_kernel(*refs):
-    half = len(refs) // 2
-    for a, b in zip(refs[:half], refs[half:]):
+        functools.partial(bwd_kernel, n, nu, nc, nr),
+        grid=(nu + nc + nr,),
+        in_specs=[single(gd.shape), single(lowt.shape),
+                  pl.BlockSpec((n, 1, r, rows), lambda t: (0, clip(t, 0, nu) // per, 0, 0)),
+                  pl.BlockSpec((rows, TF), lambda t: (0, clip(t, 0, nu))), pl.BlockSpec((TF, d), lambda t: (clip(t, 0, nu), 0)),
+                  pl.BlockSpec((TC, ff), lambda t: (clip(t, nu, nc), 0)), pl.BlockSpec((rows, TC), lambda t: (0, clip(t, nu, nc))),
+                  pl.BlockSpec((RC, d), lambda t: (clip(t, nu + nc, nr), 0)), pl.BlockSpec((RC, 128), lambda t: (clip(t, nu + nc, nr), 0)),
+                  single(vec.shape)],
+        out_specs=[single((rows, d)), pl.BlockSpec((RC, d), lambda t: (clip(t, nu + nc, nr), 0)), single((8, d)),
+                   pl.BlockSpec((1, TF), lambda t: (0, clip(t, 0, nu))), ANY, ANY, ANY, ANY],
+        out_shape=[jax.ShapeDtypeStruct((rows, d), F32), jax.ShapeDtypeStruct((rows, d), BF16), jax.ShapeDtypeStruct((8, d), F32),
+                   jax.ShapeDtypeStruct((1, ff), F32), chunk, chunk,
+                   jax.ShapeDtypeStruct((EARLY * r, d), F32), jax.ShapeDtypeStruct((r, EARLY * d), F32)],
+        scratch_shapes=scratch,
+        compiler_params=pltpu.CompilerParams(collective_id=3, has_side_effects=True, vmem_limit_bytes=60 << 20),
+        cost_estimate=cost(8 * rows * d * ff, 8 * d * ff + 4 * rows * ff + rows * d * 18),
+        name="bwd",
+    )(gd, lowt, hidt.reshape(n, parts, r, rows), dg, wd, wu, gs, xhat, r1, vec)
+
+
+def ctx_bwd_kernel(n, nc, ga, wo, ctxt, gc, dwo, gl, gr, ssem, rsem):
+    t = pl.program_id(0)
+    rows = ga.shape[0]
+    me = lax.axis_index("dp")
+    right, left = lax.rem(me + 1, n), lax.rem(me + n - 1, n)
+    copies = [pltpu.make_async_remote_copy(src_ref=gc.at[pl.ds(rows - HALO, HALO), :], dst_ref=gl, send_sem=ssem.at[0], recv_sem=rsem.at[0],
+                                           device_id=(right,), device_id_type=MESH),
+              pltpu.make_async_remote_copy(src_ref=gc.at[pl.ds(0, HALO), :], dst_ref=gr, send_sem=ssem.at[1], recv_sem=rsem.at[1],
+                                           device_id=(left,), device_id_type=MESH)]
+
+    @pl.when(t == 0)
+    def _():
+        enter([left, right])
+
+    @pl.when(t < nc)
+    def _():
+        gc[:, lanes(t, TC)] = dot_nt(ga[...], wo[...]).astype(BF16)
+
+    @pl.when(t == nc - 1)
+    def _():
+        for c in copies:
+            c.start()
+
+    @pl.when(t >= nc)
+    def _():
+        dwo[...] = dot(ctxt[...], ga[:, lanes(t - nc, TC)]).astype(BF16)
+
+    @pl.when(t == 2 * nc - 1)
+    def _():
+        for c in copies:
+            c.wait()
+
+
+def ctx_bwd_call(n, ga, wo, ctxt):
+    rows, d = ga.shape
+    nc = d // TC
+    edge = jax.ShapeDtypeStruct((HALO, d), BF16)
+    return pl.pallas_call(
+        functools.partial(ctx_bwd_kernel, n, nc),
+        grid=(2 * nc,),
+        in_specs=[single(ga.shape), pl.BlockSpec((TC, d), lambda t: (clip(t, 0, nc), 0)), single(ctxt.shape)],
+        out_specs=[single((rows, d)), pl.BlockSpec((d, TC), lambda t: (0, clip(t, nc, nc))), ANY, ANY],
+        out_shape=[jax.ShapeDtypeStruct((rows, d), BF16), jax.ShapeDtypeStruct((d, d), BF16), edge, edge],
+        scratch_shapes=[pltpu.SemaphoreType.DMA((2,)), pltpu.SemaphoreType.DMA((2,))],
+        compiler_params=pltpu.CompilerParams(collective_id=4, has_side_effects=True, vmem_limit_bytes=40 << 20),
+        cost_estimate=cost(4 * rows * d * d, rows * d * 8 + 4 * d * d),
+        name="ctx_bwd",
+    )(ga, wo, ctxt)
+
+
+def in_bwd_kernel(n, nc, x, gsf, dq, dk, dv, wq, wk, wv, sd, su, so, sv, tg, rd, ru, ro, rv, rq, rk, rw, xt, bq, bk, bv, od, ou, oo, ov, *rest):
+    t = pl.program_id(0)
+    ssem, rsem, lsem = rest[-3:]
+    p = Place(n)
+    plan = [(sd, od, rd), (su, ou, ru), (so, oo, ro), (bq, None, rq), (bk, None, rk), (bv, None, rw), (sv, ov, rv)]
+    red = [Reduce(p, s, o, rest[8 * i:8 * i + 8], out, ssem, rsem, lsem, i) for i, (s, o, out) in enumerate(plan)]
+
+    @pl.when(t == 0)
+    def _():
+        enter(p.peers())
+
+    start = [(0, red[i].begin) for i in (0, 1, 2, 6)]
+    run_at(t, start)
+
+    @pl.when(t == 0)
+    def _():
+        xt[...] = x[...].T
+
+    for i, (a, b) in enumerate(((dq, bq), (dk, bk), (dv, bv))):
+        @pl.when((t >= i * nc) & (t < (i + 1) * nc))
+        def _():
+            c = lanes(t - i * nc, TC)
+            b[..., c] = dot(xt[...], a[:, c]).astype(BF16).reshape(b.shape[:-1] + (TC,))
+
+    @pl.when(t >= 3 * nc)
+    def _():
+        g = gsf[...] + dot_nt(dq[...], wq[...]) + dot_nt(dk[...], wk[...]) + dot_nt(dv[...], wv[...])
+        tg[...] = g.astype(BF16)
+
+    a, b, o, q, k, v, s = red
+    end = [(0, a.go, 1), (1, b.go, 1), (2, o.go, 1), (3, q.begin), (5, q.go, 1), (6, a.go, 2), (7, k.begin), (8, s.go, 1), (9, k.go, 1), (10, b.go, 2),
+           (11, v.begin), (12, a.go, 3), (13, v.go, 1), (14, o.go, 2)]
+    last = 4 * nc - 1
+    end += [(last, s.go, 2), (last, b.go, 3), (last, a.go, 4), (last, q.go, 2), (last, o.go, 3), (last, k.go, 2), (last, b.go, 4), (last, q.go, 3),
+            (last, s.go, 3), (last, v.go, 2), (last, o.go, 4), (last, k.go, 3), (last, q.go, 4), (last, v.go, 3), (last, s.go, 4), (last, k.go, 4),
+            (last, v.go, 4)]
+    end += [(last, c.finish) for c in red]
+    run_at(t, end)
+
+
+def in_bwd_call(n, x, gsf, dq, dk, dv, wq, wk, wv, dwd3, dwu3, dwo, small):
+    rows, d = x.shape
+    nc = d // TC
+    r = d // n
+    z = grid_of(n)
+    col = pl.BlockSpec((rows, TC), lambda t: (0, clip(t, 3 * nc, nc)))
+    wrow = pl.BlockSpec((TC, d), lambda t: (clip(t, 3 * nc, nc), 0))
+    chunk = pltpu.VMEM(z + (2, r, d), BF16)
+    own = pltpu.VMEM(z + (r, d), BF16)
+    share = jax.ShapeDtypeStruct((r, d), F32)
+    sr, sc = small.shape[0] // n, small.shape[1]
+    k = reduce_slots(n)
+    scratch = [pltpu.VMEM((d, rows), BF16)] + [chunk] * 3 + [own] * 3 + [pltpu.VMEM(z + (sr, sc), F32)]
+    for i in range(6):
+        scratch += reduce_buffers(n, r, d, BF16)
+    scratch += reduce_buffers(n, sr, sc, F32)
+    scratch += [pltpu.SemaphoreType.DMA((7, k)), pltpu.SemaphoreType.DMA((7, k)), pltpu.SemaphoreType.DMA((7, 2))]
+    return pl.pallas_call(
+        functools.partial(in_bwd_kernel, n, nc),
+        grid=(4 * nc,),
+        in_specs=[single((rows, d)), col] + [single((rows, d))] * 3 + [wrow] * 3 + [ANY] * 4,
+        out_specs=[col] + [ANY] * 7,
+        out_shape=[jax.ShapeDtypeStruct((rows, d), BF16), share, share, share, jax.ShapeDtypeStruct((sr, sc), F32), share, share, share],
+        scratch_shapes=scratch,
+        compiler_params=pltpu.CompilerParams(collective_id=5, has_side_effects=True, vmem_limit_bytes=60 << 20),
+        cost_estimate=cost(12 * rows * d * d, rows * d * 14 + 12 * d * d),
+        name="in_bwd",
+    )(x, gsf, dq, dk, dv, wq, wk, wv, dwd3, dwu3, dwo.reshape(z + (2, r, d)), small.reshape(z + (2, sr, sc)))
+
+
+def hand_on_kernel(q, k, v, o, ua, ub, da, db, qo, ko, vo, oo, u, d):
+    for a, b in ((q, qo), (k, ko), (v, vo), (o, oo)):
         b[...] = a[...]
-
-
-def hand_on(arrays):
+    u[:, : ua.shape[1]] = ua[...]
+    u[:, ua.shape[1]:] = ub[...]
+    d[: da.shape[0], :] = da[...]
+    d[da.shape[0]:, :] = db[...]
+
+
+def hand_on(q, k, v, o, ua, ub, da, db):
+    r, d = q.shape
     return pl.pallas_call(
         hand_on_kernel,
-        out_shape=[jax.ShapeDtypeStruct(a.shape, a.dtype) for a in arrays],
+        out_shape=[jax.ShapeDtypeStruct((r, d), F32)] * 4
+        + [jax.ShapeDtypeStruct((r, ua.shape[1] + ub.shape[1]), F32), jax.ShapeDtypeStruct((da.shape[0] + db.shape[0], d), F32)],
         name="hand_on",
-    )(*arrays)
+    )(q, k, v, o, ua, ub, da, db)
 
 
 def sequence_table(lengths, own, rows):
@@ -786,12 +882,6 @@
     length = jnp.sum(jnp.where(inside, lengths[None, :], 0), axis=1)
     lead = (first == at) | (jnp.arange(blocks) == 0)
     return jnp.stack([(first - own * rows + HALO) // GRAN, jnp.where(lead, length // GRAN, 0)]).astype(jnp.int32)
-
-
-def halo(x, n):
-    right = [(i, i + 1) for i in range(n - 1)]
-    left = [(i + 1, i) for i in range(n - 1)]
-    return lax.ppermute(x[-HALO:], "dp", right), lax.ppermute(x[:HALO], "dp", left)
 
 
 def pack(values, n, rows, dtype):
@@ -818,14 +908,13 @@
     tab = sequence_table(lengths, own, rows)
     q, k, v = qkv_call(xl, tokens, xr, wq, wk, wv, vec)
     ctx, lse = attn_fwd_call(tab, q, k, v, rows)
-    xhat, low, r1, hidt, dg, layer_out, gs, sums2 = fwd_call(ctx, wo, tokens, wu, bu, wd, cotangent, vec)
-    dwd, dwu, gsf, sums1, sumu, gc, dwo = bwd_call(low, gs, hidt, dg, wu, wd, xhat, r1, ctx, wo, vec)
-    gl, gr = halo(gc, n)
-    dq, dk, dv = attn_bwd_call(tab, q, k, v, lse, gl, gc, gr)
-    tg, dwq, dwk, dwv, sums0 = in_bwd_call(tokens, gsf, dq, dk, dv, wq, wk, wv)
+    xhat, lowt, ctxt, r1, hidt, dg, layer_out, gs, gd, sums2 = fwd_call(ctx, wo, tokens, wu, bu, wd, cotangent, vec)
+    gsf, ga, sums1, sumu, dwd3, dwu3, rd, ru = bwd_call(n, gd, lowt, hidt, dg, wd, wu, gs, xhat, r1, vec)
+    gc, dwo, gl, gr = ctx_bwd_call(n, ga, wo, ctxt)
+    dq, dk, dv, sums0 = attn_bwd_call(tab, q, k, v, lse, gl, gc, gr)
     small = pack([sums0[0], sums0[1], sums1[2], sums2[2], sums1[0], sums1[1], sums2[0], sums2[1], sumu], n, 8, F32)
-    tiny, gd, gu, go, gq, gk, gv = reduce_call(n, [small, dwd, dwu, dwo, dwq, dwk, dwv], d)
-    gq, gk, gv, go, gu, gd = hand_on([gq, gk, gv, go, gu, gd])
+    tg, rd3, ru3, go, tiny, gq, gk, gv = in_bwd_call(n, tokens, gsf, dq, dk, dv, wq, wk, wv, dwd3, dwu3, dwo, small)
+    gq, gk, gv, go, gu, gd = hand_on(gq, gk, gv, go, ru, ru3, rd, rd3)
     vecs, ubg = unpack(tiny, 1, part)
     t = [vecs[i] for i in range(8)]
     return (layer_out, tg, gq, gk, gv, go, gu, gd, t[0], t[1], t[2], ubg[0], t[3], t[4], t[5], t[6], t[7])

time: 515 us -> 476 us (0.924)
  Pallas kernels: 487 us -> 448 us
  starting transfers between devices: 9.36 us -> 0 us
  local copies, waits for them, and re-layouts: 11.5 us -> 19.8 us
    pallas_call x4, Pallas kernels: 259 us -> 212 us  [the longest x1 97.4 us: in_bwd_call(): pl.pallas_call(functools.partial(in_bwd_kernel, n, nc), grid=(4 * nc,), i...]
    unnamed x11 -> x20, local copies, waits for them, and re-layouts: 3.42 us -> 13.2 us
    ppermute x2 -> x0, starting transfers between devices: 9.36 us -> none  [the longest x1 8.07 us: halo(): lax.ppermute(x[-HALO:], 'dp', right)]
  transfers between devices with their start and end apart: 2 -> 0, of which waited for: 1 -> 0; matrix products, arithmetic and copies ran while one was open for 0% -> 0% of each run, Pallas kernels for 0% -> 0%
where the time goes in v4:
time: 476 us; the launch traced here: 472 us
  Pallas kernels  448 us (94%)
  local copies, waits for them, and re-layouts  19.8 us (4%)
    pallas_call x1, Pallas kernels, gather_call(): pl.pallas_call(functools.partial(gather_kernel, n, plan, len(shards)), in...  131 us
    pallas_call x1, Pallas kernels, in_bwd_call(): pl.pallas_call(functools.partial(in_bwd_kernel, n, nc), grid=(4 * nc,), i...  97.4 us
    pallas_call x1, Pallas kernels, bwd_call(): pl.pallas_call(functools.partial(bwd_kernel, n, nu, nc, nr), grid=(nu + n...  94 us
    pallas_call x1, Pallas kernels, fwd_call(): pl.pallas_call(functools.partial(fwd_kernel, nu, nc), grid=(2 * nc + nu,)...  49 us
    pallas_call x1, Pallas kernels, attn_bwd_call(): pl.pallas_call(attn_bwd_kernel, grid_spec=pltpu.PrefetchScalarGridSpec(nu...  22.3 us
    pallas_call x1, Pallas kernels, ctx_bwd_call(): pl.pallas_call(functools.partial(ctx_bwd_kernel, n, nc), grid=(2 * nc,),...  18.3 us
    pallas_call x1, Pallas kernels, attn_fwd_call(): pl.pallas_call(attn_fwd_kernel, grid_spec=pltpu.PrefetchScalarGridSpec(nu...  16.8 us
    pallas_call x1, Pallas kernels, qkv_call(): pl.pallas_call(qkv_kernel, grid=(d // tn,), in_specs=[whole(xl.shape), wh...  16.7 us

profile of v4, /device:TPU:0, one launch (start us, length us, event | category | flops | bytes accessed | tf_op | source)
XLA Modules:
  0.0 471.6 jit_solution(6725509663970532658)
XLA Ops:
  0.7 0.8 select_reduce_fusion
  2.1 0.9 select_reduce_fusion.2
  3.6 0.9 concatenate.6
  5.2 131.0 %gather.1 = (bf16[4,2,2,2,16,256]{5,4,3,2,1,0:T(8,128)(2,1)}, bf16[4,2,2,2,32,1024]{5,4,3,2,1,0:T(8,128)(2,1)}, bf16[4,2,2,2,32,1024]{5,4,3,2,1,0:T(8,128)(2,1)}...) custom-call(bf16[16,256]{1,0:T(8,128)(2,1)} %reshape.275.refs_0_, ...), custom_call_target="tpu_custom_call" | custom-call | tf_op jit(solution)/shard_map/gather/pallas_call | solution.py:488
  136.2 1.0 copy.37
  138.0 0.7 reshape.280.vec
  138.7 16.7 %qkv.1 = (bf16[1792,1024]{1,0:T(8,128)(2,1)}, bf16[1792,1024]{1,0:T(8,128)(2,1)}, bf16[1792,1024]{1,0:T(8,128)(2,1)}) custom-call(bf16[384,1024]{1,0:T(8,128)(2,1)} %get-tuple-element.71.xl, bf16[1024,1024]{1,0:T(8,128)(2,1)} %x.7, bf16[384,1024]{1,0:T(8,128)(2,1)} %get-tuple-element.72.xr, bf16[1024,1024]{1,0:T(8,128)(2,1)} %bitcast.90, ...), custom_call_target="tpu_custom_call" | custom-call | flops 11274289152 | bytes 20971520 | tf_op jit(solution)/shard_map/qkv/pallas_call | solution.py:62
  155.3 16.8 %attn_fwd.1 = (bf16[1024,1024]{1,0:T(8,128)(2,1)}, f32[16,1792]{1,0:T(8,128)}) custom-call(s32[2,8]{1,0:T(2,128)} %pad_add_fusion.tab, bf16[1792,1024]{1,0:T(8,128)(2,1)} %get-tuple-element.77.q_ref, bf16[1792,1024]{1,0:T(8,128)(2,1)} %get-tuple-element.78.k_ref, bf16[1792,1024]{1,0:T(8,128)(2,1)} %get-tuple-element.79.v_ref), custom_call_target="tpu_custom_call" | custom-call | flops 4294967296 | bytes 14680064 | tf_op jit(solution)/shard_map/attn_fwd/pallas_call | solution.py:136
  172.2 49.0 %fwd.1 = (f32[1024,1024]{1,0:T(8,128)}, bf16[1024,1024]{1,0:T(8,128)(2,1)}, bf16[1024,1024]{1,0:T(8,128)(2,1)}, f32[1024,128]{1,0:T(8,128)}, bf16[4096,1024]{1,0...) custom-call(bf16[1024,1024]{1,0:T(8,128)(2,1)} %get-tuple-element.80, ...), custom_call_target="tpu_custom_call" | custom-call | flops 17179869184 | bytes 48234496 | tf_op jit(solution)/shard_map/fwd/pallas_call | solution.py:318
  221.2 94.0 %bwd.1 = (f32[1024,1024]{1,0:T(8,128)}, bf16[1024,1024]{1,0:T(8,128)(2,1)}, f32[8,1024]{1,0:T(8,128)}, f32[1,4096]{1,0:T(1,128)}, bf16[4,2,2,2,32,1024]{5,4,3,2,...) custom-call(bf16[1024,1024]{1,0:T(8,128)(2,1)} %get-tuple-element.85.gd, ...), custom_call_target="tpu_custom_call" | custom-call | flops 34359738368 | bytes 69206016 | tf_op jit(solution)/shard_map/bwd/pallas_call | solution.py:715
  315.2 0.9 slice_reduce_fusion
  316.5 1.6 copy-done.2
  318.1 1.6 copy-done.3
  319.7 18.3 %ctx_bwd.1 = (bf16[1024,1024]{1,0:T(8,128)(2,1)S(1)}, bf16[1024,1024]{1,0:T(8,128)(2,1)S(1)}, bf16[384,1024]{1,0:T(8,128)(2,1)S(1)}, bf16[384,1024]{1,0:T(8,128)(2,1)S(1)}) custom-call(bf16[1024,1024]{1,0:T(8,128)(2,1)S(1)} %copy-done.3, bf16[1024,1024]{1,0:T(8,128)(2,1)S(1)} %bitcast.64, bf16[1024,1024]{1,0:T(8,128)(2,1)S(1)} %copy-done.2), custom_call_target="tpu_custom_call" | custom-call | flops 4294967296 | bytes 12582912 | tf_op jit(solution)/shard_map/ctx_bwd/pallas_call | solution.py:773
  338.1 1.3 copy-done.1
  339.4 1.3 copy-done.4
  340.7 0.9 copy-done.5
  341.6 0.9 copy-done.6
  342.5 22.3 %attn_bwd.1 = (bf16[1024,1024]{1,0:T(8,128)(2,1)}, bf16[1024,1024]{1,0:T(8,128)(2,1)}, bf16[1024,1024]{1,0:T(8,128)(2,1)}, f32[8,1024]{1,0:T(8,128)}) custom-call(s32[2,8]{1,0:T(2,128)} %pad_add_fusion.tab, bf16[1792,1024]{1,0:T(8,128)(2,1)} %get-tuple-element.77.q_ref, bf16[1792,1024]{1,0:T(8,128)(2,1)} %get-tuple-element.78.k_ref, ...), custom_call_target="tpu_custom_call" | custom-call | flops 10737418240 | bytes 25690112 | tf_op jit(solution)/shard_map/attn_bwd/pallas_call | solution.py:197
  364.8 0.9 slice_reduce_fusion.6
  365.9 0.8 copy.38
  366.7 97.4 %in_bwd.1 = (bf16[1024,1024]{1,0:T(8,128)(2,1)}, f32[32,1024]{1,0:T(8,128)}, f32[32,1024]{1,0:T(8,128)}, f32[32,1024]{1,0:T(8,128)}, f32[8,256]{1,0:T(8,128)}, /...) custom-call(bf16[1024,1024]{1,0:T(8,128)(2,1)} %x.7, f32[1024,1024]{1,0:T(8,128)} %get-tuple-element.92.gsf, ...), custom_call_target="tpu_custom_call" | custom-call | flops 12884901888 | bytes 27262976 | tf_op jit(solution)/shard_map/in_bwd/pallas_call | solution.py:843
  465.9 2.6 hand_on.1
  468.5 3.1 copy.41
  (33 shorter events, 5.2 us)
Async XLA Ops:
  221.1 95.4 %copy-start = (bf16[4,2,2,2,32,1024]{5,4,3,2,1,0:T(8,128)(2,1)S(1)}, bf16[4,2,2,2,32,1024]{5,4,3,2,1,0:T(8,128)(2,1)}, u32[]{:S(2)}) copy-start(bf16[4,2,2,2,32,1024]{5,4,3,2,1,0:T(8,128)(2,1)} %get-tuple-element.81) | copy-start | bytes 6291460
  316.5 1.6 copy-start.2
  318.1 1.6 copy-start.3
  338.1 1.3 copy-start.1
  339.4 1.3 copy-start.4
  340.7 0.9 copy-start.5
  341.6 0.9 copy-start.6
  342.5 23.3 %copy-start.7 = (f32[1,4096]{1,0:T(1,128)S(1)}, f32[1,4096]{1,0:T(1,128)}, u32[]{:S(2)}) copy-start(f32[1,4096]{1,0:T(1,128)} %get-tuple-element.108) | copy-start | bytes 49156

commit v5 on v4

--- a/solution.py
+++ b/solution.py
@@ -36,41 +36,6 @@
 
 def cost(flops, nbytes, trans=0):
     return pl.CostEstimate(flops=flops, bytes_accessed=nbytes, transcendentals=trans)
-
-
-def qkv_kernel(xl, xo, xr, wq, wk, wv, vec, q, k, v, x):
-    rows = xo.shape[0]
-
-    @pl.when(pl.program_id(0) == 0)
-    def _():
-        x[pl.ds(0, HALO), :] = xl[...]
-        x[pl.ds(HALO, rows), :] = xo[...]
-        x[pl.ds(HALO + rows, HALO), :] = xr[...]
-
-    q[...] = (dot(x[...], wq[...]) + vec[0:1, :]).astype(BF16)
-    k[...] = dot(x[...], wk[...]).astype(BF16)
-    v[...] = (dot(x[...], wv[...]) + vec[1:2, :]).astype(BF16)
-
-
-def qkv_call(xl, xo, xr, wq, wk, wv, vec):
-    rows, d = xo.shape
-    win = rows + 2 * HALO
-    tn = 256
-    wspec = pl.BlockSpec((d, tn), lambda j: (0, j))
-    ospec = pl.BlockSpec((win, tn), lambda j: (0, j))
-    out = jax.ShapeDtypeStruct((win, d), BF16)
-    return pl.pallas_call(
-        qkv_kernel,
-        grid=(d // tn,),
-        in_specs=[whole(xl.shape), whole(xo.shape), whole(xr.shape), wspec, wspec, wspec,
-                  pl.BlockSpec((8, tn), lambda j: (0, j))],
-        out_specs=[ospec] * 3,
-        out_shape=[out] * 3,
-        scratch_shapes=[pltpu.VMEM((win, d), BF16)],
-        compiler_params=params(),
-        cost_estimate=cost(6 * win * d * d, 2 * (4 * win * d + 3 * d * d)),
-        name="qkv",
-    )(xl, xo, xr, wq, wk, wv, vec)
 
 
 LANES = 512
@@ -250,89 +215,8 @@
     return u * phi, phi + u * (0.3989422804014327 * jnp.exp(-0.5 * u * u))
 
 
-def fwd_kernel(nu, nc, ctx, wo, x, wu, bu, wd, g, vec, xhat, lowt, ctxt, r1, hidt, dg, out, gs, gd, sums, z, hid, low):
-    t = pl.program_id(0)
-    rows = x.shape[0]
-
-    @pl.when(t < nc)
-    def _():
-        c = lanes(t, TC)
-        z[:, c] = dot(ctx[...], wo[...]) + x[:, c].astype(F32)
-
-    @pl.when(t == nc - 1)
-    def _():
-        def fin(r):
-            n, rr = norm_stats(z[r, :] + vec[2:3, :])
-            xhat[r, :] = n
-            r1[r, :] = jnp.broadcast_to(rr, (RC, r1.shape[1]))
-            v = (n * vec[4:5, :] + vec[5:6, :]).astype(BF16)
-            low[r, :] = v
-            lowt[:, r] = v.T
-            ctxt[:, r] = ctx[r, :].T
-
-        chunks(rows, fin)
-
-    @pl.when((t >= nc) & (t < nc + nu))
-    def _():
-        for j in range(TF // TC):
-            c = slice(j * TC, (j + 1) * TC)
-            h, s = gelu_parts(dot(low[...], wu[:, c]) + bu[:, c])
-            h = h.astype(BF16)
-            dg[:, c] = s.astype(BF16)
-            hid[:, lanes((t - nc) * (TF // TC) + j, TC)] = h
-            hidt[c, :] = h.T
-
-    @pl.when(t >= nc + nu)
-    def _():
-        c = lanes(t - nc - nu, TC)
-        z[:, c] = dot(hid[...], wd[...])
-
-    @pl.when(t == 2 * nc + nu - 1)
-    def _():
-        sums[...] = jnp.zeros_like(sums)
-
-        def fin(r):
-            v = (xhat[r, :] * vec[4:5, :] + vec[5:6, :]) + (z[r, :] + vec[3:4, :])
-            n, rr = norm_stats(v)
-            out[r, :] = (n * vec[6:7, :] + vec[7:8, :]).astype(BF16)
-            gv = g[r, :].astype(F32)
-            sums[0:1, :] += colsum(gv * n)
-            sums[1:2, :] += colsum(gv)
-            grad = norm_back(gv * vec[6:7, :], n, rr)
-            gs[r, :] = grad
-            low_g = grad.astype(BF16)
-            gd[r, :] = low_g
-            sums[2:3, :] += colsum(low_g.astype(F32))
-
-        chunks(rows, fin)
-
-
 def single(shape):
     return pl.BlockSpec(shape, lambda *_: (0,) * len(shape), pipeline_mode=pl.Buffered(1))
-
-
-def fwd_call(ctx, wo, x, wu, bu, wd, g, vec):
-    rows, d = x.shape
-    ff = wu.shape[1]
-    nu, nc = ff // TF, d // TC
-    return pl.pallas_call(
-        functools.partial(fwd_kernel, nu, nc),
-        grid=(2 * nc + nu,),
-        in_specs=[single(ctx.shape), pl.BlockSpec((d, TC), lambda t: (0, clip(t, 0, nc))), single(x.shape),
-                  pl.BlockSpec((d, TF), lambda t: (0, clip(t, nc, nu))), pl.BlockSpec((1, TF), lambda t: (0, clip(t, nc, nu))),
-                  pl.BlockSpec((ff, TC), lambda t: (0, clip(t, nc + nu, nc))), single(g.shape), single(vec.shape)],
-        out_specs=[single((rows, d)), single((d, rows)), single((d, rows)), single((rows, 128)),
-                   pl.BlockSpec((TF, rows), lambda t: (clip(t, nc, nu), 0)), pl.BlockSpec((rows, TF), lambda t: (0, clip(t, nc, nu))),
-                   single((rows, d)), single((rows, d)), single((rows, d)), single((8, d))],
-        out_shape=[jax.ShapeDtypeStruct((rows, d), F32), jax.ShapeDtypeStruct((d, rows), BF16), jax.ShapeDtypeStruct((d, rows), BF16),
-                   jax.ShapeDtypeStruct((rows, 128), F32), jax.ShapeDtypeStruct((ff, rows), BF16),
-                   jax.ShapeDtypeStruct((rows, ff), BF16), jax.ShapeDtypeStruct((rows, d), BF16),
-                   jax.ShapeDtypeStruct((rows, d), F32), jax.ShapeDtypeStruct((rows, d), BF16), jax.ShapeDtypeStruct((8, d), F32)],
-        scratch_shapes=[pltpu.VMEM((rows, d), F32), pltpu.VMEM((rows, ff), BF16), pltpu.VMEM((rows, d), BF16)],
-        compiler_params=params(60),
-        cost_estimate=cost(4 * rows * d * ff, 4 * d * ff + 4 * rows * ff + rows * d * 14, 2 * rows * ff),
-        name="fwd",
-    )(ctx, wo, x, wu, bu, wd, g, vec)
 
 
 def grid_of(n):
@@ -441,61 +325,11 @@
                 cp.wait_send()
 
 
-def gather_kernel(n, plan, nsrc, *refs):
-    srcs, xsrc, outs = refs[:nsrc], refs[nsrc], refs[nsrc + 1:2 * nsrc + 1]
-    xl, xr = refs[2 * nsrc + 1:2 * nsrc + 3]
-    ssem, rsem, lsem, hs, hr = refs[2 * nsrc+3:]
-    p = Place(n)
-    right, left = lax.rem(p.me + 1, n), lax.rem(p.me + n - 1, n)
-    enter(p.peers() + [left, right])
-    rows = xsrc.shape[0]
-    halo = [pltpu.make_async_remote_copy(src_ref=xsrc.at[pl.ds(rows-HALO,HALO),:], dst_ref=xl, send_sem=hs.at[0], recv_sem=hr.at[0], device_id=(right,), device_id_type=MESH),
-            pltpu.make_async_remote_copy(src_ref=xsrc.at[pl.ds(0,HALO),:], dst_ref=xr, send_sem=hs.at[1], recv_sem=hr.at[1], device_id=(left,), device_id_type=MESH)]
-    for h in halo: h.start()
-    g = [Gather(p, srcs[a], outs[a], r, c, ssem, rsem, lsem, i) for i, (a, r, c) in enumerate(plan)]
-    for s in range(len(g) + 4):
-        for ph in (0, 1, 2, 3, 4):
-            i = s - ph
-            if 0 <= i < len(g):
-                if ph > 0:
-                    g[i].wait(ph - 1)
-                if ph < 4:
-                    g[i].start(ph)
-    for c in g:
-        c.sent()
-    for h in halo: h.wait()
-
-
-def gather_plan(shards, d):
-    least = min(s.shape[0] for s in shards if s.shape[-1] >= d)
-    plan = []
-    for a, s in enumerate(shards):
-        if s.shape[1] < d:
-            plan.append((a, (0, s.shape[0]), (0, s.shape[1])))
-            continue
-        for j in range(s.shape[1] // d):
-            for i in range(s.shape[0] // least):
-                plan.append((a, (i * least, least), (j * d, d)))
-    return plan
-
-
-def gather_call(n, shards, tokens, order=None):
-    d = tokens.shape[1]
-    plan = gather_plan(shards, d)
-    k = gather_slots(n)
-    outs = [jax.ShapeDtypeStruct(grid_of(n) + (2,) + s.shape, s.dtype) for s in shards]
-    halo = jax.ShapeDtypeStruct((HALO, d), tokens.dtype)
-    res = pl.pallas_call(
-        functools.partial(gather_kernel, n, plan, len(shards)),
-        in_specs=[ANY] * (len(shards)+1),
-        out_specs=[ANY] * (len(shards)+2),
-        out_shape=outs+[halo,halo],
-        scratch_shapes=[pltpu.SemaphoreType.DMA((len(plan), k)), pltpu.SemaphoreType.DMA((len(plan), k)),
-                        pltpu.SemaphoreType.DMA((len(plan),)),pltpu.SemaphoreType.DMA((2,)),pltpu.SemaphoreType.DMA((2,))],
-        compiler_params=pltpu.CompilerParams(collective_id=1, has_side_effects=True),
-        name="gather",
-    )(*shards, tokens)
-    return [r.reshape((n * s.shape[0],) + s.shape[1:]) for r, s in zip(res, shards)] + list(res[-2:])
+def gather_go(g, ph):
+    if ph > 0:
+        g.wait(ph - 1)
+    if ph < 4:
+        g.start(ph)
 
 
 def reduce_slots(n):
@@ -549,15 +383,19 @@
             dev, o = p.at("z", k)
             self.ph[3].append(copy(bufs[6].at[o], bufs[5].at[k - 1], dev))
 
-    def begin(self):
-        self.ph[0][0].start()
-        if self.own is not None:
-            self.get.start()
-
     def go(self, i):
+        if i == 0:
+            self.ph[0][0].start()
+            if self.own is not None:
+                self.get.start()
+            return
         p, bufs = self.p, self.bufs
         nz, ny, nx = p.size
         dt = bufs[0].dtype
+        if i == 5:
+            for cp in self.ph[1]:
+                cp.start()
+            return
         for cp in self.ph[i - 1]:
             cp.wait_recv()
         if i == 1:
@@ -571,6 +409,7 @@
                 return c
 
             lax.fori_loop(0, nz, add, 0)
+            return
         elif i == 2:
             def add(z, c):
                 a = bufs[0][z, :, pl.ds(p.x, 1), :, self.ca].astype(F32)[:, 0]
@@ -619,25 +458,252 @@
                     e[1](*e[2:])
 
 
-EARLY = 3
-
-
-def bwd_kernel(n, nu, nc, nr, gd, lowt, hidt, dg, wd, wu, gs, xhat, r1, vec, gsf, ga, sums, sumu, dwd3, dwu3, rd, ru, gu, bufd, bufu, *rest):
+FIRST_PLAN = (
+    (0, 1, 0), (0, 1, 1), (0, 0, 0), (0, 2, 0), (0, 1, 2), (0, 0, 1), (0, 7, 0), (0, 0, 2),
+    (0, 6, 0), (0, 1, 3), (0, 2, 1), (0, 0, 3), (0, 7, 1), (0, 3, 0), (0, 2, 2), (0, 0, 4),
+    (0, 1, 4), (1, 8, 0), (1, 5, 0), (2, 6, 1), (3, 7, 2), (3, 3, 1), (3, 6, 2), (3, 3, 2),
+    (3, 4, 0), (4, 2, 3), (4, 5, 1), (4, 2, 4), (5, 4, 1), (5, 5, 2), (5, 7, 3), (7, 4, 2),
+    (7, 8, 1), (8, 3, 3), (8, 3, 4), (9, 6, 3), (9, 7, 4), (10, 8, 2), (11, 5, 3), (11, 4, 3),
+    (11, 8, 3), (12, 4, 4), (12, 6, 4), (12, 5, 4), (12, 8, 4),
+)
+ZERO_ROW, OB, DB, FG, FS, SG, SS, UB = 1, 3, 4, 5, 6, 7, 8, 9
+
+
+def first_kernel(n, nc, ps, qs, ks, vs, os, us, xs, wq, wk, wv, wo, wu, vec, q, k, v,
+                 x, pk, w3, y3, ssem, rsem, lsem, hs, hr, xsem, osem):
+    t = pl.program_id(0)
+    p = Place(n)
+    rows, d = xs.shape
+    r = qs.shape[0]
+    right, left = lax.rem(p.me + 1, n), lax.rem(p.me + n - 1, n)
+    edges = [pltpu.make_async_remote_copy(src_ref=xs.at[pl.ds(rows - HALO, HALO), :], dst_ref=x.at[pl.ds(0, HALO), :], send_sem=hs.at[0],
+                                          recv_sem=hr.at[0], device_id=(right,), device_id_type=MESH),
+             pltpu.make_async_remote_copy(src_ref=xs.at[pl.ds(0, HALO), :], dst_ref=x.at[pl.ds(HALO + rows, HALO), :], send_sem=hs.at[1],
+                                          recv_sem=hr.at[1], device_id=(left,), device_id_type=MESH)]
+    mine = pltpu.make_async_copy(xs, x.at[pl.ds(HALO, rows), :], xsem)
+    plan = [(ps, pk, 0), (qs, w3.at[0], 0), (ks, w3.at[1], 0), (vs, w3.at[2], 0), (os, wo, 0)] + [(us, wu, j * d) for j in range(us.shape[1] // d)]
+    g = [Gather(p, a, b, (0, a.shape[0]), (c, d), ssem, rsem, lsem, i) for i, (a, b, c) in enumerate(plan)]
+    weights = [pltpu.make_async_copy(w3.at[i], o, osem.at[i]) for i, o in enumerate((wq, wk, wv))]
+    results = [pltpu.make_async_copy(y3.at[i], o, osem.at[3 + i]) for i, o in enumerate((q, k, v))]
+
+    def vectors():
+        vec[...] = jnp.sum(pk[...].astype(F32).reshape(n, pk.shape[-2], d), axis=0)
+
+    @pl.when(t == 0)
+    def _():
+        enter(p.peers() + [left, right])
+
+    @pl.when((t > 0) & (t <= 3 * nc))
+    def _():
+        i = (t - 1) // nc
+        c = lanes(lax.rem(t - 1, nc), TC)
+        y = dot(x[...], w3[pl.ds(i, 1), ..., c].reshape(d, TC)) + vec[pl.ds(i, 1), c]
+        y3[pl.ds(i, 1), :, c] = y.astype(BF16)[None]
+
+    events = []
+    for step, i, ph in FIRST_PLAN:
+        events.append((step, gather_go, g[i], ph))
+        if i == 0 and ph == 0:
+            events += [(0, mine.start)] + [(0, c.start) for c in edges]
+        if ph == 4 and i == 0:
+            events.append((step, vectors))
+        if ph == 4 and 1 <= i <= 3:
+            events.append((step, weights[i - 1].start))
+    events += [(0, mine.wait)] + [(0, c.wait_recv) for c in edges]
+    events += [((i + 1) * nc, c.start) for i, c in enumerate(results)]
+    last = 3 * nc
+    events += [(last, c.sent) for c in g] + [(last, c.wait_send) for c in edges] + [(last, c.wait) for c in weights + results]
+    run_at(t, events)
+
+
+def first_call(n, packed, wq, wk, wv, wo, wu, x):
+    rows, d = x.shape
+    win = rows + 2 * HALO
+    nc = d // TC
+    r = wq.shape[0]
+    z = grid_of(n) + (2,)
+    count = 5 + wu.shape[1] // d
+    k = gather_slots(n)
+    mat = jax.ShapeDtypeStruct(z + (r, d), BF16)
+    out = jax.ShapeDtypeStruct((win, d), BF16)
+    res = pl.pallas_call(
+        functools.partial(first_kernel, n, nc),
+        grid=(3 * nc + 1,),
+        in_specs=[ANY] * 7,
+        out_specs=[ANY] * 5 + [single(packed.shape)] + [ANY] * 3,
+        out_shape=[mat] * 4 + [jax.ShapeDtypeStruct(z + wu.shape, BF16), jax.ShapeDtypeStruct(packed.shape, F32)] + [out] * 3,
+        scratch_shapes=[pltpu.VMEM((win, d), BF16), pltpu.VMEM(z + packed.shape, BF16), pltpu.VMEM((3,) + z + (r, d), BF16),
+                        pltpu.VMEM((3, win, d), BF16), pltpu.SemaphoreType.DMA((count, k)), pltpu.SemaphoreType.DMA((count, k)),
+                        pltpu.SemaphoreType.DMA((count,)), pltpu.SemaphoreType.DMA((2,)), pltpu.SemaphoreType.DMA((2,)),
+                        pltpu.SemaphoreType.DMA, pltpu.SemaphoreType.DMA((6,))],
+        compiler_params=pltpu.CompilerParams(collective_id=1, has_side_effects=True, vmem_limit_bytes=56 << 20),
+        cost_estimate=cost(6 * win * d * d, 2 * (4 * win * d + 3 * d * d)),
+        name="first",
+    )(packed, wq, wk, wv, wo, wu, x)
+    ws = [w.reshape((-1, w.shape[-1])) for w in res[:5]]
+    return ws + list(res[5:])
+
+
+DOWN_PLAN = (
+    (0, 1, 0), (2, 1, 1), (2, 0, 0), (3, 1, 2), (3, 2, 0), (3, 0, 1), (4, 2, 1), (4, 3, 0),
+    (4, 0, 2), (6, 3, 1), (6, 1, 3), (6, 2, 2), (7, 0, 3), (8, 3, 2), (9, 2, 3), (9, 1, 4),
+    (9, 0, 4), (10, 3, 3), (11, 2, 4), (11, 3, 4),
+)
+
+
+def fwd_kernel(n, nu, nc, ctx, wo, x, wu, wds, g, vec, xhat, lowt, ctxt, r1, hidt, dg, out, gs, gd, sums, wd, z, hid, low, wt,
+               ssem, rsem, lsem, wsem):
+    t = pl.program_id(0)
+    rows, d = x.shape
+    p = Place(n)
+    blocks = len(set(e[1] for e in DOWN_PLAN))
+    r = wds.shape[0] // blocks
+    ga = [Gather(p, wds, wd, (i * r, r), (0, d), ssem, rsem, lsem, i) for i in range(blocks)]
+    fetch = [pltpu.make_async_copy(wd.at[:, :, :, :, :, pl.ds(j * TC, TC)], wt.at[j % 2], wsem.at[j]) for j in range(nc)]
+    first = nc + nu
+
+    @pl.when(t == 0)
+    def _():
+        enter(p.peers())
+
+    run_at(t, [(first + j, fetch[j].wait) for j in range(nc)] + [(first + j, fetch[j + 1].start) for j in range(nc - 1)])
+
+    @pl.when(t < nc)
+    def _():
+        c = lanes(t, TC)
+        z[:, c] = dot(ctx[...], wo[...]) + x[:, c].astype(F32)
+
+    @pl.when(t == nc - 1)
+    def _():
+        def fin(r):
+            n, rr = norm_stats(z[r, :] + vec[OB:OB + 1, :])
+            xhat[r, :] = n
+            r1[r, :] = jnp.broadcast_to(rr, (RC, r1.shape[1]))
+            v = (n * vec[FG:FG + 1, :] + vec[FS:FS + 1, :]).astype(BF16)
+            low[r, :] = v
+            lowt[:, r] = v.T
+            ctxt[:, r] = ctx[r, :].T
+
+        chunks(rows, fin)
+
+    @pl.when((t >= nc) & (t < nc + nu))
+    def _():
+        for j in range(TF // TC):
+            c = slice(j * TC, (j + 1) * TC)
+            tile = (t - nc) * (TF // TC) + j
+            bias = vec[pl.ds(UB + tile // (d // TC), 1), lanes(lax.rem(tile, d // TC), TC)]
+            h, s = gelu_parts(dot(low[...], wu[:, c]) + bias)
+            h = h.astype(BF16)
+            dg[:, c] = s.astype(BF16)
+            hid[:, lanes(tile, TC)] = h
+            hidt[c, :] = h.T
+
+    @pl.when(t >= nc + nu)
+    def _():
+        c = lanes(t - nc - nu, TC)
+        z[:, c] = dot(hid[...], wt[pl.ds(lax.rem(t - first, 2), 1)].reshape(hid.shape[1], TC))
+
+    @pl.when(t == 2 * nc + nu - 1)
+    def _():
+        sums[...] = jnp.zeros_like(sums)
+
+        def fin(r):
+            v = (xhat[r, :] * vec[FG:FG + 1, :] + vec[FS:FS + 1, :]) + (z[r, :] + vec[DB:DB + 1, :])
+            n, rr = norm_stats(v)
+            out[r, :] = (n * vec[SG:SG + 1, :] + vec[SS:SS + 1, :]).astype(BF16)
+            gv = g[r, :].astype(F32)
+            sums[0:1, :] += colsum(gv * n)
+            sums[1:2, :] += colsum(gv)
+            grad = norm_back(gv * vec[SG:SG + 1, :], n, rr)
+            gs[r, :] = grad
+            low_g = grad.astype(BF16)
+            gd[r, :] = low_g
+            sums[2:3, :] += colsum(low_g.astype(F32))
+
+        chunks(rows, fin)
+
+    run_at(t, [(e[0], gather_go, ga[e[1]], e[2]) for e in DOWN_PLAN] + [(first - 1, c.sent) for c in ga] + [(first - 1, fetch[0].start)])
+
+
+def fwd_call(n, ctx, wo, x, wu, wd, g, vec):
+    rows, d = x.shape
+    ff = wu.shape[1]
+    nu, nc = ff // TF, d // TC
+    z = grid_of(n) + (2,)
+    k = gather_slots(n)
+    blocks = ff // d
+    full = jax.ShapeDtypeStruct(z + wd.shape, BF16)
+    *res, down = pl.pallas_call(
+        functools.partial(fwd_kernel, n, nu, nc),
+        grid=(2 * nc + nu,),
+        in_specs=[single(ctx.shape), pl.BlockSpec((d, TC), lambda t: (0, clip(t, 0, nc))), single(x.shape),
+                  pl.BlockSpec((d, TF), lambda t: (0, clip(t, nc, nu))), ANY, single(g.shape), single(vec.shape)],
+        out_specs=[single((rows, d)), single((d, rows)), single((d, rows)), single((rows, 128)),
+                   pl.BlockSpec((TF, rows), lambda t: (clip(t, nc, nu), 0)), pl.BlockSpec((rows, TF), lambda t: (0, clip(t, nc, nu))),
+                   single((rows, d)), single((rows, d)), single((rows, d)), single((8, d)), ANY],
+        out_shape=[jax.ShapeDtypeStruct((rows, d), F32), jax.ShapeDtypeStruct((d, rows), BF16), jax.ShapeDtypeStruct((d, rows), BF16),
+                   jax.ShapeDtypeStruct((rows, 128), F32), jax.ShapeDtypeStruct((ff, rows), BF16),
+                   jax.ShapeDtypeStruct((rows, ff), BF16), jax.ShapeDtypeStruct((rows, d), BF16),
+                   jax.ShapeDtypeStruct((rows, d), F32), jax.ShapeDtypeStruct((rows, d), BF16), jax.ShapeDtypeStruct((8, d), F32), full],
+        scratch_shapes=[pltpu.VMEM((rows, d), F32), pltpu.VMEM((rows, ff), BF16), pltpu.VMEM((rows, d), BF16),
+                        pltpu.VMEM((2,) + z + (wd.shape[0], TC), BF16), pltpu.SemaphoreType.DMA((blocks, k)),
+                        pltpu.SemaphoreType.DMA((blocks, k)), pltpu.SemaphoreType.DMA((blocks,)), pltpu.SemaphoreType.DMA((nc,))],
+        compiler_params=pltpu.CompilerParams(collective_id=2, has_side_effects=True, vmem_limit_bytes=62 << 20),
+        cost_estimate=cost(4 * rows * d * ff, 4 * d * ff + 4 * rows * ff + rows * d * 14, 2 * rows * ff),
+        name="fwd",
+    )(ctx, wo, x, wu, wd, g, vec)
+    return res + [down.reshape(ff, d)]
+
+
+BWD_PLAN = (
+    (1, 1, 0, 0), (1, 1, 1, 0), (2, 0, 0, 1), (2, 0, 0, 5), (2, 0, 1, 1), (3, 1, 3, 0),
+    (3, 1, 1, 5), (3, 1, 0, 2), (3, 1, 2, 0), (4, 0, 3, 1), (4, 0, 3, 5), (4, 0, 2, 1),
+    (5, 1, 5, 0), (5, 1, 1, 2), (5, 1, 4, 0), (6, 0, 0, 3), (6, 0, 2, 5), (6, 0, 5, 1),
+    (6, 0, 4, 1), (6, 0, 4, 5), (7, 0, 3, 2), (7, 0, 1, 3), (8, 1, 5, 5), (9, 1, 2, 2),
+    (10, 1, 3, 3), (12, 1, 2, 3), (12, 1, 5, 2), (14, 1, 4, 2), (15, 1, 5, 3), (20, 1, 4, 3),
+    (21, 1, 1, 4), (22, 1, 2, 4), (23, 1, 3, 4), (23, 1, 5, 4), (23, 1, 0, 4), (23, 1, 4, 4),
+)
+EARLY = 6
+
+
+def bwd_kernel(n, nu, nc, nr, gd, lowt, hidt, dg, wd, wu, gs, xhat, r1, vec, wo, ctxt,
+               gsf, sums, sumu, gc, dwo, rd, ru, gl, gr, *rest):
     t = pl.program_id(0)
     d, rows = lowt.shape
-    ssem, rsem, lsem, wsem = rest[-4:]
+    per = d // TF
+    count = 2 * (nu // per)
+    late = rest[:count - EARLY]
+    gu, bufd, bufu, ga = rest[count - EARLY:count - EARLY + 4]
+    rest = rest[count - EARLY + 4:]
+    ssem, rsem, lsem, wsem, hs, hr = rest[-6:]
     p = Place(n)
     r = d // n
     red = []
-    for i in range(2 * EARLY):
+    for i in range(EARLY):
         j = i // 2
         out = rd.at[pl.ds(j * r, r), :] if i % 2 == 0 else ru.at[:, pl.ds(j * d, d)]
         red.append(Reduce(p, (bufd, bufu)[i % 2], None, rest[8 * i:8 * i + 8], out, ssem, rsem, lsem, i))
-    late = [pltpu.make_async_copy(bufd, dwd3, wsem.at[0]), pltpu.make_async_copy(bufu, dwu3, wsem.at[1])]
+    right, left = lax.rem(p.me + 1, n), lax.rem(p.me + n - 1, n)
+    edges = [pltpu.make_async_remote_copy(src_ref=gc.at[pl.ds(rows - HALO, HALO), :], dst_ref=gl, send_sem=hs.at[0], recv_sem=hr.at[0],
+                                          device_id=(right,), device_id_type=MESH),
+             pltpu.make_async_remote_copy(src_ref=gc.at[pl.ds(0, HALO), :], dst_ref=gr, send_sem=hs.at[1], recv_sem=hr.at[1],
+                                          device_id=(left,), device_id_type=MESH)]
+    last = nu + 3 * nc + nr - 1
+    mid = [(e[0], red[e[2]].go, e[3]) for e in BWD_PLAN if e[1] == 0]
+    end = [(e[0], red[e[2]].go, e[3]) for e in BWD_PLAN if e[1] == 1]
+    for i in range(EARLY, count):
+        c = pltpu.make_async_copy((bufd, bufu)[i % 2], late[i - EARLY], wsem.at[i - EARLY])
+        end.append((per * (i // 2 + 1) - 1, c.start))
+        if per * (i // 2 + 1) < nu:
+            mid.append((per * (i // 2 + 1), c.wait))
+        else:
+            end.append((last, c.wait))
+    end += [(nu + 2 * nc + nr - 1, c.start) for c in edges] + [(last, c.wait) for c in edges]
+    end += [(last, c.finish) for c in red]
 
     @pl.when(t == 0)
     def _():
-        enter(p.peers())
+        enter(p.peers() + [left, right])
 
     @pl.when(t < nu)
     def _():
@@ -647,18 +713,11 @@
             gu[:, lanes(t * (TF // TC) + j, TC)] = g
             sumu[:, c] = colsum(g.astype(F32))
 
-    mid = []
-    for j in range(EARLY):
-        mid += [(2 * j + 2, red[2 * j].go, 1), (2 * j + 2, red[2 * j + 1].go, 1)]
-        if j > 0:
-            mid += [(2 * j + 2, red[2 * j - 1].go, 2)]
-        if j > 1:
-            mid += [(2 * j + 2, red[2 * j - 3].go, 4)]
     run_at(t, mid)
 
     @pl.when(t < nu)
     def _():
-        half = lax.rem(t, d // TF)
+        half = lax.rem(t, per)
         for j in range(TF // TC):
             c = lanes(half * (TF // TC) + j, TC)
             bufu[..., c] = dot(lowt[...], gu[:, lanes(t * (TF // TC) + j, TC)]).astype(BF16).reshape(bufu.shape[:-1] + (TC,))
@@ -672,32 +731,33 @@
     def _():
         sums[...] = jnp.zeros_like(sums)
 
-    @pl.when(t >= nu + nc)
+    @pl.when((t >= nu + nc) & (t < nu + nc + nr))
     def _():
         at = lanes(t - nu - nc, RC)
         gf = gsf[at, :]
         nn = xhat[...]
         sums[0:1, :] += colsum(gf * nn)
         sums[1:2, :] += colsum(gf)
-        grad = norm_back(gf * vec[4:5, :], nn, r1[:, 0:1])
+        grad = norm_back(gf * vec[FG:FG + 1, :], nn, r1[:, 0:1])
         gsf[at, :] = grad
         low_g = grad.astype(BF16)
-        ga[...] = low_g
+        ga[at, :] = low_g
         sums[2:3, :] += colsum(low_g.astype(F32))
 
-    end = []
-    for j in range(EARLY):
-        s = 2 * j + 1
-        end += [(s, red[2 * j].begin), (s, red[2 * j + 1].begin)]
-    end += [(3, red[0].go, 2), (4, red[0].go, 3), (5, red[1].go, 3), (5, red[2].go, 2), (5, red[0].go, 4)]
-    end += [(6, red[2].go, 3), (7, late[0].start), (7, late[1].start), (7, red[3].go, 3), (7, red[4].go, 2), (8, red[2].go, 4),
-            (8, red[5].go, 2), (9, red[4].go, 3), (9, red[3].go, 4), (10, red[5].go, 3), (12, red[4].go, 4)]
-    last = nu + nc + nr - 1
-    end += [(last, red[5].go, 4)] + [(last, c.wait) for c in late] + [(last, c.finish) for c in red]
+    first = nu + nc + nr
+
+    @pl.when((t >= first) & (t < first + nc))
+    def _():
+        gc[:, lanes(t - first, TC)] = dot_nt(ga[...], wo[...]).astype(BF16)
+
+    @pl.when(t >= first + nc)
+    def _():
+        dwo[...] = dot(ctxt[...], ga[:, lanes(t - first - nc, TC)]).astype(BF16)
+
     run_at(t, end)
 
 
-def bwd_call(n, gd, lowt, hidt, dg, wd, wu, gs, xhat, r1, vec):
+def bwd_call(n, gd, lowt, hidt, dg, wd, wu, gs, xhat, r1, vec, wo, ctxt):
     d, rows = lowt.shape
     ff = wu.shape[1]
     nu, nc, nr = ff // TF, d // TC, rows // RC
@@ -707,98 +767,59 @@
     per = d // TF
     chunk = jax.ShapeDtypeStruct(z + (d,), BF16)
     k = reduce_slots(n)
-    scratch = [pltpu.VMEM((rows, ff), BF16), pltpu.VMEM(z + (d,), BF16), pltpu.VMEM(z + (d,), BF16)]
-    for i in range(2 * EARLY):
+    late = 2 * parts - EARLY
+    scratch = [pltpu.VMEM((rows, ff), BF16), pltpu.VMEM(z + (d,), BF16), pltpu.VMEM(z + (d,), BF16), pltpu.VMEM((rows, d), BF16)]
+    for i in range(EARLY):
         scratch += reduce_buffers(n, r, d, BF16)
-    scratch += [pltpu.SemaphoreType.DMA((2 * EARLY, k)), pltpu.SemaphoreType.DMA((2 * EARLY, k)), pltpu.SemaphoreType.DMA((2 * EARLY, 2)),
-                pltpu.SemaphoreType.DMA((2,))]
+    scratch += [pltpu.SemaphoreType.DMA((EARLY, k)), pltpu.SemaphoreType.DMA((EARLY, k)), pltpu.SemaphoreType.DMA((EARLY, 2)),
+                pltpu.SemaphoreType.DMA((late,)), pltpu.SemaphoreType.DMA((2,)), pltpu.SemaphoreType.DMA((2,))]
+    edge = jax.ShapeDtypeStruct((HALO, d), BF16)
+    first = nu + nc + nr
     return pl.pallas_call(
         functools.partial(bwd_kernel, n, nu, nc, nr),
-        grid=(nu + nc + nr,),
+        grid=(nu + 3 * nc + nr,),
         in_specs=[single(gd.shape), single(lowt.shape),
                   pl.BlockSpec((n, 1, r, rows), lambda t: (0, clip(t, 0, nu) // per, 0, 0)),
                   pl.BlockSpec((rows, TF), lambda t: (0, clip(t, 0, nu))), pl.BlockSpec((TF, d), lambda t: (clip(t, 0, nu), 0)),
                   pl.BlockSpec((TC, ff), lambda t: (clip(t, nu, nc), 0)), pl.BlockSpec((rows, TC), lambda t: (0, clip(t, nu, nc))),
                   pl.BlockSpec((RC, d), lambda t: (clip(t, nu + nc, nr), 0)), pl.BlockSpec((RC, 128), lambda t: (clip(t, nu + nc, nr), 0)),
-                  single(vec.shape)],
-        out_specs=[single((rows, d)), pl.BlockSpec((RC, d), lambda t: (clip(t, nu + nc, nr), 0)), single((8, d)),
-                   pl.BlockSpec((1, TF), lambda t: (0, clip(t, 0, nu))), ANY, ANY, ANY, ANY],
-        out_shape=[jax.ShapeDtypeStruct((rows, d), F32), jax.ShapeDtypeStruct((rows, d), BF16), jax.ShapeDtypeStruct((8, d), F32),
-                   jax.ShapeDtypeStruct((1, ff), F32), chunk, chunk,
-                   jax.ShapeDtypeStruct((EARLY * r, d), F32), jax.ShapeDtypeStruct((r, EARLY * d), F32)],
+                  single(vec.shape), pl.BlockSpec((TC, d), lambda t: (clip(t, first, nc), 0)), single(ctxt.shape)],
+        out_specs=[single((rows, d)), single((8, d)), pl.BlockSpec((1, TF), lambda t: (0, clip(t, 0, nu))), single((rows, d)),
+                   pl.BlockSpec((d, TC), lambda t: (0, clip(t, first + nc, nc)))] + [ANY] * (4 + late),
+        out_shape=[jax.ShapeDtypeStruct((rows, d), F32), jax.ShapeDtypeStruct((8, d), F32), jax.ShapeDtypeStruct((1, ff), F32),
+                   jax.ShapeDtypeStruct((rows, d), BF16), jax.ShapeDtypeStruct((d, d), BF16),
+                   jax.ShapeDtypeStruct(((EARLY + 1) // 2 * r, d), F32), jax.ShapeDtypeStruct((r, EARLY // 2 * d), F32), edge, edge]
+        + [chunk] * late,
         scratch_shapes=scratch,
-        compiler_params=pltpu.CompilerParams(collective_id=3, has_side_effects=True, vmem_limit_bytes=60 << 20),
+        compiler_params=pltpu.CompilerParams(collective_id=3, has_side_effects=True, vmem_limit_bytes=62 << 20),
         cost_estimate=cost(8 * rows * d * ff, 8 * d * ff + 4 * rows * ff + rows * d * 18),
         name="bwd",
-    )(gd, lowt, hidt.reshape(n, parts, r, rows), dg, wd, wu, gs, xhat, r1, vec)
-
-
-def ctx_bwd_kernel(n, nc, ga, wo, ctxt, gc, dwo, gl, gr, ssem, rsem):
+    )(gd, lowt, hidt.reshape(n, parts, r, rows), dg, wd, wu, gs, xhat, r1, vec, wo, ctxt)
+
+
+IN_PLAN = (
+    (0, 6, 0), (0, 1, 0), (2, 6, 1), (2, 2, 0), (2, 6, 5), (3, 1, 1), (3, 1, 5), (4, 6, 2),
+    (4, 3, 0), (5, 3, 1), (5, 3, 5), (5, 1, 2), (5, 0, 0), (6, 2, 1), (7, 4, 0), (7, 2, 5),
+    (7, 4, 1), (8, 4, 5), (9, 1, 3), (10, 0, 1), (10, 6, 3), (10, 0, 5), (10, 3, 2), (11, 3, 3),
+    (11, 5, 0), (11, 2, 2), (12, 0, 2), (12, 5, 1), (12, 6, 4), (12, 5, 5), (12, 2, 3), (12, 4, 2),
+    (13, 0, 3), (13, 4, 3), (13, 5, 2), (13, 5, 3), (13, 1, 4), (14, 2, 4), (15, 0, 4), (15, 4, 4),
+    (15, 3, 4), (15, 5, 4),
+)
+
+
+def in_bwd_kernel(n, nc, left, x, gsf, dq, dk, dv, wq, wk, wv, *rest):
     t = pl.program_id(0)
-    rows = ga.shape[0]
-    me = lax.axis_index("dp")
-    right, left = lax.rem(me + 1, n), lax.rem(me + n - 1, n)
-    copies = [pltpu.make_async_remote_copy(src_ref=gc.at[pl.ds(rows - HALO, HALO), :], dst_ref=gl, send_sem=ssem.at[0], recv_sem=rsem.at[0],
-                                           device_id=(right,), device_id_type=MESH),
-              pltpu.make_async_remote_copy(src_ref=gc.at[pl.ds(0, HALO), :], dst_ref=gr, send_sem=ssem.at[1], recv_sem=rsem.at[1],
-                                           device_id=(left,), device_id_type=MESH)]
-
-    @pl.when(t == 0)
-    def _():
-        enter([left, right])
-
-    @pl.when(t < nc)
-    def _():
-        gc[:, lanes(t, TC)] = dot_nt(ga[...], wo[...]).astype(BF16)
-
-    @pl.when(t == nc - 1)
-    def _():
-        for c in copies:
-            c.start()
-
-    @pl.when(t >= nc)
-    def _():
-        dwo[...] = dot(ctxt[...], ga[:, lanes(t - nc, TC)]).astype(BF16)
-
-    @pl.when(t == 2 * nc - 1)
-    def _():
-        for c in copies:
-            c.wait()
-
-
-def ctx_bwd_call(n, ga, wo, ctxt):
-    rows, d = ga.shape
-    nc = d // TC
-    edge = jax.ShapeDtypeStruct((HALO, d), BF16)
-    return pl.pallas_call(
-        functools.partial(ctx_bwd_kernel, n, nc),
-        grid=(2 * nc,),
-        in_specs=[single(ga.shape), pl.BlockSpec((TC, d), lambda t: (clip(t, 0, nc), 0)), single(ctxt.shape)],
-        out_specs=[single((rows, d)), pl.BlockSpec((d, TC), lambda t: (0, clip(t, nc, nc))), ANY, ANY],
-        out_shape=[jax.ShapeDtypeStruct((rows, d), BF16), jax.ShapeDtypeStruct((d, d), BF16), edge, edge],
-        scratch_shapes=[pltpu.SemaphoreType.DMA((2,)), pltpu.SemaphoreType.DMA((2,))],
-        compiler_params=pltpu.CompilerParams(collective_id=4, has_side_effects=True, vmem_limit_bytes=40 << 20),
-        cost_estimate=cost(4 * rows * d * d, rows * d * 8 + 4 * d * d),
-        name="ctx_bwd",
-    )(ga, wo, ctxt)
-
-
-def in_bwd_kernel(n, nc, x, gsf, dq, dk, dv, wq, wk, wv, sd, su, so, sv, tg, rd, ru, ro, rv, rq, rk, rw, xt, bq, bk, bv, od, ou, oo, ov, *rest):
-    t = pl.program_id(0)
+    srcs, rest = rest[:left + 2], rest[left + 2:]
+    tg, outs, rest = rest[0], rest[1:left + 6], rest[left + 6:]
+    xt, bq, bk, bv, owns, rest = rest[0], rest[1], rest[2], rest[3], rest[4:left + 6], rest[left + 6:]
     ssem, rsem, lsem = rest[-3:]
     p = Place(n)
-    plan = [(sd, od, rd), (su, ou, ru), (so, oo, ro), (bq, None, rq), (bk, None, rk), (bv, None, rw), (sv, ov, rv)]
-    red = [Reduce(p, s, o, rest[8 * i:8 * i + 8], out, ssem, rsem, lsem, i) for i, (s, o, out) in enumerate(plan)]
+    plan = list(zip(srcs[:-1], owns[:-1])) + [(b, None) for b in (bq, bk, bv)] + [(srcs[-1], owns[-1])]
+    red = [Reduce(p, s, o, rest[8 * i:8 * i + 8], outs[i], ssem, rsem, lsem, i) for i, (s, o) in enumerate(plan)]
 
     @pl.when(t == 0)
     def _():
         enter(p.peers())
-
-    start = [(0, red[i].begin) for i in (0, 1, 2, 6)]
-    run_at(t, start)
-
-    @pl.when(t == 0)
-    def _():
         xt[...] = x[...].T
 
     for i, (a, b) in enumerate(((dq, bq), (dk, bk), (dv, bv))):
@@ -812,18 +833,10 @@
         g = gsf[...] + dot_nt(dq[...], wq[...]) + dot_nt(dk[...], wk[...]) + dot_nt(dv[...], wv[...])
         tg[...] = g.astype(BF16)
 
-    a, b, o, q, k, v, s = red
-    end = [(0, a.go, 1), (1, b.go, 1), (2, o.go, 1), (3, q.begin), (5, q.go, 1), (6, a.go, 2), (7, k.begin), (8, s.go, 1), (9, k.go, 1), (10, b.go, 2),
-           (11, v.begin), (12, a.go, 3), (13, v.go, 1), (14, o.go, 2)]
-    last = 4 * nc - 1
-    end += [(last, s.go, 2), (last, b.go, 3), (last, a.go, 4), (last, q.go, 2), (last, o.go, 3), (last, k.go, 2), (last, b.go, 4), (last, q.go, 3),
-            (last, s.go, 3), (last, v.go, 2), (last, o.go, 4), (last, k.go, 3), (last, q.go, 4), (last, v.go, 3), (last, s.go, 4), (last, k.go, 4),
-            (last, v.go, 4)]
-    end += [(last, c.finish) for c in red]
-    run_at(t, end)
-
-
-def in_bwd_call(n, x, gsf, dq, dk, dv, wq, wk, wv, dwd3, dwu3, dwo, small):
+    run_at(t, [(e[0], red[e[1]].go, e[2]) for e in IN_PLAN] + [(4 * nc - 1, c.finish) for c in red])
+
+
+def in_bwd_call(n, x, gsf, dq, dk, dv, wq, wk, wv, late, dwo, small):
     rows, d = x.shape
     nc = d // TC
     r = d // n
@@ -835,41 +848,52 @@
     share = jax.ShapeDtypeStruct((r, d), F32)
     sr, sc = small.shape[0] // n, small.shape[1]
     k = reduce_slots(n)
-    scratch = [pltpu.VMEM((d, rows), BF16)] + [chunk] * 3 + [own] * 3 + [pltpu.VMEM(z + (sr, sc), F32)]
-    for i in range(6):
+    left = len(late)
+    total = left + 5
+    scratch = [pltpu.VMEM((d, rows), BF16)] + [chunk] * 3 + [own] * (left + 1) + [pltpu.VMEM(z + (sr, sc), F32)]
+    for i in range(total - 1):
         scratch += reduce_buffers(n, r, d, BF16)
     scratch += reduce_buffers(n, sr, sc, F32)
-    scratch += [pltpu.SemaphoreType.DMA((7, k)), pltpu.SemaphoreType.DMA((7, k)), pltpu.SemaphoreType.DMA((7, 2))]
+    scratch += [pltpu.SemaphoreType.DMA((total, k)), pltpu.SemaphoreType.DMA((total, k)), pltpu.SemaphoreType.DMA((total, 2))]
     return pl.pallas_call(
-        functools.partial(in_bwd_kernel, n, nc),
+        functools.partial(in_bwd_kernel, n, nc, left),
         grid=(4 * nc,),
-        in_specs=[single((rows, d)), col] + [single((rows, d))] * 3 + [wrow] * 3 + [ANY] * 4,
-        out_specs=[col] + [ANY] * 7,
-        out_shape=[jax.ShapeDtypeStruct((rows, d), BF16), share, share, share, jax.ShapeDtypeStruct((sr, sc), F32), share, share, share],
+        in_specs=[single((rows, d)), col] + [single((rows, d))] * 3 + [wrow] * 3 + [ANY] * (left + 2),
+        out_specs=[col] + [ANY] * total,
+        out_shape=[jax.ShapeDtypeStruct((rows, d), BF16)] + [share] * (left + 4) + [jax.ShapeDtypeStruct((sr, sc), F32)],
         scratch_shapes=scratch,
-        compiler_params=pltpu.CompilerParams(collective_id=5, has_side_effects=True, vmem_limit_bytes=60 << 20),
+        compiler_params=pltpu.CompilerParams(collective_id=5, has_side_effects=True, vmem_limit_bytes=62 << 20),
         cost_estimate=cost(12 * rows * d * d, rows * d * 14 + 12 * d * d),
         name="in_bwd",
-    )(x, gsf, dq, dk, dv, wq, wk, wv, dwd3, dwu3, dwo.reshape(z + (2, r, d)), small.reshape(z + (2, sr, sc)))
-
-
-def hand_on_kernel(q, k, v, o, ua, ub, da, db, qo, ko, vo, oo, u, d):
-    for a, b in ((q, qo), (k, ko), (v, vo), (o, oo)):
-        b[...] = a[...]
-    u[:, : ua.shape[1]] = ua[...]
-    u[:, ua.shape[1]:] = ub[...]
-    d[: da.shape[0], :] = da[...]
-    d[da.shape[0]:, :] = db[...]
-
-
-def hand_on(q, k, v, o, ua, ub, da, db):
-    r, d = q.shape
+    )(x, gsf, dq, dk, dv, wq, wk, wv, *late, dwo.reshape(z + (2, r, d)), small.reshape(z + (2, sr, sc)))
+
+
+def hand_on_kernel(groups, axes, *refs):
+    total = sum(groups)
+    at = 0
+    for g, axis, out in zip(groups, axes, refs[total:]):
+        start = 0
+        for a in refs[at:at + g]:
+            size = a.shape[axis]
+            if axis == 0:
+                out[start:start + size, :] = a[...]
+            else:
+                out[:, start:start + size] = a[...]
+            start += size
+        at += g
+
+
+def hand_on(parts, axes):
+    shapes = []
+    for ps, axis in zip(parts, axes):
+        shape = list(ps[0].shape)
+        shape[axis] = sum(p.shape[axis] for p in ps)
+        shapes.append(jax.ShapeDtypeStruct(tuple(shape), ps[0].dtype))
     return pl.pallas_call(
-        hand_on_kernel,
-        out_shape=[jax.ShapeDtypeStruct((r, d), F32)] * 4
-        + [jax.ShapeDtypeStruct((r, ua.shape[1] + ub.shape[1]), F32), jax.ShapeDtypeStruct((da.shape[0] + db.shape[0], d), F32)],
+        functools.partial(hand_on_kernel, tuple(len(p) for p in parts), axes),
+        out_shape=shapes,
         name="hand_on",
-    )(q, k, v, o, ua, ub, da, db)
+    )(*[a for p in parts for a in p])
 
 
 def sequence_table(lengths, own, rows):
@@ -902,19 +926,23 @@
     rows, d = tokens.shape
     part = d // n
     qb, vb, ob, ub, db, fg, fs, sg, ss = shards[6:]
-    packed = pack([qb, vb, ob, db, fg, fs, sg, ss, ub], 1, 16, BF16)
-    packed, wq, wk, wv, wo, wu, wd, xl, xr = gather_call(n, [packed] + list(shards[:6]), tokens)
-    vec, bu = unpack(packed.astype(F32), n, part)
+    mine = jnp.stack([qb, jnp.zeros_like(qb), vb, ob, db, fg, fs, sg, ss])
+    mine = lax.dynamic_update_slice(jnp.zeros((UB, d), BF16), mine, (0, own * part))
+    ups = lax.dynamic_update_slice(jnp.zeros((ub.shape[0] * n,), BF16), ub, (own * ub.shape[0],)).reshape(-1, d)
+    packed = jnp.concatenate([mine, ups, jnp.zeros((16 - UB - ups.shape[0], d), BF16)])
+    wq, wk, wv, wo, wu, vec, q, k, v = first_call(n, packed, *shards[:5], tokens)
     tab = sequence_table(lengths, own, rows)
-    q, k, v = qkv_call(xl, tokens, xr, wq, wk, wv, vec)
     ctx, lse = attn_fwd_call(tab, q, k, v, rows)
-    xhat, lowt, ctxt, r1, hidt, dg, layer_out, gs, gd, sums2 = fwd_call(ctx, wo, tokens, wu, bu, wd, cotangent, vec)
-    gsf, ga, sums1, sumu, dwd3, dwu3, rd, ru = bwd_call(n, gd, lowt, hidt, dg, wd, wu, gs, xhat, r1, vec)
-    gc, dwo, gl, gr = ctx_bwd_call(n, ga, wo, ctxt)
+    xhat, lowt, ctxt, r1, hidt, dg, layer_out, gs, gd, sums2, wd = fwd_call(n, ctx, wo, tokens, wu, shards[5], cotangent, vec)
+    gsf, sums1, sumu, gc, dwo, rd, ru, gl, gr, *late = bwd_call(n, gd, lowt, hidt, dg, wd, wu, gs, xhat, r1, vec, wo, ctxt)
     dq, dk, dv, sums0 = attn_bwd_call(tab, q, k, v, lse, gl, gc, gr)
     small = pack([sums0[0], sums0[1], sums1[2], sums2[2], sums1[0], sums1[1], sums2[0], sums2[1], sumu], n, 8, F32)
-    tg, rd3, ru3, go, tiny, gq, gk, gv = in_bwd_call(n, tokens, gsf, dq, dk, dv, wq, wk, wv, dwd3, dwu3, dwo, small)
-    gq, gk, gv, go, gu, gd = hand_on(gq, gk, gv, go, ru, ru3, rd, rd3)
+    tg, *more = in_bwd_call(n, tokens, gsf, dq, dk, dv, wq, wk, wv, late, dwo, small)
+    left = len(late)
+    go, gq, gk, gv, tiny = more[left:]
+    downs = [rd] + [more[i] for i in range(left) if (EARLY + i) % 2 == 0]
+    ups = [ru] + [more[i] for i in range(left) if (EARLY + i) % 2 == 1]
+    gq, gk, gv, go, gu, gd, tg, layer_out = hand_on([[gq], [gk], [gv], [go], ups, downs, [tg], [layer_out]], (0, 0, 0, 0, 1, 0, 0, 0))
     vecs, ubg = unpack(tiny, 1, part)
     t = [vecs[i] for i in range(8)]
     return (layer_out, tg, gq, gk, gv, go, gu, gd, t[0], t[1], t[2], ubg[0], t[3], t[4], t[5], t[6], t[7])

time: 476 us -> 443 us (0.931); the launches traced: 472 us -> 446 us
  Pallas kernels: 448 us -> 434 us
  local copies, waits for them, and re-layouts: 19.8 us -> 6.97 us
    pallas_call x7 -> x5, Pallas kernels: 409 us -> 389 us  [the longest x1 111 us: first_call(): pl.pallas_call(functools.partial(first_kernel, n, nc), grid=(3 * nc + 1,)...]
    unnamed x20 -> x6, local copies, waits for them, and re-layouts: 13.2 us -> 0.8 us
where the time goes in v5:
time: 443 us; the launch traced here: 446 us
  Pallas kernels  434 us (98%)
  local copies, waits for them, and re-layouts  6.97 us (2%)
    pallas_call x1, Pallas kernels, first_call(): pl.pallas_call(functools.partial(first_kernel, n, nc), grid=(3 * nc + 1,)...  111 us
    pallas_call x1, Pallas kernels, bwd_call(): pl.pallas_call(functools.partial(bwd_kernel, n, nu, nc, nr), grid=(nu + 3...  100 us
    pallas_call x1, Pallas kernels, in_bwd_call(): pl.pallas_call(functools.partial(in_bwd_kernel, n, nc, left), grid=(4 * n...  91.7 us
    pallas_call x1, Pallas kernels, fwd_call(): pl.pallas_call(functools.partial(fwd_kernel, n, nu, nc), grid=(2 * nc + n...  80.5 us
    pallas_call x1, Pallas kernels, attn_bwd_call(): pl.pallas_call(attn_bwd_kernel, grid_spec=pltpu.PrefetchScalarGridSpec(nu...  26.2 us
    pallas_call x1, Pallas kernels, attn_fwd_call(): pl.pallas_call(attn_fwd_kernel, grid_spec=pltpu.PrefetchScalarGridSpec(nu...  19.3 us

profile of v5, /device:TPU:0, one launch (start us, length us, event | category | flops | bytes accessed | tf_op | source)
XLA Modules:
  0.0 445.6 jit_solution(293191942577559667)
XLA Ops:
  0.7 0.1 pad.7.clone
  0.8 0.8 select_reduce_fusion
  1.5 0.7 add.60
  2.2 0.9 select_reduce_fusion.2
  3.1 0.6 pad_add_fusion.tab
  3.7 1.4 stack.41
  5.2 0.8 dynamic_update_slice.7
  6.0 0.2 dynamic_update_slice.6
  6.2 0.7 maximum_maximum_fusion.ps
  6.9 111.1 %first.1 = (bf16[4,2,2,2,32,1024]{5,4,3,2,1,0:T(8,128)(2,1)}, bf16[4,2,2,2,32,1024]{5,4,3,2,1,0:T(8,128)(2,1)}, bf16[4,2,2,2,32,1024]{5,4,3,2,1,0:T(8,128)(2,1)}...) custom-call(bf16[16,1024]{1,0:T(8,128)(2,1)} %maximum_maximum_fusion, ...), custom_call_target="tpu_custom_call" | custom-call | flops 11274289152 | bytes 20971520 | tf_op jit(solution)/shard_map/first/pallas_call | solution.py:529
  118.1 19.3 %attn_fwd.1 = (bf16[1024,1024]{1,0:T(8,128)(2,1)}, f32[16,1792]{1,0:T(8,128)}) custom-call(s32[2,8]{1,0:T(2,128)} %pad_add_fusion.tab, bf16[1792,1024]{1,0:T(8,128)(2,1)} %get-tuple-element.70.q_ref, bf16[1792,1024]{1,0:T(8,128)(2,1)} %get-tuple-element.71.k_ref, bf16[1792,1024]{1,0:T(8,128)(2,1)} %get-tuple-element.72.v_ref), custom_call_target="tpu_custom_call" | custom-call | flops 4294967296 | bytes 14680064 | tf_op jit(solution)/shard_map/attn_fwd/pallas_call | solution.py:101
  137.3 80.5 %fwd.1 = (f32[1024,1024]{1,0:T(8,128)}, bf16[1024,1024]{1,0:T(8,128)(2,1)}, bf16[1024,1024]{1,0:T(8,128)(2,1)}, f32[1024,128]{1,0:T(8,128)}, bf16[4096,1024]{1,0...) custom-call(bf16[1024,1024]{1,0:T(8,128)(2,1)} %get-tuple-element.73, ...), custom_call_target="tpu_custom_call" | custom-call | flops 17179869184 | bytes 48234496 | tf_op jit(solution)/shard_map/fwd/pallas_call | solution.py:636
  217.8 100.0 %bwd.1 = (f32[1024,1024]{1,0:T(8,128)}, f32[8,1024]{1,0:T(8,128)}, f32[1,4096]{1,0:T(1,128)}, bf16[1024,1024]{1,0:T(8,128)(2,1)}, bf16[1024,1024]{1,0:T(8,128)(2...) custom-call(bf16[1024,1024]{1,0:T(8,128)(2,1)} %get-tuple-element.77, ...), custom_call_target="tpu_custom_call" | custom-call | flops 34359738368 | bytes 69206016 | tf_op jit(solution)/shard_map/bwd/pallas_call | solution.py:778
  317.8 0.9 slice_reduce_fusion
  318.8 26.2 %attn_bwd.1 = (bf16[1024,1024]{1,0:T(8,128)(2,1)}, bf16[1024,1024]{1,0:T(8,128)(2,1)}, bf16[1024,1024]{1,0:T(8,128)(2,1)}, f32[8,1024]{1,0:T(8,128)}) custom-call(s32[2,8]{1,0:T(2,128)} %pad_add_fusion.tab, bf16[1792,1024]{1,0:T(8,128)(2,1)} %get-tuple-element.70.q_ref, bf16[1792,1024]{1,0:T(8,128)(2,1)} %get-tuple-element.71.k_ref, ...), custom_call_target="tpu_custom_call" | custom-call | flops 10737418240 | bytes 25690112 | tf_op jit(solution)/shard_map/attn_bwd/pallas_call | solution.py:162
  345.0 0.9 slice_reduce_fusion.6
  345.9 0.1 reshape_squeeze.25
  346.0 0.1 reshape_squeeze.31
  346.5 0.1 concatenate.7
  346.6 0.8 copy.35
  347.4 91.7 %in_bwd.1 = (bf16[1024,1024]{1,0:T(8,128)(2,1)}, f32[32,1024]{1,0:T(8,128)}, f32[32,1024]{1,0:T(8,128)}, f32[32,1024]{1,0:T(8,128)}, f32[32,1024]{1,0:T(8,128)},...) custom-call(bf16[1024,1024]{1,0:T(8,128)(2,1)} %x.5, f32[1024,1024]{1,0:T(8,128)} %get-tuple-element.86.gsf, ...), custom_call_target="tpu_custom_call" | custom-call | flops 12884901888 | bytes 27262976 | tf_op jit(solution)/shard_map/in_bwd/pallas_call | solution.py:858
  439.1 5.4 %hand_on.1 = (f32[32,1024]{1,0:T(8,128)}, f32[32,1024]{1,0:T(8,128)}, f32[32,1024]{1,0:T(8,128)}, f32[32,1024]{1,0:T(8,128)}, f32[32,4096]{1,0:T(8,128)}, /*inde...) custom-call(f32[32,1024]{1,0:T(8,128)} %get-tuple-element.104.refs_0_, ...), custom_call_target="tpu_custom_call" | custom-call | tf_op jit(solution)/shard_map/hand_on/pallas_call | solution.py:892
  444.5 0.5 slice_bitcast_fusion.5
  445.0 0.6 slice_bitcast_fusion
  (19 shorter events, 0.5 us)
Async XLA Ops:
  318.8 27.7 %copy-start = (f32[1,4096]{1,0:T(1,128)S(1)}, f32[1,4096]{1,0:T(1,128)}, u32[]{:S(2)}) copy-start(f32[1,4096]{1,0:T(1,128)} %get-tuple-element.103) | copy-start | bytes 49156
  439.1 5.4 %copy-start.1 = (f32[8,256]{1,0:T(8,128)S(1)}, f32[8,256]{1,0:T(8,128)}, u32[]{:S(2)}) copy-start(f32[8,256]{1,0:T(8,128)} %get-tuple-element.122) | copy-start | bytes 24580

commit v6 on v5

--- a/solution.py
+++ b/solution.py
@@ -72,50 +72,11 @@
     return x * jnp.asarray(0.125, BF16)
 
 
-def attn_fwd_kernel(tab, q_ref, k_ref, v_ref, o_ref, lse_ref, ctx):
-    def work(rows, pairs):
-        mine = masks((rows.size, 2 * HD))
-        st = []
-        for c, h in pairs:
-            q, k = eighth(q_ref[rows, c]), k_ref[rows, c]
-            st += [dot_nt(k, jnp.where(m, q, jnp.zeros_like(q))) for m in mine]
-        top = [jnp.max(s, axis=0, keepdims=True) for s in st]
-        e = [jnp.exp(s - m) for s, m in zip(st, top)]
-        total = [jnp.sum(x, axis=0, keepdims=True) for x in e]
-        for i, (c, h) in enumerate(pairs):
-            vt = v_ref[rows, c].T
-            parts = []
-            for j in range(2):
-                x = 2 * i + j
-                parts.append(dot(vt[j * HD:(j + 1) * HD, :], e[x].astype(BF16)) * (1.0 / total[x]))
-                lse_ref[pl.ds(h + j, 1), rows] = top[x] + jnp.log(total[x])
-            ctx[rows, c] = jnp.concatenate(parts, axis=0).T.astype(BF16)
-
-    sequences(tab, o_ref.shape[0] // GRAN, work)
-    o_ref[...] = ctx[pl.ds(HALO, o_ref.shape[0]), :]
-
-
-def attn_fwd_call(tab, q, k, v, rows):
-    win, d = q.shape
-    spec = pl.BlockSpec((win, LANES), lambda h, t: (0, h))
-    return pl.pallas_call(
-        attn_fwd_kernel,
-        grid_spec=pltpu.PrefetchScalarGridSpec(
-            num_scalar_prefetch=1,
-            grid=(d // LANES,),
-            in_specs=[spec] * 3,
-            out_specs=[pl.BlockSpec((rows, LANES), lambda h, t: (0, h)), pl.BlockSpec((LANES // HD, win), lambda h, t: (h, 0))],
-            scratch_shapes=[pltpu.VMEM((win, LANES), BF16)],
-        ),
-        out_shape=[jax.ShapeDtypeStruct((rows, d), BF16), jax.ShapeDtypeStruct((d // HD, win), F32)],
-        compiler_params=params(),
-        cost_estimate=cost(8 * rows * 512 * d, 8 * win * d, rows * 512 * 16),
-        name="attn_fwd",
-    )(tab, q, k, v)
-
-
-def attn_bwd_kernel(tab, q_ref, k_ref, v_ref, lse_ref, gl, go, gr, dq_o, dk_o, dv_o, sums, g_s, dq_s, dk_s, dv_s):
+def attn_bwd_kernel(tab, q_ref, k_ref, v_ref, ll, lo, lr, gl, go, gr, dq_o, dk_o, dv_o, sums, lse_ref, g_s, dq_s, dk_s, dv_s):
     rows_own = go.shape[0]
+    lse_ref[:, pl.ds(0, HALO)] = ll[...]
+    lse_ref[:, pl.ds(HALO, rows_own)] = lo[...]
+    lse_ref[:, pl.ds(HALO + rows_own, HALO)] = lr[...]
     g_s[pl.ds(0, HALO), :] = gl[...]
     g_s[pl.ds(HALO, rows_own), :] = go[...]
     g_s[pl.ds(HALO + rows_own, HALO), :] = gr[...]
@@ -152,7 +113,7 @@
     sums[1:2, :] = jnp.sum(dv_o[...].astype(F32), axis=0, keepdims=True)
 
 
-def attn_bwd_call(tab, q, k, v, lse, gl, go, gr):
+def attn_bwd_call(tab, q, k, v, ll, lse, lr, gl, go, gr):
     win, d = q.shape
     rows = go.shape[0]
     spec = pl.BlockSpec((win, LANES), lambda h, t: (0, h))
@@ -164,15 +125,15 @@
         grid_spec=pltpu.PrefetchScalarGridSpec(
             num_scalar_prefetch=1,
             grid=(d // LANES,),
-            in_specs=[spec] * 3 + [pl.BlockSpec((LANES // HD, win), lambda h, t: (h, 0)), halo, own, halo],
+            in_specs=[spec] * 3 + [pl.BlockSpec((LANES // HD, a.shape[1]), lambda h, t: (h, 0)) for a in (ll, lse, lr)] + [halo, own, halo],
             out_specs=[own] * 3 + [pl.BlockSpec((8, LANES), lambda h, t: (0, h))],
-            scratch_shapes=[pltpu.VMEM((win, LANES), BF16)] * 4,
+            scratch_shapes=[pltpu.VMEM((LANES // HD, win), F32)] + [pltpu.VMEM((win, LANES), BF16)] * 4,
         ),
         out_shape=[out] * 3 + [jax.ShapeDtypeStruct((8, d), F32)],
         compiler_params=params(),
         cost_estimate=cost(20 * rows * 512 * d, 14 * win * d, rows * 512 * 16),
         name="attn_bwd",
-    )(tab, q, k, v, lse, gl, go, gr)
+    )(tab, q, k, v, ll, lse, lr, gl, go, gr)
 
 
 def norm_stats(z):
@@ -271,7 +232,7 @@
 
 
 class Gather:
-    def __init__(self, place, src, dst, rows, cols, ssem, rsem, lsem, index):
+    def __init__(self, place, src, dst, rows, cols, ssem, rsem, lsem, index, to=None):
         self.p, self.index = place, index
         self.src, self.dst, self.rows, self.cols = src, dst, rows, cols
         self.ssem, self.rsem, self.lsem = ssem, rsem, lsem
@@ -279,10 +240,11 @@
         r0, nr = rows
         c0, nc = cols
         rs = pl.ds(r0, nr)
-        full = pl.ds(c0, nc)
-        halves = (pl.ds(c0, nc // 2), pl.ds(c0 + nc // 2, nc // 2))
-        al = pl.ds(0, p.size[0])
-        self.local = pltpu.make_async_copy(src.at[rs, full], dst.at[p.z, p.y, p.x, p.c, rs, full], lsem.at[index])
+        to = c0 if to is None else to
+        mine_cols = pl.ds(c0, nc)
+        full = pl.ds(to, nc)
+        halves = (pl.ds(to, nc // 2), pl.ds(to + nc // 2, nc // 2))
+        self.local = pltpu.make_async_copy(src.at[rs, mine_cols], dst.at[p.z, p.y, p.x, p.c, rs, full], lsem.at[index])
         slot = 0
 
         def copy(s, d, dev):
@@ -295,7 +257,7 @@
         mine = dst.at[p.z, p.y, p.x, p.c, rs, full]
         self.ph = [[], [], [], []]
         for k in p.steps("z"):
-            self.ph[0].append(copy(src.at[rs, full], mine, p.at("z", k)[0]))
+            self.ph[0].append(copy(src.at[rs, mine_cols], mine, p.at("z", k)[0]))
         for h, axis in ((0, "y"), (1, "x")):
             s = dst.at[:, p.y, p.x, p.c, rs, halves[h]]
             for k in p.steps(axis):
@@ -459,13 +421,13 @@
 
 
 FIRST_PLAN = (
-    (0, 1, 0), (0, 1, 1), (0, 0, 0), (0, 2, 0), (0, 1, 2), (0, 0, 1), (0, 7, 0), (0, 0, 2),
-    (0, 6, 0), (0, 1, 3), (0, 2, 1), (0, 0, 3), (0, 7, 1), (0, 3, 0), (0, 2, 2), (0, 0, 4),
-    (0, 1, 4), (1, 8, 0), (1, 5, 0), (2, 6, 1), (3, 7, 2), (3, 3, 1), (3, 6, 2), (3, 3, 2),
-    (3, 4, 0), (4, 2, 3), (4, 5, 1), (4, 2, 4), (5, 4, 1), (5, 5, 2), (5, 7, 3), (7, 4, 2),
-    (7, 8, 1), (8, 3, 3), (8, 3, 4), (9, 6, 3), (9, 7, 4), (10, 8, 2), (11, 5, 3), (11, 4, 3),
-    (11, 8, 3), (12, 4, 4), (12, 6, 4), (12, 5, 4), (12, 8, 4),
+    (0, 0, 0), (0, 1, 0), (0, 0, 1), (0, 1, 1), (0, 4, 0), (0, 0, 2), (0, 2, 0), (0, 1, 2),
+    (0, 4, 1), (0, 0, 3), (0, 1, 3), (0, 3, 0), (0, 2, 1), (0, 4, 2), (0, 1, 4), (0, 0, 4),
+    (2, 3, 1), (2, 2, 2), (2, 6, 0), (3, 6, 1), (3, 4, 3), (3, 5, 0), (3, 3, 2), (4, 2, 3),
+    (4, 5, 1), (4, 6, 2), (4, 2, 4), (5, 4, 4), (6, 5, 2), (7, 3, 3), (8, 6, 3), (8, 3, 4),
+    (10, 5, 3), (12, 6, 4), (12, 5, 4),
 )
+UPS_FIRST = 2
 ZERO_ROW, OB, DB, FG, FS, SG, SS, UB = 1, 3, 4, 5, 6, 7, 8, 9
 
 
@@ -481,7 +443,7 @@
              pltpu.make_async_remote_copy(src_ref=xs.at[pl.ds(0, HALO), :], dst_ref=x.at[pl.ds(HALO + rows, HALO), :], send_sem=hs.at[1],
                                           recv_sem=hr.at[1], device_id=(left,), device_id_type=MESH)]
     mine = pltpu.make_async_copy(xs, x.at[pl.ds(HALO, rows), :], xsem)
-    plan = [(ps, pk, 0), (qs, w3.at[0], 0), (ks, w3.at[1], 0), (vs, w3.at[2], 0), (os, wo, 0)] + [(us, wu, j * d) for j in range(us.shape[1] // d)]
+    plan = [(ps, pk, 0), (qs, w3.at[0], 0), (ks, w3.at[1], 0), (vs, w3.at[2], 0), (os, wo, 0)] + [(us, wu, j * d) for j in range(UPS_FIRST)]
     g = [Gather(p, a, b, (0, a.shape[0]), (c, d), ssem, rsem, lsem, i) for i, (a, b, c) in enumerate(plan)]
     weights = [pltpu.make_async_copy(w3.at[i], o, osem.at[i]) for i, o in enumerate((wq, wk, wv))]
     results = [pltpu.make_async_copy(y3.at[i], o, osem.at[3 + i]) for i, o in enumerate((q, k, v))]
@@ -522,7 +484,7 @@
     nc = d // TC
     r = wq.shape[0]
     z = grid_of(n) + (2,)
-    count = 5 + wu.shape[1] // d
+    count = 5 + UPS_FIRST
     k = gather_slots(n)
     mat = jax.ShapeDtypeStruct(z + (r, d), BF16)
     out = jax.ShapeDtypeStruct((win, d), BF16)
@@ -531,7 +493,7 @@
         grid=(3 * nc + 1,),
         in_specs=[ANY] * 7,
         out_specs=[ANY] * 5 + [single(packed.shape)] + [ANY] * 3,
-        out_shape=[mat] * 4 + [jax.ShapeDtypeStruct(z + wu.shape, BF16), jax.ShapeDtypeStruct(packed.shape, F32)] + [out] * 3,
+        out_shape=[mat] * 4 + [jax.ShapeDtypeStruct(z + (r, UPS_FIRST * d), BF16), jax.ShapeDtypeStruct(packed.shape, F32)] + [out] * 3,
         scratch_shapes=[pltpu.VMEM((win, d), BF16), pltpu.VMEM(z + packed.shape, BF16), pltpu.VMEM((3,) + z + (r, d), BF16),
                         pltpu.VMEM((3, win, d), BF16), pltpu.SemaphoreType.DMA((count, k)), pltpu.SemaphoreType.DMA((count, k)),
                         pltpu.SemaphoreType.DMA((count,)), pltpu.SemaphoreType.DMA((2,)), pltpu.SemaphoreType.DMA((2,)),
@@ -545,30 +507,86 @@
 
 
 DOWN_PLAN = (
-    (0, 1, 0), (2, 1, 1), (2, 0, 0), (3, 1, 2), (3, 2, 0), (3, 0, 1), (4, 2, 1), (4, 3, 0),
-    (4, 0, 2), (6, 3, 1), (6, 1, 3), (6, 2, 2), (7, 0, 3), (8, 3, 2), (9, 2, 3), (9, 1, 4),
-    (9, 0, 4), (10, 3, 3), (11, 2, 4), (11, 3, 4),
+    (0, 2, 0), (3, 2, 1), (3, 0, 0), (4, 2, 2), (4, 5, 0), (5, 3, 0), (7, 0, 1), (10, 0, 2),
+    (12, 1, 0), (12, 5, 1), (15, 3, 1), (16, 4, 0), (17, 1, 1), (17, 2, 3), (17, 0, 3), (18, 3, 2),
+    (19, 1, 2), (20, 0, 4), (20, 4, 1), (21, 5, 2), (21, 3, 3), (23, 4, 2), (24, 3, 4), (24, 1, 3),
+    (25, 5, 3), (25, 1, 4), (26, 2, 4), (26, 4, 3), (26, 5, 4), (27, 4, 4),
 )
 
 
-def fwd_kernel(n, nu, nc, ctx, wo, x, wu, wds, g, vec, xhat, lowt, ctxt, r1, hidt, dg, out, gs, gd, sums, wd, z, hid, low, wt,
-               ssem, rsem, lsem, wsem):
-    t = pl.program_id(0)
+AG = 256
+MASKED = -1e30
+
+
+def window(ref, b, c, late):
+    x = ref[pl.ds(pl.multiple_of(b * GRAN, GRAN), 4 * GRAN), c]
+    for i, at in enumerate(late):
+        y = ref[pl.ds(pl.multiple_of((b + i + 1) * GRAN, GRAN), 4 * GRAN), c]
+        x = jnp.where(at, y, x)
+    return x
+
+
+def attend(t, tab, q_ref, k_ref, v_ref, ctx, lse):
+    subs = ctx.shape[0] // GRAN // 2
+    group, sub = t // subs, lax.rem(t, subs)
+    units = []
+    for j in range(2):
+        b = sub * 2 + j
+        late = [tab[0, b] == b + i for i in range(1, 4)]
+        own = pl.ds(pl.multiple_of(HALO + b * GRAN, GRAN), GRAN)
+        inside = lax.broadcasted_iota(jnp.int32, (4 * GRAN, 2 * GRAN), 0) < tab[2, b] * GRAN
+        for i in range(AG // (2 * HD)):
+            c = slice(i * 2 * HD, (i + 1) * 2 * HD)
+            q = eighth(q_ref[own, c])
+            zero = jnp.zeros_like(q)
+            both = jnp.concatenate([jnp.where(m, q, zero) for m in masks(q.shape)], axis=0)
+            k, v = window(k_ref, b, c, late), window(v_ref, b, c, late)
+            units.append((b, i, jnp.where(inside, dot_nt(k, both), MASKED), v))
+    top = [jnp.max(u[2], axis=0, keepdims=True) for u in units]
+    e = [jnp.exp(u[2] - m) for u, m in zip(units, top)]
+    total = [jnp.sum(x, axis=0, keepdims=True) for x in e]
+    logs = []
+    for (b, i, _, v), m, x, s in zip(units, top, e, total):
+        y = dot(v.T, x.astype(BF16)) * (1.0 / s)
+        logs.append((b, 2 * i, m + jnp.log(s)))
+        y = jnp.concatenate([y[:HD, :GRAN], y[HD:, GRAN:]], axis=0)
+        rows = pl.ds(pl.multiple_of(b * GRAN, GRAN), GRAN)
+        ctx[rows, pl.ds(pl.multiple_of(group * AG + i * 2 * HD, 2 * HD), 2 * HD)] = y.T.astype(BF16)
+    for k in range(ctx.shape[1] // AG):
+        @pl.when(group == k)
+        def _():
+            for b, h, log in logs:
+                for i in range(2):
+                    head = k * (AG // HD) + h + i
+                    lse[head:head + 1, pl.ds(pl.multiple_of(b * GRAN, GRAN), GRAN)] = log[:, i * GRAN:(i + 1) * GRAN]
+
+
+def fwd_kernel(n, na, nu, nc, tab, q_ref, k_ref, v_ref, wo, x, wu, wus, wds, g, vec,
+               lse, xhat, lowt, ctxt, r1, hidt, dg, out, gs, gd, sums, wd, wu2, ctx, z, hid, low, wt, w3,
+               ssem, rsem, lsem, wsem, usem):
+    t = pl.program_id(0) - na
     rows, d = x.shape
     p = Place(n)
-    blocks = len(set(e[1] for e in DOWN_PLAN))
+    ups = w3.shape[0]
+    blocks = len(set(e[1] for e in DOWN_PLAN)) - ups
     r = wds.shape[0] // blocks
-    ga = [Gather(p, wds, wd, (i * r, r), (0, d), ssem, rsem, lsem, i) for i in range(blocks)]
+    ga = [Gather(p, wus, w3.at[i], (0, r), ((UPS_FIRST + i) * d, d), ssem, rsem, lsem, i, 0) for i in range(ups)]
+    ga += [Gather(p, wds, wd, (i * r, r), (0, d), ssem, rsem, lsem, ups + i) for i in range(blocks)]
+    keep = [pltpu.make_async_copy(w3.at[i], wu2.at[i], usem.at[i]) for i in range(ups)]
     fetch = [pltpu.make_async_copy(wd.at[:, :, :, :, :, pl.ds(j * TC, TC)], wt.at[j % 2], wsem.at[j]) for j in range(nc)]
     first = nc + nu
 
-    @pl.when(t == 0)
+    @pl.when(t == -na)
     def _():
         enter(p.peers())
 
+    @pl.when(t < 0)
+    def _():
+        attend(t + na, tab, q_ref, k_ref, v_ref, ctx, lse)
+
     run_at(t, [(first + j, fetch[j].wait) for j in range(nc)] + [(first + j, fetch[j + 1].start) for j in range(nc - 1)])
 
-    @pl.when(t < nc)
+    @pl.when((t >= 0) & (t < nc))
     def _():
         c = lanes(t, TC)
         z[:, c] = dot(ctx[...], wo[...]) + x[:, c].astype(F32)
@@ -586,17 +604,27 @@
 
         chunks(rows, fin)
 
-    @pl.when((t >= nc) & (t < nc + nu))
-    def _():
+    def up(weight):
         for j in range(TF // TC):
             c = slice(j * TC, (j + 1) * TC)
             tile = (t - nc) * (TF // TC) + j
             bias = vec[pl.ds(UB + tile // (d // TC), 1), lanes(lax.rem(tile, d // TC), TC)]
-            h, s = gelu_parts(dot(low[...], wu[:, c]) + bias)
+            h, s = gelu_parts(dot(low[...], weight(j, tile)) + bias)
             h = h.astype(BF16)
             dg[:, c] = s.astype(BF16)
             hid[:, lanes(tile, TC)] = h
             hidt[c, :] = h.T
+
+    split = nc + UPS_FIRST * (d // TF)
+
+    @pl.when((t >= nc) & (t < split))
+    def _():
+        up(lambda j, tile: wu[:, j * TC:(j + 1) * TC])
+
+    if ups:
+        @pl.when((t >= split) & (t < nc + nu))
+        def _():
+            up(lambda j, tile: w3[pl.ds(tile // (d // TC) - UPS_FIRST, 1), ..., lanes(lax.rem(tile, d // TC), TC)].reshape(d, TC))
 
     @pl.when(t >= nc + nu)
     def _():
@@ -622,37 +650,51 @@
 
         chunks(rows, fin)
 
-    run_at(t, [(e[0], gather_go, ga[e[1]], e[2]) for e in DOWN_PLAN] + [(first - 1, c.sent) for c in ga] + [(first - 1, fetch[0].start)])
-
-
-def fwd_call(n, ctx, wo, x, wu, wd, g, vec):
+    done = {e[1]: e[0] for e in DOWN_PLAN if e[2] == 4}
+    run_at(t + na, [(e[0], gather_go, ga[e[1]], e[2]) for e in DOWN_PLAN] + [(done[i], c.start) for i, c in enumerate(keep)]
+           + [(na + first - 1, c.sent) for c in ga] + [(na + first - 1, c.wait) for c in keep] + [(na + first - 1, fetch[0].start)])
+
+
+def fwd_call(n, tab, q, k, v, wo, x, wu, wus, wd, g, vec):
     rows, d = x.shape
-    ff = wu.shape[1]
+    win = q.shape[0]
+    ff = wus.shape[1]
     nu, nc = ff // TF, d // TC
     z = grid_of(n) + (2,)
-    k = gather_slots(n)
     blocks = ff // d
-    full = jax.ShapeDtypeStruct(z + wd.shape, BF16)
-    *res, down = pl.pallas_call(
-        functools.partial(fwd_kernel, n, nu, nc),
-        grid=(2 * nc + nu,),
-        in_specs=[single(ctx.shape), pl.BlockSpec((d, TC), lambda t: (0, clip(t, 0, nc))), single(x.shape),
-                  pl.BlockSpec((d, TF), lambda t: (0, clip(t, nc, nu))), ANY, single(g.shape), single(vec.shape)],
-        out_specs=[single((rows, d)), single((d, rows)), single((d, rows)), single((rows, 128)),
-                   pl.BlockSpec((TF, rows), lambda t: (clip(t, nc, nu), 0)), pl.BlockSpec((rows, TF), lambda t: (0, clip(t, nc, nu))),
-                   single((rows, d)), single((rows, d)), single((rows, d)), single((8, d)), ANY],
-        out_shape=[jax.ShapeDtypeStruct((rows, d), F32), jax.ShapeDtypeStruct((d, rows), BF16), jax.ShapeDtypeStruct((d, rows), BF16),
-                   jax.ShapeDtypeStruct((rows, 128), F32), jax.ShapeDtypeStruct((ff, rows), BF16),
+    ups = blocks - UPS_FIRST
+    slots = gather_slots(n)
+    count = blocks + ups
+    subs = rows // GRAN // 2
+    na = d // AG * subs
+    split = UPS_FIRST * (d // TF)
+    spec = pl.BlockSpec((win, AG), lambda t: (0, clip(t, 0, na) // subs))
+
+    def tile(t):
+        return clip(t, na + nc, nu)
+
+    *res, down, up2 = pl.pallas_call(
+        functools.partial(fwd_kernel, n, na, nu, nc),
+        grid=(na + 2 * nc + nu,),
+        in_specs=[pl.BlockSpec(memory_space=pltpu.SMEM), spec, spec, spec, pl.BlockSpec((d, TC), lambda t: (0, clip(t, na, nc))),
+                  single(x.shape), pl.BlockSpec((d, TF), lambda t: (0, clip(t, na + nc, split))), ANY, ANY, single(g.shape), single(vec.shape)],
+        out_specs=[single((d // HD, rows)), single((rows, d)), single((d, rows)), single((d, rows)), single((rows, 128)),
+                   pl.BlockSpec((TF, rows), lambda t: (tile(t), 0)), pl.BlockSpec((rows, TF), lambda t: (0, tile(t))),
+                   single((rows, d)), single((rows, d)), single((rows, d)), single((8, d)), ANY, ANY],
+        out_shape=[jax.ShapeDtypeStruct((d // HD, rows), F32), jax.ShapeDtypeStruct((rows, d), F32), jax.ShapeDtypeStruct((d, rows), BF16),
+                   jax.ShapeDtypeStruct((d, rows), BF16), jax.ShapeDtypeStruct((rows, 128), F32), jax.ShapeDtypeStruct((ff, rows), BF16),
                    jax.ShapeDtypeStruct((rows, ff), BF16), jax.ShapeDtypeStruct((rows, d), BF16),
-                   jax.ShapeDtypeStruct((rows, d), F32), jax.ShapeDtypeStruct((rows, d), BF16), jax.ShapeDtypeStruct((8, d), F32), full],
-        scratch_shapes=[pltpu.VMEM((rows, d), F32), pltpu.VMEM((rows, ff), BF16), pltpu.VMEM((rows, d), BF16),
-                        pltpu.VMEM((2,) + z + (wd.shape[0], TC), BF16), pltpu.SemaphoreType.DMA((blocks, k)),
-                        pltpu.SemaphoreType.DMA((blocks, k)), pltpu.SemaphoreType.DMA((blocks,)), pltpu.SemaphoreType.DMA((nc,))],
+                   jax.ShapeDtypeStruct((rows, d), F32), jax.ShapeDtypeStruct((rows, d), BF16), jax.ShapeDtypeStruct((8, d), F32),
+                   jax.ShapeDtypeStruct(z + wd.shape, BF16), jax.ShapeDtypeStruct((ups,) + z + (wus.shape[0], d), BF16)],
+        scratch_shapes=[pltpu.VMEM((rows, d), BF16), pltpu.VMEM((rows, d), F32), pltpu.VMEM((rows, ff), BF16), pltpu.VMEM((rows, d), BF16),
+                        pltpu.VMEM((2,) + z + (wd.shape[0], TC), BF16), pltpu.VMEM((ups,) + z + (wus.shape[0], d), BF16),
+                        pltpu.SemaphoreType.DMA((count, slots)), pltpu.SemaphoreType.DMA((count, slots)),
+                        pltpu.SemaphoreType.DMA((count,)), pltpu.SemaphoreType.DMA((nc,)), pltpu.SemaphoreType.DMA((ups,))],
         compiler_params=pltpu.CompilerParams(collective_id=2, has_side_effects=True, vmem_limit_bytes=62 << 20),
         cost_estimate=cost(4 * rows * d * ff, 4 * d * ff + 4 * rows * ff + rows * d * 14, 2 * rows * ff),
         name="fwd",
-    )(ctx, wo, x, wu, wd, g, vec)
-    return res + [down.reshape(ff, d)]
+    )(tab, q, k, v, wo, x, wu, wus, wd, g, vec)
+    return res + [down.reshape(ff, d), up2.reshape(ups, d, d)]
 
 
 BWD_PLAN = (
@@ -666,8 +708,8 @@
 EARLY = 6
 
 
-def bwd_kernel(n, nu, nc, nr, gd, lowt, hidt, dg, wd, wu, gs, xhat, r1, vec, wo, ctxt,
-               gsf, sums, sumu, gc, dwo, rd, ru, gl, gr, *rest):
+def bwd_kernel(n, nu, nc, nr, gd, lowt, hidt, dg, wd, wu, wu2, gs, xhat, r1, vec, wo, ctxt, lse,
+               gsf, sums, sumu, gc, dwo, rd, ru, gl, gr, ll, lr, *rest):
     t = pl.program_id(0)
     d, rows = lowt.shape
     per = d // TF
@@ -687,6 +729,10 @@
     edges = [pltpu.make_async_remote_copy(src_ref=gc.at[pl.ds(rows - HALO, HALO), :], dst_ref=gl, send_sem=hs.at[0], recv_sem=hr.at[0],
                                           device_id=(right,), device_id_type=MESH),
              pltpu.make_async_remote_copy(src_ref=gc.at[pl.ds(0, HALO), :], dst_ref=gr, send_sem=hs.at[1], recv_sem=hr.at[1],
+                                          device_id=(left,), device_id_type=MESH),
+             pltpu.make_async_remote_copy(src_ref=lse.at[:, pl.ds(rows - HALO, HALO)], dst_ref=ll, send_sem=hs.at[2], recv_sem=hr.at[2],
+                                          device_id=(right,), device_id_type=MESH),
+             pltpu.make_async_remote_copy(src_ref=lse.at[:, pl.ds(0, HALO)], dst_ref=lr, send_sem=hs.at[3], recv_sem=hr.at[3],
                                           device_id=(left,), device_id_type=MESH)]
     last = nu + 3 * nc + nr - 1
     mid = [(e[0], red[e[2]].go, e[3]) for e in BWD_PLAN if e[1] == 0]
@@ -725,7 +771,10 @@
 
     @pl.when((t >= nu) & (t < nu + nc))
     def _():
-        gsf[:, lanes(t - nu, TC)] = gs[...] + dot_nt(gu[...], wu[...])
+        v = gs[...] + dot_nt(gu[:, :wu.shape[1]], wu[...])
+        for i in range(wu2.shape[0]):
+            v += dot_nt(gu[:, wu.shape[1] + i * d:wu.shape[1] + (i + 1) * d], wu2[i])
+        gsf[:, lanes(t - nu, TC)] = v
 
     @pl.when(t == nu + nc)
     def _():
@@ -757,9 +806,9 @@
     run_at(t, end)
 
 
-def bwd_call(n, gd, lowt, hidt, dg, wd, wu, gs, xhat, r1, vec, wo, ctxt):
+def bwd_call(n, gd, lowt, hidt, dg, wd, wu, wu2, gs, xhat, r1, vec, wo, ctxt, lse):
     d, rows = lowt.shape
-    ff = wu.shape[1]
+    ff = wd.shape[0]
     nu, nc, nr = ff // TF, d // TC, rows // RC
     r = d // n
     parts = ff // d
@@ -772,8 +821,9 @@
     for i in range(EARLY):
         scratch += reduce_buffers(n, r, d, BF16)
     scratch += [pltpu.SemaphoreType.DMA((EARLY, k)), pltpu.SemaphoreType.DMA((EARLY, k)), pltpu.SemaphoreType.DMA((EARLY, 2)),
-                pltpu.SemaphoreType.DMA((late,)), pltpu.SemaphoreType.DMA((2,)), pltpu.SemaphoreType.DMA((2,))]
+                pltpu.SemaphoreType.DMA((late,)), pltpu.SemaphoreType.DMA((4,)), pltpu.SemaphoreType.DMA((4,))]
     edge = jax.ShapeDtypeStruct((HALO, d), BF16)
+    edge_l = jax.ShapeDtypeStruct((lse.shape[0], HALO), F32)
     first = nu + nc + nr
     return pl.pallas_call(
         functools.partial(bwd_kernel, n, nu, nc, nr),
@@ -781,20 +831,21 @@
         in_specs=[single(gd.shape), single(lowt.shape),
                   pl.BlockSpec((n, 1, r, rows), lambda t: (0, clip(t, 0, nu) // per, 0, 0)),
                   pl.BlockSpec((rows, TF), lambda t: (0, clip(t, 0, nu))), pl.BlockSpec((TF, d), lambda t: (clip(t, 0, nu), 0)),
-                  pl.BlockSpec((TC, ff), lambda t: (clip(t, nu, nc), 0)), pl.BlockSpec((rows, TC), lambda t: (0, clip(t, nu, nc))),
+                  pl.BlockSpec((TC, wu.shape[1]), lambda t: (clip(t, nu, nc), 0)),
+                  pl.BlockSpec((wu2.shape[0], TC, d), lambda t: (0, clip(t, nu, nc), 0)), pl.BlockSpec((rows, TC), lambda t: (0, clip(t, nu, nc))),
                   pl.BlockSpec((RC, d), lambda t: (clip(t, nu + nc, nr), 0)), pl.BlockSpec((RC, 128), lambda t: (clip(t, nu + nc, nr), 0)),
-                  single(vec.shape), pl.BlockSpec((TC, d), lambda t: (clip(t, first, nc), 0)), single(ctxt.shape)],
+                  single(vec.shape), pl.BlockSpec((TC, d), lambda t: (clip(t, first, nc), 0)), single(ctxt.shape), single(lse.shape)],
         out_specs=[single((rows, d)), single((8, d)), pl.BlockSpec((1, TF), lambda t: (0, clip(t, 0, nu))), single((rows, d)),
-                   pl.BlockSpec((d, TC), lambda t: (0, clip(t, first + nc, nc)))] + [ANY] * (4 + late),
+                   pl.BlockSpec((d, TC), lambda t: (0, clip(t, first + nc, nc)))] + [ANY] * (6 + late),
         out_shape=[jax.ShapeDtypeStruct((rows, d), F32), jax.ShapeDtypeStruct((8, d), F32), jax.ShapeDtypeStruct((1, ff), F32),
                    jax.ShapeDtypeStruct((rows, d), BF16), jax.ShapeDtypeStruct((d, d), BF16),
-                   jax.ShapeDtypeStruct(((EARLY + 1) // 2 * r, d), F32), jax.ShapeDtypeStruct((r, EARLY // 2 * d), F32), edge, edge]
-        + [chunk] * late,
+                   jax.ShapeDtypeStruct(((EARLY + 1) // 2 * r, d), F32), jax.ShapeDtypeStruct((r, EARLY // 2 * d), F32), edge, edge,
+                   edge_l, edge_l] + [chunk] * late,
         scratch_shapes=scratch,
         compiler_params=pltpu.CompilerParams(collective_id=3, has_side_effects=True, vmem_limit_bytes=62 << 20),
         cost_estimate=cost(8 * rows * d * ff, 8 * d * ff + 4 * rows * ff + rows * d * 18),
         name="bwd",
-    )(gd, lowt, hidt.reshape(n, parts, r, rows), dg, wd, wu, gs, xhat, r1, vec, wo, ctxt)
+    )(gd, lowt, hidt.reshape(n, parts, r, rows), dg, wd, wu, wu2, gs, xhat, r1, vec, wo, ctxt, lse)
 
 
 IN_PLAN = (
@@ -905,7 +956,7 @@
     first = jnp.sum(jnp.where(inside, starts[None, :], 0), axis=1)
     length = jnp.sum(jnp.where(inside, lengths[None, :], 0), axis=1)
     lead = (first == at) | (jnp.arange(blocks) == 0)
-    return jnp.stack([(first - own * rows + HALO) // GRAN, jnp.where(lead, length // GRAN, 0)]).astype(jnp.int32)
+    return jnp.stack([(first - own * rows + HALO) // GRAN, jnp.where(lead, length // GRAN, 0), length // GRAN]).astype(jnp.int32)
 
 
 def pack(values, n, rows, dtype):
@@ -932,10 +983,9 @@
     packed = jnp.concatenate([mine, ups, jnp.zeros((16 - UB - ups.shape[0], d), BF16)])
     wq, wk, wv, wo, wu, vec, q, k, v = first_call(n, packed, *shards[:5], tokens)
     tab = sequence_table(lengths, own, rows)
-    ctx, lse = attn_fwd_call(tab, q, k, v, rows)
-    xhat, lowt, ctxt, r1, hidt, dg, layer_out, gs, gd, sums2, wd = fwd_call(n, ctx, wo, tokens, wu, shards[5], cotangent, vec)
-    gsf, sums1, sumu, gc, dwo, rd, ru, gl, gr, *late = bwd_call(n, gd, lowt, hidt, dg, wd, wu, gs, xhat, r1, vec, wo, ctxt)
-    dq, dk, dv, sums0 = attn_bwd_call(tab, q, k, v, lse, gl, gc, gr)
+    lse, xhat, lowt, ctxt, r1, hidt, dg, layer_out, gs, gd, sums2, wd, wu2 = fwd_call(n, tab, q, k, v, wo, tokens, wu, *shards[4:6], cotangent, vec)
+    gsf, sums1, sumu, gc, dwo, rd, ru, gl, gr, ll, lr, *late = bwd_call(n, gd, lowt, hidt, dg, wd, wu, wu2, gs, xhat, r1, vec, wo, ctxt, lse)
+    dq, dk, dv, sums0 = attn_bwd_call(tab, q, k, v, ll, lse, lr, gl, gc, gr)
     small = pack([sums0[0], sums0[1], sums1[2], sums2[2], sums1[0], sums1[1], sums2[0], sums2[1], sumu], n, 8, F32)
     tg, *more = in_bwd_call(n, tokens, gsf, dq, dk, dv, wq, wk, wv, late, dwo, small)
     left = len(late)

time: 443 us -> 422 us (0.953)
  Pallas kernels: 434 us -> 411 us
    pallas_call x1, Pallas kernels: 111 us -> 85.8 us  [first_call(): pl.pallas_call(functools.partial(first_kernel, n, nc), grid=(3 * nc + 1,)...]
    pallas_call x2 -> x1, Pallas kernels: 99.8 us -> 98.8 us  [fwd_call(): pl.pallas_call(functools.partial(fwd_kernel, n, na, nu, nc), grid=(na + 2...]
where the time goes in v6:
time: 422 us
  Pallas kernels  411 us (97%)
  local copies, waits for them, and re-layouts  6.97 us (2%)
    pallas_call x1, Pallas kernels, bwd_call(): pl.pallas_call(functools.partial(bwd_kernel, n, nu, nc, nr), grid=(nu + 3...  101 us
    pallas_call x1, Pallas kernels, fwd_call(): pl.pallas_call(functools.partial(fwd_kernel, n, na, nu, nc), grid=(na + 2...  98.8 us
    pallas_call x1, Pallas kernels, in_bwd_call(): pl.pallas_call(functools.partial(in_bwd_kernel, n, nc, left), grid=(4 * n...  92.3 us
    pallas_call x1, Pallas kernels, first_call(): pl.pallas_call(functools.partial(first_kernel, n, nc), grid=(3 * nc + 1,)...  85.8 us
    pallas_call x1, Pallas kernels, attn_bwd_call(): pl.pallas_call(attn_bwd_kernel, grid_spec=pltpu.PrefetchScalarGridSpec(nu...  27.4 us

profile of v6, /device:TPU:0, one launch (start us, length us, event | category | flops | bytes accessed | tf_op | source)
XLA Modules:
  0.0 422.1 jit_solution(12940453148657892124)
XLA Ops:
  0.7 0.1 pad.7.clone
  0.8 0.8 select_reduce_fusion
  1.5 0.7 add.64
  2.2 0.9 select_reduce_fusion.2
  3.1 0.6 pad_add_fusion.tab
  3.7 1.4 stack.42
  5.2 0.8 dynamic_update_slice.7
  6.1 0.2 dynamic_update_slice.6
  6.2 0.7 maximum_maximum_fusion.ps
  6.9 85.8 %first.1 = (bf16[4,2,2,2,32,1024]{5,4,3,2,1,0:T(8,128)(2,1)}, bf16[4,2,2,2,32,1024]{5,4,3,2,1,0:T(8,128)(2,1)}, bf16[4,2,2,2,32,1024]{5,4,3,2,1,0:T(8,128)(2,1)}...) custom-call(bf16[16,1024]{1,0:T(8,128)(2,1)} %maximum_maximum_fusion, ...), custom_call_target="tpu_custom_call" | custom-call | flops 11274289152 | bytes 20971520 | tf_op jit(solution)/shard_map/first/pallas_call | solution.py:491
  92.7 98.8 %fwd.1 = (f32[16,1024]{1,0:T(8,128)}, f32[1024,1024]{1,0:T(8,128)}, bf16[1024,1024]{1,0:T(8,128)(2,1)}, bf16[1024,1024]{1,0:T(8,128)(2,1)}, f32[1024,128]{1,0:T(...) custom-call(s32[3,8]{1,0:T(4,128)} %pad_add_fusion.tab, ...), custom_call_target="tpu_custom_call" | custom-call | flops 17179869184 | bytes 48234496 | tf_op jit(solution)/shard_map/fwd/pallas_call | solution.py:676
  191.6 100.9 %bwd.1 = (f32[1024,1024]{1,0:T(8,128)}, f32[8,1024]{1,0:T(8,128)}, f32[1,4096]{1,0:T(1,128)}, bf16[1024,1024]{1,0:T(8,128)(2,1)}, bf16[1024,1024]{1,0:T(8,128)(2...) custom-call(bf16[1024,1024]{1,0:T(8,128)(2,1)} %get-tuple-element.78, ...), custom_call_target="tpu_custom_call" | custom-call | flops 34359738368 | bytes 69206016 | tf_op jit(solution)/shard_map/bwd/pallas_call | solution.py:828
  292.5 0.9 slice_reduce_fusion
  293.5 27.4 %attn_bwd.1 = (bf16[1024,1024]{1,0:T(8,128)(2,1)}, bf16[1024,1024]{1,0:T(8,128)(2,1)}, bf16[1024,1024]{1,0:T(8,128)(2,1)}, f32[8,1024]{1,0:T(8,128)}) custom-call(s32[3,8]{1,0:T(4,128)} %pad_add_fusion.tab, bf16[1792,1024]{1,0:T(8,128)(2,1)} %get-tuple-element.72.q_ref, bf16[1792,1024]{1,0:T(8,128)(2,1)} %get-tuple-element.73.k_ref, ...), custom_call_target="tpu_custom_call" | custom-call | flops 10737418240 | bytes 25690112 | tf_op jit(solution)/shard_map/attn_bwd/pallas_call | solution.py:123
  320.9 0.9 slice_reduce_fusion.6
  321.7 0.1 reshape_squeeze.25
  321.8 0.1 reshape_squeeze.31
  321.9 0.1 reshape_squeeze.24
  322.3 0.1 concatenate.7
  322.4 0.8 copy.35
  323.2 92.3 %in_bwd.1 = (bf16[1024,1024]{1,0:T(8,128)(2,1)}, f32[32,1024]{1,0:T(8,128)}, f32[32,1024]{1,0:T(8,128)}, f32[32,1024]{1,0:T(8,128)}, f32[32,1024]{1,0:T(8,128)},...) custom-call(bf16[1024,1024]{1,0:T(8,128)(2,1)} %x.5, f32[1024,1024]{1,0:T(8,128)} %get-tuple-element.89.gsf, ...), custom_call_target="tpu_custom_call" | custom-call | flops 12884901888 | bytes 27262976 | tf_op jit(solution)/shard_map/in_bwd/pallas_call | solution.py:909
  415.6 5.4 %hand_on.1 = (f32[32,1024]{1,0:T(8,128)}, f32[32,1024]{1,0:T(8,128)}, f32[32,1024]{1,0:T(8,128)}, f32[32,1024]{1,0:T(8,128)}, f32[32,4096]{1,0:T(8,128)}, /*inde...) custom-call(f32[32,1024]{1,0:T(8,128)} %get-tuple-element.108.refs_0_, ...), custom_call_target="tpu_custom_call" | custom-call | tf_op jit(solution)/shard_map/hand_on/pallas_call | solution.py:943
  421.0 0.5 slice_bitcast_fusion.5
  421.5 0.6 slice_bitcast_fusion
  (18 shorter events, 0.4 us)
Async XLA Ops:
  293.5 28.8 %copy-start = (f32[1,4096]{1,0:T(1,128)S(1)}, f32[1,4096]{1,0:T(1,128)}, u32[]{:S(2)}) copy-start(f32[1,4096]{1,0:T(1,128)} %get-tuple-element.107) | copy-start | bytes 49156
  415.6 5.4 %copy-start.1 = (f32[8,256]{1,0:T(8,128)S(1)}, f32[8,256]{1,0:T(8,128)}, u32[]{:S(2)}) copy-start(f32[8,256]{1,0:T(8,128)} %get-tuple-element.126) | copy-start | bytes 24580

commit v7 on v6

--- a/solution.py
+++ b/solution.py
@@ -353,7 +353,6 @@
             return
         p, bufs = self.p, self.bufs
         nz, ny, nx = p.size
-        dt = bufs[0].dtype
         if i == 5:
             for cp in self.ph[1]:
                 cp.start()
@@ -367,33 +366,33 @@
 
             def add(z, c):
                 mine = self.own[z] if self.own is not None else self.src[z, :, :, pl.ds(p.c, 1)][:, :, 0]
-                bufs[0][z] = (mine.astype(F32) + bufs[0][z].astype(F32)).astype(dt)
+                bufs[0][z] = mine + bufs[0][z]
                 return c
 
             lax.fori_loop(0, nz, add, 0)
             return
         elif i == 2:
             def add(z, c):
-                a = bufs[0][z, :, pl.ds(p.x, 1), :, self.ca].astype(F32)[:, 0]
+                a = bufs[0][z, :, pl.ds(p.x, 1), :, self.ca][:, 0]
                 for k in range(nx - 1):
-                    a += bufs[1][k, z].astype(F32)
-                bufs[1][0, z] = a.astype(dt)
-                b = bufs[0][z, pl.ds(p.y, 1), :, :, self.cb].astype(F32)[0]
+                    a += bufs[1][k, z]
+                bufs[1][0, z] = a
+                b = bufs[0][z, pl.ds(p.y, 1), :, :, self.cb][0]
                 for k in range(ny - 1):
-                    b += bufs[2][k, z].astype(F32)
-                bufs[2][0, z] = b.astype(dt)
+                    b += bufs[2][k, z]
+                bufs[2][0, z] = b
                 return c
 
             lax.fori_loop(0, nz, add, 0)
         elif i == 3:
-            a = bufs[1][0, :, pl.ds(p.y, 1)].astype(F32)[:, 0]
+            a = bufs[1][0, :, pl.ds(p.y, 1)][:, 0]
             for k in range(ny - 1):
-                a += bufs[3][k].astype(F32)
-            bufs[6][:, :, self.ca] = a.astype(dt)
-            b = bufs[2][0, :, pl.ds(p.x, 1)].astype(F32)[:, 0]
+                a += bufs[3][k]
+            bufs[6][:, :, self.ca] = a
+            b = bufs[2][0, :, pl.ds(p.x, 1)][:, 0]
             for k in range(nx - 1):
-                b += bufs[4][k].astype(F32)
-            bufs[6][:, :, self.cb] = b.astype(dt)
+                b += bufs[4][k]
+            bufs[6][:, :, self.cb] = b
         else:
             a = bufs[6][pl.ds(p.z, 1)].astype(F32)[0]
             for k in range(nz - 1):
@@ -698,33 +697,33 @@
 
 
 BWD_PLAN = (
-    (1, 1, 0, 0), (1, 1, 1, 0), (2, 0, 0, 1), (2, 0, 0, 5), (2, 0, 1, 1), (3, 1, 3, 0),
-    (3, 1, 1, 5), (3, 1, 0, 2), (3, 1, 2, 0), (4, 0, 3, 1), (4, 0, 3, 5), (4, 0, 2, 1),
-    (5, 1, 5, 0), (5, 1, 1, 2), (5, 1, 4, 0), (6, 0, 0, 3), (6, 0, 2, 5), (6, 0, 5, 1),
-    (6, 0, 4, 1), (6, 0, 4, 5), (7, 0, 3, 2), (7, 0, 1, 3), (8, 1, 5, 5), (9, 1, 2, 2),
-    (10, 1, 3, 3), (12, 1, 2, 3), (12, 1, 5, 2), (14, 1, 4, 2), (15, 1, 5, 3), (20, 1, 4, 3),
-    (21, 1, 1, 4), (22, 1, 2, 4), (23, 1, 3, 4), (23, 1, 5, 4), (23, 1, 0, 4), (23, 1, 4, 4),
+    (0, 0, 0), (1, 1, 0), (1, 0, 1), (2, 0, 5), (2, 2, 0), (2, 1, 1), (2, 1, 5), (3, 3, 0),
+    (3, 2, 1), (4, 2, 5), (5, 4, 0), (5, 3, 1), (6, 3, 5), (7, 5, 0), (7, 2, 2), (7, 4, 1),
+    (8, 3, 2), (8, 1, 2), (8, 5, 1), (8, 4, 5), (9, 6, 0), (9, 2, 3), (10, 6, 1), (10, 3, 3),
+    (10, 0, 2), (10, 6, 5), (11, 1, 3), (12, 5, 5), (13, 4, 2), (13, 0, 3), (14, 6, 2), (17, 4, 3),
+    (17, 2, 4), (17, 1, 4), (17, 5, 2), (19, 6, 3), (24, 5, 3), (24, 3, 4), (26, 0, 4), (27, 4, 4),
+    (27, 6, 4), (27, 5, 4),
 )
-EARLY = 6
+EARLY = 7
 
 
 def bwd_kernel(n, nu, nc, nr, gd, lowt, hidt, dg, wd, wu, wu2, gs, xhat, r1, vec, wo, ctxt, lse,
                gsf, sums, sumu, gc, dwo, rd, ru, gl, gr, ll, lr, *rest):
-    t = pl.program_id(0)
     d, rows = lowt.shape
     per = d // TF
-    count = 2 * (nu // per)
-    late = rest[:count - EARLY]
-    gu, bufd, bufu, ga = rest[count - EARLY:count - EARLY + 4]
-    rest = rest[count - EARLY + 4:]
+    nd = nu // per
+    t = pl.program_id(0) - nd
+    late = rest[:2 * nd - EARLY]
+    gu, buf0, buf1, ga = rest[2 * nd - EARLY:2 * nd - EARLY + 4]
+    rest = rest[2 * nd - EARLY + 4:]
     ssem, rsem, lsem, wsem, hs, hr = rest[-6:]
     p = Place(n)
     r = d // n
+    bufs = (buf0, buf1)
     red = []
     for i in range(EARLY):
-        j = i // 2
-        out = rd.at[pl.ds(j * r, r), :] if i % 2 == 0 else ru.at[:, pl.ds(j * d, d)]
-        red.append(Reduce(p, (bufd, bufu)[i % 2], None, rest[8 * i:8 * i + 8], out, ssem, rsem, lsem, i))
+        out = rd.at[pl.ds(i * r, r), :] if i < nd else ru.at[:, pl.ds((i - nd) * d, d)]
+        red.append(Reduce(p, bufs[i % 2], None, rest[8 * i:8 * i + 8], out, ssem, rsem, lsem, i))
     right, left = lax.rem(p.me + 1, n), lax.rem(p.me + n - 1, n)
     edges = [pltpu.make_async_remote_copy(src_ref=gc.at[pl.ds(rows - HALO, HALO), :], dst_ref=gl, send_sem=hs.at[0], recv_sem=hr.at[0],
                                           device_id=(right,), device_id_type=MESH),
@@ -735,23 +734,25 @@
              pltpu.make_async_remote_copy(src_ref=lse.at[:, pl.ds(0, HALO)], dst_ref=lr, send_sem=hs.at[3], recv_sem=hr.at[3],
                                           device_id=(left,), device_id_type=MESH)]
     last = nu + 3 * nc + nr - 1
-    mid = [(e[0], red[e[2]].go, e[3]) for e in BWD_PLAN if e[1] == 0]
-    end = [(e[0], red[e[2]].go, e[3]) for e in BWD_PLAN if e[1] == 1]
-    for i in range(EARLY, count):
-        c = pltpu.make_async_copy((bufd, bufu)[i % 2], late[i - EARLY], wsem.at[i - EARLY])
-        end.append((per * (i // 2 + 1) - 1, c.start))
-        if per * (i // 2 + 1) < nu:
-            mid.append((per * (i // 2 + 1), c.wait))
-        else:
-            end.append((last, c.wait))
+    end = [(e[0] - nd, red[e[1]].go, e[2]) for e in BWD_PLAN]
+    for i in range(EARLY, 2 * nd):
+        c = pltpu.make_async_copy(bufs[i % 2], late[i - EARLY], wsem.at[i - EARLY])
+        end += [(per * (i - nd + 1) - 1, c.start), (last, c.wait)]
     end += [(nu + 2 * nc + nr - 1, c.start) for c in edges] + [(last, c.wait) for c in edges]
     end += [(last, c.finish) for c in red]
 
-    @pl.when(t == 0)
+    @pl.when(t == -nd)
     def _():
         enter(p.peers() + [left, right])
 
-    @pl.when(t < nu)
+    for k, buf in enumerate(bufs):
+        @pl.when((t < 0) & (lax.rem(t + nd, 2) == k))
+        def _():
+            for j in range(d // TC):
+                c = slice(j * TC, (j + 1) * TC)
+                buf[..., c] = dot(hidt[...].reshape(d, rows), gd[:, c]).astype(BF16).reshape(buf.shape[:-1] + (TC,))
+
+    @pl.when((t >= 0) & (t < nu))
     def _():
         for j in range(TF // TC):
             c = slice(j * TC, (j + 1) * TC)
@@ -759,15 +760,12 @@
             gu[:, lanes(t * (TF // TC) + j, TC)] = g
             sumu[:, c] = colsum(g.astype(F32))
 
-    run_at(t, mid)
-
-    @pl.when(t < nu)
-    def _():
-        half = lax.rem(t, per)
-        for j in range(TF // TC):
-            c = lanes(half * (TF // TC) + j, TC)
-            bufu[..., c] = dot(lowt[...], gu[:, lanes(t * (TF // TC) + j, TC)]).astype(BF16).reshape(bufu.shape[:-1] + (TC,))
-            bufd[..., c] = dot(hidt[...].reshape(d, rows), gd[:, c]).astype(BF16).reshape(bufd.shape[:-1] + (TC,))
+    for k, buf in enumerate(bufs):
+        @pl.when((t >= 0) & (t < nu) & (lax.rem(t // per, 2) == k))
+        def _():
+            for j in range(TF // TC):
+                c = lanes(lax.rem(t, per) * (TF // TC) + j, TC)
+                buf[..., c] = dot(lowt[...], gu[:, lanes(t * (TF // TC) + j, TC)]).astype(BF16).reshape(buf.shape[:-1] + (TC,))
 
     @pl.when((t >= nu) & (t < nu + nc))
     def _():
@@ -801,7 +799,7 @@
 
     @pl.when(t >= first + nc)
     def _():
-        dwo[...] = dot(ctxt[...], ga[:, lanes(t - first - nc, TC)]).astype(BF16)
+        dwo[...] = dot(ctxt[...], ga[...]).astype(BF16)
 
     run_at(t, end)
 
@@ -813,10 +811,10 @@
     r = d // n
     parts = ff // d
     z = grid_of(n) + (2, r)
-    per = d // TF
     chunk = jax.ShapeDtypeStruct(z + (d,), BF16)
     k = reduce_slots(n)
     late = 2 * parts - EARLY
+    nd = parts
     scratch = [pltpu.VMEM((rows, ff), BF16), pltpu.VMEM(z + (d,), BF16), pltpu.VMEM(z + (d,), BF16), pltpu.VMEM((rows, d), BF16)]
     for i in range(EARLY):
         scratch += reduce_buffers(n, r, d, BF16)
@@ -824,22 +822,22 @@
                 pltpu.SemaphoreType.DMA((late,)), pltpu.SemaphoreType.DMA((4,)), pltpu.SemaphoreType.DMA((4,))]
     edge = jax.ShapeDtypeStruct((HALO, d), BF16)
     edge_l = jax.ShapeDtypeStruct((lse.shape[0], HALO), F32)
-    first = nu + nc + nr
+    first = nd + nu + nc + nr
     return pl.pallas_call(
         functools.partial(bwd_kernel, n, nu, nc, nr),
-        grid=(nu + 3 * nc + nr,),
+        grid=(nd + nu + 3 * nc + nr,),
         in_specs=[single(gd.shape), single(lowt.shape),
-                  pl.BlockSpec((n, 1, r, rows), lambda t: (0, clip(t, 0, nu) // per, 0, 0)),
-                  pl.BlockSpec((rows, TF), lambda t: (0, clip(t, 0, nu))), pl.BlockSpec((TF, d), lambda t: (clip(t, 0, nu), 0)),
-                  pl.BlockSpec((TC, wu.shape[1]), lambda t: (clip(t, nu, nc), 0)),
-                  pl.BlockSpec((wu2.shape[0], TC, d), lambda t: (0, clip(t, nu, nc), 0)), pl.BlockSpec((rows, TC), lambda t: (0, clip(t, nu, nc))),
-                  pl.BlockSpec((RC, d), lambda t: (clip(t, nu + nc, nr), 0)), pl.BlockSpec((RC, 128), lambda t: (clip(t, nu + nc, nr), 0)),
-                  single(vec.shape), pl.BlockSpec((TC, d), lambda t: (clip(t, first, nc), 0)), single(ctxt.shape), single(lse.shape)],
-        out_specs=[single((rows, d)), single((8, d)), pl.BlockSpec((1, TF), lambda t: (0, clip(t, 0, nu))), single((rows, d)),
-                   pl.BlockSpec((d, TC), lambda t: (0, clip(t, first + nc, nc)))] + [ANY] * (6 + late),
+                  pl.BlockSpec((n, 1, r, rows), lambda t: (0, clip(t, 0, nd), 0, 0)),
+                  pl.BlockSpec((rows, TF), lambda t: (0, clip(t, nd, nu))), pl.BlockSpec((TF, d), lambda t: (clip(t, nd, nu), 0)),
+                  pl.BlockSpec((TC, wu.shape[1]), lambda t: (clip(t, nd + nu, nc), 0)),
+                  pl.BlockSpec((wu2.shape[0], TC, d), lambda t: (0, clip(t, nd + nu, nc), 0)), pl.BlockSpec((rows, TC), lambda t: (0, clip(t, nd + nu, nc))),
+                  pl.BlockSpec((RC, d), lambda t: (clip(t, nd + nu + nc, nr), 0)), pl.BlockSpec((RC, 128), lambda t: (clip(t, nd + nu + nc, nr), 0)),
+                  single(vec.shape), pl.BlockSpec((TC, d), lambda t: (clip(t, first, nc), 0)), pl.BlockSpec((TC, rows), lambda t: (clip(t, first + nc, nc), 0)), single(lse.shape)],
+        out_specs=[single((rows, d)), single((8, d)), pl.BlockSpec((1, TF), lambda t: (0, clip(t, nd, nu))), single((rows, d)),
+                   pl.BlockSpec((TC, d), lambda t: (clip(t, first + nc, nc), 0))] + [ANY] * (6 + late),
         out_shape=[jax.ShapeDtypeStruct((rows, d), F32), jax.ShapeDtypeStruct((8, d), F32), jax.ShapeDtypeStruct((1, ff), F32),
                    jax.ShapeDtypeStruct((rows, d), BF16), jax.ShapeDtypeStruct((d, d), BF16),
-                   jax.ShapeDtypeStruct(((EARLY + 1) // 2 * r, d), F32), jax.ShapeDtypeStruct((r, EARLY // 2 * d), F32), edge, edge,
+                   jax.ShapeDtypeStruct((nd * r, d), F32), jax.ShapeDtypeStruct((r, (EARLY - nd) * d), F32), edge, edge,
                    edge_l, edge_l] + [chunk] * late,
         scratch_shapes=scratch,
         compiler_params=pltpu.CompilerParams(collective_id=3, has_side_effects=True, vmem_limit_bytes=62 << 20),
@@ -849,12 +847,11 @@
 
 
 IN_PLAN = (
-    (0, 6, 0), (0, 1, 0), (2, 6, 1), (2, 2, 0), (2, 6, 5), (3, 1, 1), (3, 1, 5), (4, 6, 2),
-    (4, 3, 0), (5, 3, 1), (5, 3, 5), (5, 1, 2), (5, 0, 0), (6, 2, 1), (7, 4, 0), (7, 2, 5),
-    (7, 4, 1), (8, 4, 5), (9, 1, 3), (10, 0, 1), (10, 6, 3), (10, 0, 5), (10, 3, 2), (11, 3, 3),
-    (11, 5, 0), (11, 2, 2), (12, 0, 2), (12, 5, 1), (12, 6, 4), (12, 5, 5), (12, 2, 3), (12, 4, 2),
-    (13, 0, 3), (13, 4, 3), (13, 5, 2), (13, 5, 3), (13, 1, 4), (14, 2, 4), (15, 0, 4), (15, 4, 4),
-    (15, 3, 4), (15, 5, 4),
+    (0, 1, 0), (2, 1, 1), (2, 1, 5), (2, 0, 0), (3, 2, 0), (5, 0, 1), (5, 0, 5), (7, 3, 0),
+    (8, 1, 2), (8, 3, 1), (8, 3, 5), (8, 5, 0), (8, 0, 2), (8, 5, 1), (9, 5, 5), (9, 2, 1),
+    (10, 1, 3), (11, 4, 0), (11, 2, 5), (11, 4, 1), (11, 0, 3), (12, 3, 2), (12, 2, 2), (13, 4, 5),
+    (13, 3, 3), (13, 2, 3), (13, 1, 4), (14, 5, 2), (14, 4, 2), (15, 0, 4), (15, 3, 4), (15, 5, 3),
+    (15, 4, 3), (15, 2, 4), (15, 5, 4), (15, 4, 4),
 )
 
 
@@ -990,9 +987,7 @@
     tg, *more = in_bwd_call(n, tokens, gsf, dq, dk, dv, wq, wk, wv, late, dwo, small)
     left = len(late)
     go, gq, gk, gv, tiny = more[left:]
-    downs = [rd] + [more[i] for i in range(left) if (EARLY + i) % 2 == 0]
-    ups = [ru] + [more[i] for i in range(left) if (EARLY + i) % 2 == 1]
-    gq, gk, gv, go, gu, gd, tg, layer_out = hand_on([[gq], [gk], [gv], [go], ups, downs, [tg], [layer_out]], (0, 0, 0, 0, 1, 0, 0, 0))
+    gq, gk, gv, go, gu, gd, tg, layer_out = hand_on([[gq], [gk], [gv], [go], [ru] + more[:left], [rd], [tg], [layer_out]], (0, 0, 0, 0, 1, 0, 0, 0))
     vecs, ubg = unpack(tiny, 1, part)
     t = [vecs[i] for i in range(8)]
     return (layer_out, tg, gq, gk, gv, go, gu, gd, t[0], t[1], t[2], ubg[0], t[3], t[4], t[5], t[6], t[7])

time: 422 us -> 409 us (0.969)
  Pallas kernels: 411 us -> 396 us
    pallas_call x1, Pallas kernels: 92.3 us -> 77.5 us  [in_bwd_call(): pl.pallas_call(functools.partial(in_bwd_kernel, n, nc, left), grid=(4 * n...]
where the time goes in v7:
time: 409 us; the launch traced here: 407 us
  Pallas kernels  396 us (97%)
  local copies, waits for them, and re-layouts  6.97 us (2%)
    pallas_call x1, Pallas kernels, bwd_call(): pl.pallas_call(functools.partial(bwd_kernel, n, nu, nc, nr), grid=(nd + n...  104 us
    pallas_call x1, Pallas kernels, fwd_call(): pl.pallas_call(functools.partial(fwd_kernel, n, na, nu, nc), grid=(na + 2...  98.8 us
    pallas_call x1, Pallas kernels, first_call(): pl.pallas_call(functools.partial(first_kernel, n, nc), grid=(3 * nc + 1,)...  85.8 us
    pallas_call x1, Pallas kernels, in_bwd_call(): pl.pallas_call(functools.partial(in_bwd_kernel, n, nc, left), grid=(4 * n...  77.5 us
    pallas_call x1, Pallas kernels, attn_bwd_call(): pl.pallas_call(attn_bwd_kernel, grid_spec=pltpu.PrefetchScalarGridSpec(nu...  24.4 us

profile of v7, /device:TPU:0, one launch (start us, length us, event | category | flops | bytes accessed | tf_op | source)
XLA Modules:
  0.0 407.4 jit_solution(6728033634112234563)
XLA Ops:
  0.7 0.1 pad.7.clone
  0.8 0.8 select_reduce_fusion
  1.5 0.7 add.64
  2.2 0.9 select_reduce_fusion.2
  3.1 0.6 pad_add_fusion.tab
  3.7 1.4 stack.42
  5.2 0.8 dynamic_update_slice.7
  6.1 0.2 dynamic_update_slice.6
  6.2 0.7 maximum_maximum_fusion.ps
  6.9 85.8 %first.1 = (bf16[4,2,2,2,32,1024]{5,4,3,2,1,0:T(8,128)(2,1)}, bf16[4,2,2,2,32,1024]{5,4,3,2,1,0:T(8,128)(2,1)}, bf16[4,2,2,2,32,1024]{5,4,3,2,1,0:T(8,128)(2,1)}...) custom-call(bf16[16,1024]{1,0:T(8,128)(2,1)} %maximum_maximum_fusion, ...), custom_call_target="tpu_custom_call" | custom-call | flops 11274289152 | bytes 20971520 | tf_op jit(solution)/shard_map/first/pallas_call | solution.py:490
  92.7 98.8 %fwd.1 = (f32[16,1024]{1,0:T(8,128)}, f32[1024,1024]{1,0:T(8,128)}, bf16[1024,1024]{1,0:T(8,128)(2,1)}, bf16[1024,1024]{1,0:T(8,128)(2,1)}, f32[1024,128]{1,0:T(...) custom-call(s32[3,8]{1,0:T(4,128)} %pad_add_fusion.tab, ...), custom_call_target="tpu_custom_call" | custom-call | flops 17179869184 | bytes 48234496 | tf_op jit(solution)/shard_map/fwd/pallas_call | solution.py:675
  191.5 104.0 %bwd.1 = (f32[1024,1024]{1,0:T(8,128)}, f32[8,1024]{1,0:T(8,128)}, f32[1,4096]{1,0:T(1,128)}, bf16[1024,1024]{1,0:T(8,128)(2,1)}, bf16[1024,1024]{1,0:T(8,128)(2...) custom-call(bf16[1024,1024]{1,0:T(8,128)(2,1)} %get-tuple-element.76, ...), custom_call_target="tpu_custom_call" | custom-call | flops 34359738368 | bytes 69206016 | tf_op jit(solution)/shard_map/bwd/pallas_call | solution.py:826
  295.6 0.9 slice_reduce_fusion
  296.5 24.4 %attn_bwd.1 = (bf16[1024,1024]{1,0:T(8,128)(2,1)}, bf16[1024,1024]{1,0:T(8,128)(2,1)}, bf16[1024,1024]{1,0:T(8,128)(2,1)}, f32[8,1024]{1,0:T(8,128)}) custom-call(s32[3,8]{1,0:T(4,128)} %pad_add_fusion.tab, bf16[1792,1024]{1,0:T(8,128)(2,1)} %get-tuple-element.70.q_ref, bf16[1792,1024]{1,0:T(8,128)(2,1)} %get-tuple-element.71.k_ref, ...), custom_call_target="tpu_custom_call" | custom-call | flops 10737418240 | bytes 25690112 | tf_op jit(solution)/shard_map/attn_bwd/pallas_call | solution.py:123
  321.0 0.9 slice_reduce_fusion.6
  321.8 0.1 reshape_squeeze.25
  321.9 0.1 reshape_squeeze.31
  322.0 0.1 reshape_squeeze.24
  322.4 0.1 concatenate.7
  322.5 0.8 copy.35
  323.3 77.5 %in_bwd.1 = (bf16[1024,1024]{1,0:T(8,128)(2,1)}, f32[32,1024]{1,0:T(8,128)}, f32[32,1024]{1,0:T(8,128)}, f32[32,1024]{1,0:T(8,128)}, f32[32,1024]{1,0:T(8,128)}, /*index=5*/f32[32,1024]{1,0:T(8,128)}, f32[8,256]{1,0:T(8,128)}) custom-call(bf16[1024,1024]{1,0:T(8,128)(2,1)} %x.5, f32[1024,1024]{1,0:T(8,128)} %get-tuple-element.87.gsf, ...), custom_call_target="tpu_custom_call" | custom-call | flops 12884901888 | bytes 27262976 | tf_op jit(solution)/shard_map/in_bwd/pallas_call | solution.py:906
  400.9 5.3 %hand_on.1 = (f32[32,1024]{1,0:T(8,128)}, f32[32,1024]{1,0:T(8,128)}, f32[32,1024]{1,0:T(8,128)}, f32[32,1024]{1,0:T(8,128)}, f32[32,4096]{1,0:T(8,128)}, /*inde...) custom-call(f32[32,1024]{1,0:T(8,128)} %get-tuple-element.105.refs_0_, ...), custom_call_target="tpu_custom_call" | custom-call | tf_op jit(solution)/shard_map/hand_on/pallas_call | solution.py:940
  406.3 0.5 slice_bitcast_fusion.5
  406.8 0.6 slice_bitcast_fusion
  (18 shorter events, 0.4 us)
Async XLA Ops:
  296.5 25.9 %copy-start = (f32[1,4096]{1,0:T(1,128)S(1)}, f32[1,4096]{1,0:T(1,128)}, u32[]{:S(2)}) copy-start(f32[1,4096]{1,0:T(1,128)} %get-tuple-element.104) | copy-start | bytes 49156
  400.9 5.4 %copy-start.1 = (f32[8,256]{1,0:T(8,128)S(1)}, f32[8,256]{1,0:T(8,128)}, u32[]{:S(2)}) copy-start(f32[8,256]{1,0:T(8,128)} %get-tuple-element.122) | copy-start | bytes 24580

commit v8 on v7

--- a/solution.py
+++ b/solution.py
@@ -697,12 +697,12 @@
 
 
 BWD_PLAN = (
-    (0, 0, 0), (1, 1, 0), (1, 0, 1), (2, 0, 5), (2, 2, 0), (2, 1, 1), (2, 1, 5), (3, 3, 0),
-    (3, 2, 1), (4, 2, 5), (5, 4, 0), (5, 3, 1), (6, 3, 5), (7, 5, 0), (7, 2, 2), (7, 4, 1),
-    (8, 3, 2), (8, 1, 2), (8, 5, 1), (8, 4, 5), (9, 6, 0), (9, 2, 3), (10, 6, 1), (10, 3, 3),
-    (10, 0, 2), (10, 6, 5), (11, 1, 3), (12, 5, 5), (13, 4, 2), (13, 0, 3), (14, 6, 2), (17, 4, 3),
-    (17, 2, 4), (17, 1, 4), (17, 5, 2), (19, 6, 3), (24, 5, 3), (24, 3, 4), (26, 0, 4), (27, 4, 4),
-    (27, 6, 4), (27, 5, 4),
+    (0, 0, 0), (1, 1, 0), (1, 0, 1), (1, 0, 5), (2, 2, 0), (2, 1, 1), (3, 3, 0), (3, 1, 5),
+    (3, 2, 1), (5, 4, 0), (5, 2, 5), (5, 3, 1), (6, 3, 5), (6, 1, 2), (7, 5, 0), (7, 0, 2),
+    (7, 4, 1), (8, 5, 1), (8, 2, 2), (8, 4, 5), (9, 6, 0), (10, 5, 5), (10, 2, 3), (11, 4, 2),
+    (11, 0, 3), (11, 3, 2), (12, 6, 1), (12, 5, 2), (12, 1, 3), (13, 4, 3), (14, 3, 3), (14, 6, 5),
+    (19, 5, 3), (20, 6, 2), (25, 3, 4), (25, 6, 3), (26, 2, 4), (26, 5, 4), (26, 4, 4), (27, 1, 4),
+    (27, 0, 4), (27, 6, 4),
 )
 EARLY = 7
 

time: 409 us -> 413 us (level)
  Pallas kernels: 396 us -> 401 us
    pallas_call x1, Pallas kernels: 77.5 us -> 89.3 us  [in_bwd_call(): pl.pallas_call(functools.partial(in_bwd_kernel, n, nc, left), grid=(4 * n...]
where the time goes in v8:
time: 413 us; the launch traced here: 412 us
  Pallas kernels  401 us (97%)
  local copies, waits for them, and re-layouts  6.97 us (2%)
    pallas_call x1, Pallas kernels, bwd_call(): pl.pallas_call(functools.partial(bwd_kernel, n, nu, nc, nr), grid=(nd + n...  101 us
    pallas_call x1, Pallas kernels, fwd_call(): pl.pallas_call(functools.partial(fwd_kernel, n, na, nu, nc), grid=(na + 2...  98.8 us
    pallas_call x1, Pallas kernels, in_bwd_call(): pl.pallas_call(functools.partial(in_bwd_kernel, n, nc, left), grid=(4 * n...  89.3 us
    pallas_call x1, Pallas kernels, first_call(): pl.pallas_call(functools.partial(first_kernel, n, nc), grid=(3 * nc + 1,)...  85.8 us
    pallas_call x1, Pallas kernels, attn_bwd_call(): pl.pallas_call(attn_bwd_kernel, grid_spec=pltpu.PrefetchScalarGridSpec(nu...  20.4 us

profile of v8, /device:TPU:0, one launch (start us, length us, event | category | flops | bytes accessed | tf_op | source)
XLA Modules:
  0.0 412.1 jit_solution(7851344416896573058)
XLA Ops:
  0.7 0.1 pad.7.clone
  0.8 0.8 select_reduce_fusion
  1.5 0.7 add.64
  2.2 0.9 select_reduce_fusion.2
  3.1 0.6 pad_add_fusion.tab
  3.7 1.4 stack.42
  5.2 0.8 dynamic_update_slice.7
  6.1 0.2 dynamic_update_slice.6
  6.2 0.7 maximum_maximum_fusion.ps
  6.9 85.8 %first.1 = (bf16[4,2,2,2,32,1024]{5,4,3,2,1,0:T(8,128)(2,1)}, bf16[4,2,2,2,32,1024]{5,4,3,2,1,0:T(8,128)(2,1)}, bf16[4,2,2,2,32,1024]{5,4,3,2,1,0:T(8,128)(2,1)}...) custom-call(bf16[16,1024]{1,0:T(8,128)(2,1)} %maximum_maximum_fusion, ...), custom_call_target="tpu_custom_call" | custom-call | flops 11274289152 | bytes 20971520 | tf_op jit(solution)/shard_map/first/pallas_call | solution.py:490
  92.7 98.8 %fwd.1 = (f32[16,1024]{1,0:T(8,128)}, f32[1024,1024]{1,0:T(8,128)}, bf16[1024,1024]{1,0:T(8,128)(2,1)}, bf16[1024,1024]{1,0:T(8,128)(2,1)}, f32[1024,128]{1,0:T(...) custom-call(s32[3,8]{1,0:T(4,128)} %pad_add_fusion.tab, ...), custom_call_target="tpu_custom_call" | custom-call | flops 17179869184 | bytes 48234496 | tf_op jit(solution)/shard_map/fwd/pallas_call | solution.py:675
  191.5 101.0 %bwd.1 = (f32[1024,1024]{1,0:T(8,128)}, f32[8,1024]{1,0:T(8,128)}, f32[1,4096]{1,0:T(1,128)}, bf16[1024,1024]{1,0:T(8,128)(2,1)}, bf16[1024,1024]{1,0:T(8,128)(2...) custom-call(bf16[1024,1024]{1,0:T(8,128)(2,1)} %get-tuple-element.76, ...), custom_call_target="tpu_custom_call" | custom-call | flops 34359738368 | bytes 69206016 | tf_op jit(solution)/shard_map/bwd/pallas_call | solution.py:826
  292.6 0.9 slice_reduce_fusion
  293.5 20.4 %attn_bwd.1 = (bf16[1024,1024]{1,0:T(8,128)(2,1)}, bf16[1024,1024]{1,0:T(8,128)(2,1)}, bf16[1024,1024]{1,0:T(8,128)(2,1)}, f32[8,1024]{1,0:T(8,128)}) custom-call(s32[3,8]{1,0:T(4,128)} %pad_add_fusion.tab, bf16[1792,1024]{1,0:T(8,128)(2,1)} %get-tuple-element.70.q_ref, bf16[1792,1024]{1,0:T(8,128)(2,1)} %get-tuple-element.71.k_ref, ...), custom_call_target="tpu_custom_call" | custom-call | flops 10737418240 | bytes 25690112 | tf_op jit(solution)/shard_map/attn_bwd/pallas_call | solution.py:123
  313.9 0.9 slice_reduce_fusion.6
  314.8 0.1 reshape_squeeze.25
  314.8 0.1 reshape_squeeze.31
  314.9 0.1 reshape_squeeze.24
  315.3 0.1 concatenate.7
  315.5 0.8 copy.35
  316.3 89.3 %in_bwd.1 = (bf16[1024,1024]{1,0:T(8,128)(2,1)}, f32[32,1024]{1,0:T(8,128)}, f32[32,1024]{1,0:T(8,128)}, f32[32,1024]{1,0:T(8,128)}, f32[32,1024]{1,0:T(8,128)}, /*index=5*/f32[32,1024]{1,0:T(8,128)}, f32[8,256]{1,0:T(8,128)}) custom-call(bf16[1024,1024]{1,0:T(8,128)(2,1)} %x.5, f32[1024,1024]{1,0:T(8,128)} %get-tuple-element.87.gsf, ...), custom_call_target="tpu_custom_call" | custom-call | flops 12884901888 | bytes 27262976 | tf_op jit(solution)/shard_map/in_bwd/pallas_call | solution.py:906
  405.6 5.3 %hand_on.1 = (f32[32,1024]{1,0:T(8,128)}, f32[32,1024]{1,0:T(8,128)}, f32[32,1024]{1,0:T(8,128)}, f32[32,1024]{1,0:T(8,128)}, f32[32,4096]{1,0:T(8,128)}, /*inde...) custom-call(f32[32,1024]{1,0:T(8,128)} %get-tuple-element.105.refs_0_, ...), custom_call_target="tpu_custom_call" | custom-call | tf_op jit(solution)/shard_map/hand_on/pallas_call | solution.py:940
  411.0 0.5 slice_bitcast_fusion.5
  411.5 0.6 slice_bitcast_fusion
  (18 shorter events, 0.4 us)
Async XLA Ops:
  293.5 21.8 %copy-start = (f32[1,4096]{1,0:T(1,128)S(1)}, f32[1,4096]{1,0:T(1,128)}, u32[]{:S(2)}) copy-start(f32[1,4096]{1,0:T(1,128)} %get-tuple-element.104) | copy-start | bytes 49156
  405.6 5.4 %copy-start.1 = (f32[8,256]{1,0:T(8,128)S(1)}, f32[8,256]{1,0:T(8,128)}, u32[]{:S(2)}) copy-start(f32[8,256]{1,0:T(8,128)} %get-tuple-element.122) | copy-start | bytes 24580
